TPU v7x, 256 devices: a whole 4x4x8 slice. The times are simulated.
256 devices in a mesh: ty: 16 (over y, z_hi), tx: 16 (over x, z_lo, core).
Axes of the slice: x: 4, y: 4, z: 8 (z_hi: 4, z_lo: 2; z = z_hi * 2 + z_lo), core: 2. Of those that a mesh axis runs over, the one named last changes fastest.
Arguments:
- object_tiles: float32 [2, 2, 4096, 4096], P(None, None, 'ty', 'tx'), may hold values from -5 to 5
- probe_field: float32 [2, 256, 256], replicated, may hold values from -6 to 6
- prop_angle: float32 [256, 256], replicated, may hold values from -3.140625 to 3.140625
- scan_offsets: int32 [2, 16, 16, 2, 2], P(None, 'ty', 'tx'), may hold values from 0 to 255, as said below
- probe_counts: int32 [2, 16, 16], P(None, 'ty', 'tx'), may hold values from 0 to 2, as said below
- amplitudes: float32 [2, 16, 16, 2, 256, 256], P(None, 'ty', 'tx'), may hold values from 0 to 2.5
Outputs:
- object_out: float32 [2, 2, 4096, 4096], P(None, None, 'ty', 'tx')
Inputs may be any that keep to these rules, and one draw needn't show every extreme that they name: `probe_counts`: every tile has at most 2 live slots in an iteration, and some tile has exactly 2 in every iteration; slots at or past a tile's count are not used. `scan_offsets`: on tiles of the last tile row the row offset is at most 0, and on tiles of the last tile column the column offset is at most 0, so every window lies inside the object.
All inputs are finite; a program needn't handle non-finite values.
Results may differ from a plain program's by a relative error of at most 0.0003.
Values sent between devices are 32-bit elements; how exact they have to be, the bound alone decides.
No kernel may reach another device: no remote copies, remote signals or barrier semaphores. Data moves between devices by JAX's collectives and lax.ppermute only.
A program may use at most 128 MiB of HBM per device.

v0:
```python
import numpy as np

import jax
import jax.numpy as jnp
from jax import lax
from jax.experimental import pallas as pl
from jax.experimental.pallas import tpu as pltpu
from jax.sharding import PartitionSpec as P


ITERS = 2
SLOTS = 2
SIDE = 256
HALF = SIDE // 2

soft_floor = 0.01
step_size = 0.25


def dft_tables():
    k = np.arange(HALF)
    stack = []
    for parity in (0, 1):
        angle = 2.0 * np.pi * ((2 * k[:, None] + parity) * k[None, :] % SIDE) / SIDE
        cos, sin = np.cos(angle) / 16.0, np.sin(angle) / 16.0
        stack.append(np.block([[cos, sin], [-sin, cos]]))
    both = np.stack([np.stack(stack), np.stack([t.T for t in stack])])
    high = both.astype(jnp.bfloat16)
    low = (both - high.astype(np.float64)).astype(jnp.bfloat16)
    return np.stack([high, low], axis=2)


def shifted(value, axis, steps):
    count = lax.axis_size(axis)
    first, last = (max(0, -steps), min(count, count - steps))
    return lax.ppermute(value, axis, [(source, source + steps) for source in range(first, last)])


def split(value):
    high = value.astype(jnp.bfloat16)
    return high, (value - high.astype(jnp.float32)).astype(jnp.bfloat16)


def dot(left, right):
    return jnp.dot(left, right, preferred_element_type=jnp.float32)


def table_left(tables, flip, parity, value):
    high, low = split(value)
    t_high, t_low = tables[flip, parity, 0], tables[flip, parity, 1]
    return dot(t_high, high) + (dot(t_high, low) + dot(t_low, high))


def table_right(tables, flip, parity, value):
    high, low = split(value)
    t_high, t_low = tables[flip, parity, 0], tables[flip, parity, 1]
    return dot(high, t_high) + (dot(low, t_high) + dot(high, t_low))


def rows_cat(a, b):
    return jnp.concatenate([a, b], axis=0)


def lanes_cat(a, b):
    return jnp.concatenate([a, b], axis=1)


def forward(tables, re, im):
    ra, rb, ia, ib = re[:HALF], re[HALF:], im[:HALF], im[HALF:]
    even = table_left(tables, 0, 0, rows_cat(ra + rb, ia + ib))
    odd = table_left(tables, 0, 1, rows_cat(ra - rb, ia - ib))
    real = rows_cat(even[:HALF], odd[:HALF])
    imag = rows_cat(even[HALF:], odd[HALF:])
    ra, rb, ia, ib = real[:, :HALF], real[:, HALF:], imag[:, :HALF], imag[:, HALF:]
    return (
        table_right(tables, 1, 0, lanes_cat(ra + rb, ia + ib)),
        table_right(tables, 1, 1, lanes_cat(ra - rb, ia - ib)),
    )


def inverse(tables, even, odd):
    even = table_right(tables, 0, 0, even)
    odd = table_right(tables, 0, 1, odd)
    real = lanes_cat(even[:, :HALF] + odd[:, :HALF], even[:, :HALF] - odd[:, :HALF])
    imag = lanes_cat(even[:, HALF:] + odd[:, HALF:], even[:, HALF:] - odd[:, HALF:])
    even = table_left(tables, 1, 0, rows_cat(real[:HALF], imag[:HALF]))
    odd = table_left(tables, 1, 1, rows_cat(real[HALF:], imag[HALF:]))
    return (
        rows_cat(even[:HALF] + odd[:HALF], even[:HALF] - odd[:HALF]),
        rows_cat(even[HALF:] + odd[HALF:], even[HALF:] - odd[HALF:]),
    )


def masks(off_ref, iteration, slot):
    row = off_ref[iteration, slot, 0]
    col = off_ref[iteration, slot, 1]
    below = lax.broadcasted_iota(jnp.int32, (SIDE, SIDE), 0) < row
    right = lax.broadcasted_iota(jnp.int32, (SIDE, SIDE), 1) < col
    return below, right


def picked(below, right, own, rgt, low, dia, plane):
    upper = jnp.where(right, rgt[plane], own[plane])
    lower = jnp.where(right, dia[plane], low[plane])
    return jnp.where(below, lower, upper)


def placed(below, right, value, plane, stay, move):
    zero = jnp.zeros_like(value)
    left_part = jnp.where(right, zero, value)
    right_part = jnp.where(right, value, zero)
    stay[0, plane] += jnp.where(below, zero, left_part)
    stay[1, plane] += jnp.where(below, left_part, zero)
    move[0, plane] += jnp.where(below, zero, right_part)
    move[1, plane] += jnp.where(below, right_part, zero)


def prepare_kernel(off_ref, probe_ref, cos_ref, sin_ref, amp_ref, perm_ref,
                   rolled_ref, prop_ref, ampl_ref, twice):
    def reorder(src):
        rest = src[...]
        total = None
        for _ in range(3):
            part = rest.astype(jnp.bfloat16)
            rest = rest - part.astype(jnp.float32)
            part = dot(dot(perm_ref[0], part).astype(jnp.bfloat16), perm_ref[1])
            total = part if total is None else total + part
        return total

    def put(dst, value):
        dst[0] = value[:, :HALF]
        dst[1] = value[:, HALF:]

    def tile_loop(index, carry):
        it, slot = index // SLOTS, index % SLOTS
        row = off_ref[it, slot, 0]
        col = off_ref[it, slot, 1]
        for plane in range(2):
            start = pl.multiple_of(SIDE - 8 - row // 8 * 8, 8)
            turned = pltpu.roll(twice[plane, pl.ds(start, SIDE + 8), :], row % 8, 0)
            rolled_ref[it, slot, plane] = pltpu.roll(turned[8:], col, 1)
        put(ampl_ref.at[it, slot], reorder(amp_ref.at[it, slot]))
        return carry

    for plane in range(2):
        twice[plane, :SIDE] = probe_ref[plane]
        twice[plane, SIDE:] = probe_ref[plane]
    put(prop_ref.at[0], reorder(cos_ref))
    put(prop_ref.at[1], reorder(sin_ref))
    lax.fori_loop(0, ITERS * SLOTS, tile_loop, 0)


def first_kernel(iteration, off_ref, cnt_ref, own, rgt, low, dia, rolled, prop, tables, mid_ref):
    def body(slot, carry):
        below, right = masks(off_ref, iteration, slot)
        one_re = picked(below, right, own, rgt, low, dia, 0)
        one_im = picked(below, right, own, rgt, low, dia, 1)
        p_re, p_im = rolled[iteration, slot, 0], rolled[iteration, slot, 1]
        spec = forward(tables, p_re * one_re - p_im * one_im, p_re * one_im + p_im * one_re)
        moved = []
        for q in range(2):
            re, im = spec[q][:, :HALF], spec[q][:, HALF:]
            h_re, h_im = prop[0, q], prop[1, q]
            moved.append(lanes_cat(re * h_re - im * h_im, re * h_im + im * h_re))
        mid_ref[slot, 0], mid_ref[slot, 1] = inverse(tables, *moved)
        return carry

    lax.fori_loop(0, cnt_ref[iteration], body, 0)


def second_kernel(iteration, off_ref, cnt_ref, own, rgt, low, dia, mid_ref, ampl, tables,
                  stay, move, carry_ref):
    stay[...] = jnp.zeros_like(stay)
    move[...] = jnp.zeros_like(move)

    def body(slot, carry):
        below, right = masks(off_ref, iteration, slot)
        two_re = picked(below, right, own, rgt, low, dia, 0)
        two_im = picked(below, right, own, rgt, low, dia, 1)
        m_re, m_im = mid_ref[slot, 0], mid_ref[slot, 1]
        far = forward(tables, m_re * two_re - m_im * two_im, m_re * two_im + m_im * two_re)
        chi = []
        for q in range(2):
            re, im = far[q][:, :HALF], far[q][:, HALF:]
            factor = 1.0 - ampl[iteration, slot, q] * lax.rsqrt(re * re + im * im + soft_floor)
            chi.append(lanes_cat(re * factor, im * factor))
        b_re, b_im = inverse(tables, *chi)
        placed(below, right, m_re * b_re + m_im * b_im, 0, stay, move)
        placed(below, right, m_re * b_im - m_im * b_re, 1, stay, move)
        carry_ref[slot, 0] = two_re * b_re + two_im * b_im
        carry_ref[slot, 1] = two_re * b_im - two_im * b_re
        return carry

    lax.fori_loop(0, cnt_ref[iteration], body, 0)


def third_kernel(iteration, off_ref, cnt_ref, carry_ref, rolled, prop, tables, stay, move):
    stay[...] = jnp.zeros_like(stay)
    move[...] = jnp.zeros_like(move)

    def body(slot, carry):
        below, right = masks(off_ref, iteration, slot)
        spec = forward(tables, carry_ref[slot, 0], carry_ref[slot, 1])
        turned = []
        for q in range(2):
            re, im = spec[q][:, :HALF], spec[q][:, HALF:]
            h_re, h_im = prop[0, q], prop[1, q]
            turned.append(lanes_cat(re * h_re + im * h_im, im * h_re - re * h_im))
        e_re, e_im = inverse(tables, *turned)
        p_re, p_im = rolled[iteration, slot, 0], rolled[iteration, slot, 1]
        placed(below, right, p_re * e_re + p_im * e_im, 0, stay, move)
        placed(below, right, p_re * e_im - p_im * e_re, 1, stay, move)
        return carry

    lax.fori_loop(0, cnt_ref[iteration], body, 0)


SMEM = pl.BlockSpec(memory_space=pltpu.SMEM)
VMEM = pl.BlockSpec(memory_space=pltpu.VMEM)
LIMIT = 24 * 1024 * 1024


def f32(*shape):
    return jax.ShapeDtypeStruct(shape, jnp.float32)


def call(body, scalars, arrays, outs, scratch=()):
    args = [*scalars, *arrays]
    return pl.pallas_call(
        body,
        out_shape=outs,
        in_specs=[SMEM] * len(scalars) + [VMEM] * len(arrays),
        out_specs=[VMEM] * len(outs),
        scratch_shapes=scratch,
        compiler_params=pltpu.CompilerParams(vmem_limit_bytes=LIMIT),
        cost_estimate=pl.CostEstimate(flops=4 * 10**9, bytes_accessed=8 * 2**20, transcendentals=0),
    )(*args)


def shards(object_tiles, probe_field, prop_angle, scan_offsets, probe_counts, amplitudes):
    tables = jnp.asarray(dft_tables())
    lane = np.arange(SIDE)
    source = np.concatenate([lane[0::2], lane[1::2]])
    perm = np.zeros((SIDE, SIDE), np.float32)
    perm[source, lane] = 1.0
    perm = jnp.asarray(np.stack([perm.T, perm]).astype(jnp.bfloat16))
    offsets = scan_offsets.reshape(ITERS, SLOTS, 2)
    counts = probe_counts.reshape(ITERS)
    measured = amplitudes.reshape(ITERS, SLOTS, SIDE, SIDE)

    own = [object_tiles[0], object_tiles[1]]
    low, rgt, dia = [None, None], [None, None], [None, None]
    for s in (0, 1):
        low[s] = shifted(own[s], "ty", -1)
        rgt[s] = shifted(own[s], "tx", -1)
    for s in (0, 1):
        dia[s] = shifted(low[s], "tx", -1)

    rolled, prop, ampl = call(
        prepare_kernel, [offsets],
        [probe_field, jnp.cos(prop_angle), jnp.sin(prop_angle), measured, perm],
        [f32(ITERS, SLOTS, 2, SIDE, SIDE), f32(2, 2, SIDE, HALF), f32(ITERS, SLOTS, 2, SIDE, HALF)],
        [pltpu.VMEM((2, 2 * SIDE, SIDE), jnp.float32)],
    )
    pair = f32(2, 2, SIDE, SIDE)

    for iteration in range(ITERS):
        def bind(kernel, iteration=iteration):
            return lambda *refs: kernel(iteration, *refs)

        scalars = [offsets, counts]
        (mid,) = call(bind(first_kernel), scalars,
                      [own[0], rgt[0], low[0], dia[0], rolled, prop, tables], [pair])
        stay2, move2, carry = call(bind(second_kernel), scalars,
                                   [own[1], rgt[1], low[1], dia[1], mid, ampl, tables], [pair] * 3)
        stay1, move1 = call(bind(third_kernel), scalars,
                            [carry, rolled, prop, tables], [pair] * 2)
        stay, move = [stay1, stay2], [move1, move2]
        last = iteration == ITERS - 1
        came, above, below = [None, None], [None, None], [None, None]
        for s in (1, 0):
            came[s] = shifted(move[s], "tx", 1)
            sums = (stay[s][0] + came[s][0], stay[s][1] + came[s][1])
            above[s], below[s] = lax.optimization_barrier(sums)
        for s in (1, 0):
            from_above = shifted(below[s], "ty", 1)
            if last:
                own[s] = own[s] - step_size * (above[s] + from_above)
                continue
            from_below = shifted(above[s], "ty", -1)
            own[s] = own[s] - step_size * (above[s] + from_above)
            low[s] = low[s] - step_size * (from_below + below[s])
            both = shifted(jnp.stack([own[s], low[s]]), "tx", -1)
            rgt[s], dia[s] = both[0], both[1]
    return jnp.stack(own)


def solution(mesh):
    in_specs = (
        P(None, None, "ty", "tx"),
        P(),
        P(),
        P(None, "ty", "tx", None, None),
        P(None, "ty", "tx"),
        P(None, "ty", "tx", None, None, None),
    )
    out_specs = P(None, None, "ty", "tx")

    return jax.shard_map(shards, mesh=mesh, in_specs=in_specs, out_specs=out_specs, check_vma=False)
```

profile of v0, /device:TPU:172, one launch (start us, length us, event | category | flops | bytes accessed | tf_op | source)
XLA Modules:
  0.0 281.3 jit_solution(8563358554127134510)
XLA Ops:
  0.0 1.4 slice_bitcast_fusion.5
  1.5 2.5 collective-permute-start.4
  3.9 1.9 collective-permute-start.1
  5.9 1.9 collective-permute-start.3
  7.8 2.5 collective-permute-start
  10.3 15.4 %collective-permute-done.4.refs_4_ = f32[2,256,256]{2,1,0:T(8,128)S(1)} collective-permute-done((f32[2,256,256]{2,1,0:T(8,128)S(1)}, f32[2,256,256]{2,1,0:T(8,128)S(1)}, u32[]{:S(2)}, u32[]{:S(2)}) %collective-permute-start.4) | collective-permute-done | bytes 524320 | tf_op jit(solution)/shard_map/ppermute | solution.py:36
  25.7 13.1 %collective-permute-start.5 = (f32[2,256,256]{2,1,0:T(8,128)S(1)}, f32[2,256,256]{2,1,0:T(8,128)S(1)}, u32[]{:S(2)}, u32[]{:S(2)}) collective-permute-start(f32[2,256,256]{2,1,0:T(8,128)S(1)} %collective-permute-done.4.refs_4_), channel_id=1, source_target_pairs={{1,0},{2,1},{3,2},{4,3},{5,4},{6,5},{7,6},{8,7},{9,8},{10,9},{11,1... | collective-permute-start | bytes 1572872 | tf_op jit(solution)/shard_map/ppermute | solution.py:36
  38.8 1.0 fusion.8
  39.8 11.0 %collective-permute-done.1.refs_4_ = f32[2,256,256]{2,1,0:T(8,128)S(1)} collective-permute-done((f32[2,256,256]{2,1,0:T(8,128)S(1)}, f32[2,256,256]{2,1,0:T(8,128)S(1)}, u32[]{:S(2)}, u32[]{:S(2)}) %collective-permute-start.1) | collective-permute-done | bytes 524320 | tf_op jit(solution)/shard_map/ppermute | solution.py:36
  50.8 2.3 collective-permute-start.2
  53.1 0.0 copy-done.5
  53.1 0.0 copy-done
  53.1 0.0 copy-start.3
  53.1 0.0 copy-start.4
  53.1 3.6 %shard_map.82 = (f32[2,2,2,256,256]{4,3,2,1,0:T(8,128)S(1)}, f32[2,2,256,128]{3,2,1,0:T(8,128)S(1)}, f32[2,2,2,256,128]{4,3,2,1,0:T(8,128)S(1)}) custom-call(s32[2,2,2]{2,1,0:T(2,128)S(1)} %bitcast.48, f32[2,256,256]{2,1,0:T(8,128)S(1)} %copy-done.1, f32[256,256]{1,0:T(8,128)S(1)} %get-tuple-element.64.cos_ref, f32[256,256]{1,0:T(8,128)S(1)} %get-tuple-element.63.sin_ref, ...), custom_call_target="tpu_custom_call" | custom-call | flops 4000000000 | bytes 8388608 | tf_op jit(solution)/shard_map/pallas_call | solution.py:229
  56.8 0.0 collective-permute-done.3.refs_3_
  56.8 8.9 %collective-permute-done.5.refs_5_ = f32[2,256,256]{2,1,0:T(8,128)S(1)} collective-permute-done((f32[2,256,256]{2,1,0:T(8,128)S(1)}, f32[2,256,256]{2,1,0:T(8,128)S(1)}, u32[]{:S(2)}, u32[]{:S(2)}) %collective-permute-start.5) | collective-permute-done | bytes 524320 | tf_op jit(solution)/shard_map/ppermute | solution.py:36
  65.7 0.6 shard_map.83.refs_6_
  66.3 0.0 collective-permute-done.refs_3_
  66.3 10.4 %collective-permute-done.2.refs_5_ = f32[2,256,256]{2,1,0:T(8,128)S(1)} collective-permute-done((f32[2,256,256]{2,1,0:T(8,128)S(1)}, f32[2,256,256]{2,1,0:T(8,128)S(1)}, u32[]{:S(2)}, u32[]{:S(2)}) %collective-permute-start.2) | collective-permute-done | bytes 524320 | tf_op jit(solution)/shard_map/ppermute | solution.py:36
  76.7 0.7 shard_map.84
  77.4 0.7 shard_map.85
  78.1 1.9 collective-permute-start.6
  80.0 1.9 collective-permute-start.8
  81.9 33.7 %collective-permute-done.6 = f32[2,2,256,256]{3,2,1,0:T(8,128)S(1)} collective-permute-done((f32[2,2,256,256]{3,2,1,0:T(8,128)S(1)}, f32[2,2,256,256]{3,2,1,0:T(8,128)S(1)}, u32[]{:S(2)}, u32[]{:S(2)}) %collective-permute-start.6) | collective-permute-done | bytes 1048608 | tf_op jit(solution)/shard_map/ppermute | solution.py:36
  115.7 0.1 fusion.6
  115.8 0.0 copy-start.6
  115.8 2.1 collective-permute-start.7
  117.9 24.9 %collective-permute-done.8 = f32[2,2,256,256]{3,2,1,0:T(8,128)S(1)} collective-permute-done((f32[2,2,256,256]{3,2,1,0:T(8,128)S(1)}, f32[2,2,256,256]{3,2,1,0:T(8,128)S(1)}, u32[]{:S(2)}, u32[]{:S(2)}) %collective-permute-start.8) | collective-permute-done | bytes 1048608 | tf_op jit(solution)/shard_map/ppermute | solution.py:36
  142.8 0.1 fusion.4
  143.0 1.9 collective-permute-start.9
  144.9 6.0 %collective-permute-start.12 = (f32[2,256,256]{2,1,0:T(8,128)S(1)}, f32[2,256,256]{2,1,0:T(8,128)S(1)}, u32[]{:S(2)}, u32[]{:S(2)}) collective-permute-start(f32[2,256,256]{2,1,0:T(8,128)S(1)} %get-tuple-element.32), channel_id=1, source_target_pairs={{16,0},{32,16},{48,32},{64,48},{80,64},{96,80},{112,96},{128,112},... | collective-permute-start | bytes 1572872 | tf_op jit(solution)/shard_map/ppermute | solution.py:36
  151.0 4.4 %collective-permute-start.10 = (f32[2,256,256]{2,1,0:T(8,128)S(1)}, f32[2,256,256]{2,1,0:T(8,128)S(1)}, u32[]{:S(2)}, u32[]{:S(2)}) collective-permute-start(f32[2,256,256]{2,1,0:T(8,128)S(1)} %get-tuple-element.36), channel_id=1, source_target_pairs={{16,0},{32,16},{48,32},{64,48},{80,64},{96,80},{112,96},{128,112},... | collective-permute-start | bytes 1572872 | tf_op jit(solution)/shard_map/ppermute | solution.py:36
  155.4 0.0 collective-permute-done.7
  155.4 3.3 %collective-permute-done.9 = f32[2,256,256]{2,1,0:T(8,128)S(1)} collective-permute-done((f32[2,256,256]{2,1,0:T(8,128)S(1)}, f32[2,256,256]{2,1,0:T(8,128)S(1)}, u32[]{:S(2)}, u32[]{:S(2)}) %collective-permute-start.9) | collective-permute-done | bytes 524320 | tf_op jit(solution)/shard_map/ppermute | solution.py:36
  158.7 0.2 multiply_subtract_fusion.3
  158.9 6.0 %collective-permute-done.12 = f32[2,256,256]{2,1,0:T(8,128)S(1)} collective-permute-done((f32[2,256,256]{2,1,0:T(8,128)S(1)}, f32[2,256,256]{2,1,0:T(8,128)S(1)}, u32[]{:S(2)}, u32[]{:S(2)}) %collective-permute-start.12) | collective-permute-done | bytes 524320 | tf_op jit(solution)/shard_map/ppermute | solution.py:36
  164.9 0.1 multiply_subtract_fusion.refs_4_
  165.0 0.1 pad_maximum_fusion.1
  165.1 5.4 %collective-permute-start.13 = (f32[2,2,256,256]{3,2,1,0:T(8,128)S(1)}, f32[2,2,256,256]{3,2,1,0:T(8,128)S(1)}, u32[]{:S(2)}, u32[]{:S(2)}) collective-permute-start(f32[2,2,256,256]{3,2,1,0:T(8,128)S(1)} %pad_maximum_fusion.1), channel_id=1, source_target_pairs={{1,0},{2,1},{3,2},{4,3},{5,4},{6,5},{7,6},{8,7},{9,8},{10,9},{11,1... | collective-permute-start | bytes 3145736 | tf_op jit(solution)/shard_map/ppermute | solution.py:36
  170.5 2.4 collective-permute-done.10
  172.9 0.1 multiply_subtract_fusion.1.refs_4_
  173.1 0.1 pad_maximum_fusion
  173.1 1.9 collective-permute-start.11
  175.1 7.9 %collective-permute-done.13 = f32[2,2,256,256]{3,2,1,0:T(8,128)S(1)} collective-permute-done((f32[2,2,256,256]{3,2,1,0:T(8,128)S(1)}, f32[2,2,256,256]{3,2,1,0:T(8,128)S(1)}, u32[]{:S(2)}, u32[]{:S(2)}) %collective-permute-start.13) | collective-permute-done | bytes 1048608 | tf_op jit(solution)/shard_map/ppermute | solution.py:36
  183.0 0.1 slice_bitcast_fusion
  183.1 0.6 shard_map.86.refs_6_
  183.7 12.7 %collective-permute-done.11 = f32[2,2,256,256]{3,2,1,0:T(8,128)S(1)} collective-permute-done((f32[2,2,256,256]{3,2,1,0:T(8,128)S(1)}, f32[2,2,256,256]{3,2,1,0:T(8,128)S(1)}, u32[]{:S(2)}, u32[]{:S(2)}) %collective-permute-start.11) | collective-permute-done | bytes 1048608 | tf_op jit(solution)/shard_map/ppermute | solution.py:36
  196.3 0.1 slice_bitcast_fusion.2
  196.4 0.7 shard_map.87
  197.1 0.7 shard_map.88
  197.8 1.9 collective-permute-start.14
  199.8 1.9 collective-permute-start.16
  201.7 36.8 %collective-permute-done.14 = f32[2,2,256,256]{3,2,1,0:T(8,128)S(1)} collective-permute-done((f32[2,2,256,256]{3,2,1,0:T(8,128)S(1)}, f32[2,2,256,256]{3,2,1,0:T(8,128)S(1)}, u32[]{:S(2)}, u32[]{:S(2)}) %collective-permute-start.14) | collective-permute-done | bytes 1048608 | tf_op jit(solution)/shard_map/ppermute | solution.py:36
  238.5 0.2 fusion.2
  238.7 3.6 %collective-permute-start.15 = (f32[2,256,256]{2,1,0:T(8,128)S(1)}, f32[2,256,256]{2,1,0:T(8,128)S(1)}, u32[]{:S(2)}, u32[]{:S(2)}) collective-permute-start(f32[2,256,256]{2,1,0:T(8,128)S(1)} %get-tuple-element.42), channel_id=1, source_target_pairs={{0,16},{16,32},{32,48},{48,64},{64,80},{80,96},{96,112},{112,128},... | collective-permute-start | bytes 1572872 | tf_op jit(solution)/shard_map/ppermute | solution.py:36
  242.3 18.9 %collective-permute-done.16 = f32[2,2,256,256]{3,2,1,0:T(8,128)S(1)} collective-permute-done((f32[2,2,256,256]{3,2,1,0:T(8,128)S(1)}, f32[2,2,256,256]{3,2,1,0:T(8,128)S(1)}, u32[]{:S(2)}, u32[]{:S(2)}) %collective-permute-start.16) | collective-permute-done | bytes 1048608 | tf_op jit(solution)/shard_map/ppermute | solution.py:36
  261.2 0.1 fusion
  261.3 2.7 collective-permute-start.17
  264.0 0.0 collective-permute-done.15
  264.0 0.1 subtract_bitcast_fusion.1
  264.1 16.0 %collective-permute-done.17 = f32[2,256,256]{2,1,0:T(8,128)S(1)} collective-permute-done((f32[2,256,256]{2,1,0:T(8,128)S(1)}, f32[2,256,256]{2,1,0:T(8,128)S(1)}, u32[]{:S(2)}, u32[]{:S(2)}) %collective-permute-start.17) | collective-permute-done | bytes 524320 | tf_op jit(solution)/shard_map/ppermute | solution.py:36
  280.1 0.1 subtract_bitcast_fusion
  280.3 1.0 pad_maximum_fusion.2
  (11 shorter events, 0.0 us)
Async XLA Ops:
  0.0 53.1 %copy-start.5 = (bf16[2,256,256]{2,1,0:T(8,128)(2,1)S(1)}, bf16[2,256,256]{2,1,0:T(8,128)(2,1)}, u32[]{:S(2)}) copy-start(bf16[2,256,256]{2,1,0:T(8,128)(2,1)} %constant.7.clone.perm_ref) | copy-start | bytes 786436
  0.0 38.8 %copy-start.7 = (f32[256,256]{1,0:T(8,128)S(1)}, f32[256,256]{1,0:T(8,128)}, u32[]{:S(2)}) copy-start(f32[256,256]{1,0:T(8,128)} %param.10) | copy-start | bytes 786436
  0.0 53.1 %copy-start = (f32[2,1,1,2,256,256]{5,4,3,2,1,0:T(8,128)S(1)}, f32[2,1,1,2,256,256]{5,4,3,2,1,0:T(8,128)}, u32[]{:S(2)}) copy-start(f32[2,1,1,2,256,256]{5,4,3,2,1,0:T(8,128)} %param.13) | copy-start | bytes 3145732
  0.0 53.1 %copy-start.2 = (s32[2,1,1,2,2]{4,3,2,1,0:T(2,128)S(1)}, s32[2,1,1,2,2]{4,3,2,1,0:T(2,128)}, u32[]{:S(2)}) copy-start(s32[2,1,1,2,2]{4,3,2,1,0:T(2,128)} %param.11) | copy-start | bytes 100
  0.0 53.1 %copy-start.1 = (f32[2,256,256]{2,1,0:T(8,128)S(1)}, f32[2,256,256]{2,1,0:T(8,128)}, u32[]{:S(2)}) copy-start(f32[2,256,256]{2,1,0:T(8,128)} %probe_ref.1) | copy-start | bytes 1572868
  1.5 24.3 %collective-permute-start.4 = (f32[2,256,256]{2,1,0:T(8,128)S(1)}, f32[2,256,256]{2,1,0:T(8,128)S(1)}, u32[]{:S(2)}, u32[]{:S(2)}) collective-permute-start(f32[2,256,256]{2,1,0:T(8,128)S(1)} %get-tuple-element.61.refs_2_), channel_id=1, source_target_pairs={{16,0},{32,16},{48,32},{64,48},{80,64},{96,80},{112,96},{128,112},... | collective-permute-start | bytes 1572872 | tf_op jit(solution)/shard_map/ppermute | solution.py:36
  3.9 46.9 %collective-permute-start.1 = (f32[2,256,256]{2,1,0:T(8,128)S(1)}, f32[2,256,256]{2,1,0:T(8,128)S(1)}, u32[]{:S(2)}, u32[]{:S(2)}) collective-permute-start(f32[2,256,256]{2,1,0:T(8,128)S(1)} %get-tuple-element.62.refs_2_), channel_id=1, source_target_pairs={{16,0},{32,16},{48,32},{64,48},{80,64},{96,80},{112,96},{128,112},... | collective-permute-start | bytes 1572872 | tf_op jit(solution)/shard_map/ppermute | solution.py:36
  5.9 50.9 %collective-permute-start.3 = (f32[2,256,256]{2,1,0:T(8,128)S(1)}, f32[2,256,256]{2,1,0:T(8,128)S(1)}, u32[]{:S(2)}, u32[]{:S(2)}) collective-permute-start(f32[2,256,256]{2,1,0:T(8,128)S(1)} %get-tuple-element.61.refs_2_), channel_id=1, source_target_pairs={{1,0},{2,1},{3,2},{4,3},{5,4},{6,5},{7,6},{8,7},{9,8},{10,9},{11,1... | collective-permute-start | bytes 1572872 | tf_op jit(solution)/shard_map/ppermute | solution.py:36
  7.8 58.5 %collective-permute-start = (f32[2,256,256]{2,1,0:T(8,128)S(1)}, f32[2,256,256]{2,1,0:T(8,128)S(1)}, u32[]{:S(2)}, u32[]{:S(2)}) collective-permute-start(f32[2,256,256]{2,1,0:T(8,128)S(1)} %get-tuple-element.62.refs_2_), channel_id=1, source_target_pairs={{1,0},{2,1},{3,2},{4,3},{5,4},{6,5},{7,6},{8,7},{9,8},{10,9},{11,1... | collective-permute-start | bytes 1572872 | tf_op jit(solution)/shard_map/ppermute | solution.py:36
  25.7 40.0 %collective-permute-start.5 = (f32[2,256,256]{2,1,0:T(8,128)S(1)}, f32[2,256,256]{2,1,0:T(8,128)S(1)}, u32[]{:S(2)}, u32[]{:S(2)}) collective-permute-start(f32[2,256,256]{2,1,0:T(8,128)S(1)} %collective-permute-done.4.refs_4_), channel_id=1, source_target_pairs={{1,0},{2,1},{3,2},{4,3},{5,4},{6,5},{7,6},{8,7},{9,8},{10,9},{11,1... | collective-permute-start | bytes 1572872 | tf_op jit(solution)/shard_map/ppermute | solution.py:36
  50.8 25.8 %collective-permute-start.2 = (f32[2,256,256]{2,1,0:T(8,128)S(1)}, f32[2,256,256]{2,1,0:T(8,128)S(1)}, u32[]{:S(2)}, u32[]{:S(2)}) collective-permute-start(f32[2,256,256]{2,1,0:T(8,128)S(1)} %collective-permute-done.1.refs_4_), channel_id=1, source_target_pairs={{1,0},{2,1},{3,2},{4,3},{5,4},{6,5},{7,6},{8,7},{9,8},{10,9},{11,1... | collective-permute-start | bytes 1572872 | tf_op jit(solution)/shard_map/ppermute | solution.py:36
  53.1 12.6 %copy-start.3 = (s32[2,1,1]{0,2,1:T(1,128)S(1)}, s32[2,1,1]{0,2,1:T(1,128)}, u32[]{:S(2)}) copy-start(s32[2,1,1]{0,2,1:T(1,128)} %param.12) | copy-start | bytes 28
  53.1 12.6 %copy-start.4 = (bf16[2,2,2,256,256]{4,3,2,1,0:T(8,128)(2,1)S(1)}, bf16[2,2,2,256,256]{4,3,2,1,0:T(8,128)(2,1)}, u32[]{:S(2)}) copy-start(bf16[2,2,2,256,256]{4,3,2,1,0:T(8,128)(2,1)} %constant.6.clone.refs_8_.refs_5_) | copy-start | bytes 3145732
  78.1 37.6 %collective-permute-start.6 = (f32[2,2,256,256]{3,2,1,0:T(8,128)S(1)}, f32[2,2,256,256]{3,2,1,0:T(8,128)S(1)}, u32[]{:S(2)}, u32[]{:S(2)}) collective-permute-start(f32[2,2,256,256]{3,2,1,0:T(8,128)S(1)} %get-tuple-element.31), channel_id=1, source_target_pairs={{0,1},{1,2},{2,3},{3,4},{4,5},{5,6},{6,7},{7,8},{8,9},{9,10},{10,1... | collective-permute-start | bytes 3145736 | tf_op jit(solution)/shard_map/ppermute | solution.py:36
  80.0 62.8 %collective-permute-start.8 = (f32[2,2,256,256]{3,2,1,0:T(8,128)S(1)}, f32[2,2,256,256]{3,2,1,0:T(8,128)S(1)}, u32[]{:S(2)}, u32[]{:S(2)}) collective-permute-start(f32[2,2,256,256]{3,2,1,0:T(8,128)S(1)} %get-tuple-element.35), channel_id=1, source_target_pairs={{0,1},{1,2},{2,3},{3,4},{4,5},{5,6},{6,7},{7,8},{8,9},{9,10},{10,1... | collective-permute-start | bytes 3145736 | tf_op jit(solution)/shard_map/ppermute | solution.py:36
  115.8 42.9 %copy-start.6 = (f32[2,2,256,256]{3,2,1,0:T(8,128)S(1)}, f32[2,2,256,256]{3,2,1,0:T(8,128)}, u32[]{:S(2)}) copy-start(f32[2,2,256,256]{3,2,1,0:T(8,128)} %param.8) | copy-start | bytes 3145732
  115.8 39.5 %collective-permute-start.7 = (f32[2,256,256]{2,1,0:T(8,128)S(1)}, f32[2,256,256]{2,1,0:T(8,128)S(1)}, u32[]{:S(2)}, u32[]{:S(2)}) collective-permute-start(f32[2,256,256]{2,1,0:T(8,128)S(1)} %get-tuple-element.33), channel_id=1, source_target_pairs={{0,16},{16,32},{32,48},{48,64},{64,80},{80,96},{96,112},{112,128},... | collective-permute-start | bytes 1572872 | tf_op jit(solution)/shard_map/ppermute | solution.py:36
  143.0 15.7 %collective-permute-start.9 = (f32[2,256,256]{2,1,0:T(8,128)S(1)}, f32[2,256,256]{2,1,0:T(8,128)S(1)}, u32[]{:S(2)}, u32[]{:S(2)}) collective-permute-start(f32[2,256,256]{2,1,0:T(8,128)S(1)} %get-tuple-element.37), channel_id=1, source_target_pairs={{0,16},{16,32},{32,48},{48,64},{64,80},{80,96},{96,112},{112,128},... | collective-permute-start | bytes 1572872 | tf_op jit(solution)/shard_map/ppermute | solution.py:36
  144.9 20.0 %collective-permute-start.12 = (f32[2,256,256]{2,1,0:T(8,128)S(1)}, f32[2,256,256]{2,1,0:T(8,128)S(1)}, u32[]{:S(2)}, u32[]{:S(2)}) collective-permute-start(f32[2,256,256]{2,1,0:T(8,128)S(1)} %get-tuple-element.32), channel_id=1, source_target_pairs={{16,0},{32,16},{48,32},{64,48},{80,64},{96,80},{112,96},{128,112},... | collective-permute-start | bytes 1572872 | tf_op jit(solution)/shard_map/ppermute | solution.py:36
  151.0 22.0 %collective-permute-start.10 = (f32[2,256,256]{2,1,0:T(8,128)S(1)}, f32[2,256,256]{2,1,0:T(8,128)S(1)}, u32[]{:S(2)}, u32[]{:S(2)}) collective-permute-start(f32[2,256,256]{2,1,0:T(8,128)S(1)} %get-tuple-element.36), channel_id=1, source_target_pairs={{16,0},{32,16},{48,32},{64,48},{80,64},{96,80},{112,96},{128,112},... | collective-permute-start | bytes 1572872 | tf_op jit(solution)/shard_map/ppermute | solution.py:36
  165.1 17.9 %collective-permute-start.13 = (f32[2,2,256,256]{3,2,1,0:T(8,128)S(1)}, f32[2,2,256,256]{3,2,1,0:T(8,128)S(1)}, u32[]{:S(2)}, u32[]{:S(2)}) collective-permute-start(f32[2,2,256,256]{3,2,1,0:T(8,128)S(1)} %pad_maximum_fusion.1), channel_id=1, source_target_pairs={{1,0},{2,1},{3,2},{4,3},{5,4},{6,5},{7,6},{8,7},{9,8},{10,9},{11,1... | collective-permute-start | bytes 3145736 | tf_op jit(solution)/shard_map/ppermute | solution.py:36
  173.1 23.2 %collective-permute-start.11 = (f32[2,2,256,256]{3,2,1,0:T(8,128)S(1)}, f32[2,2,256,256]{3,2,1,0:T(8,128)S(1)}, u32[]{:S(2)}, u32[]{:S(2)}) collective-permute-start(f32[2,2,256,256]{3,2,1,0:T(8,128)S(1)} %pad_maximum_fusion), channel_id=1, source_target_pairs={{1,0},{2,1},{3,2},{4,3},{5,4},{6,5},{7,6},{8,7},{9,8},{10,9},{11,1... | collective-permute-start | bytes 3145736 | tf_op jit(solution)/shard_map/ppermute | solution.py:36
  197.8 40.6 %collective-permute-start.14 = (f32[2,2,256,256]{3,2,1,0:T(8,128)S(1)}, f32[2,2,256,256]{3,2,1,0:T(8,128)S(1)}, u32[]{:S(2)}, u32[]{:S(2)}) collective-permute-start(f32[2,2,256,256]{3,2,1,0:T(8,128)S(1)} %get-tuple-element.40), channel_id=1, source_target_pairs={{0,1},{1,2},{2,3},{3,4},{4,5},{5,6},{6,7},{7,8},{8,9},{9,10},{10,1... | collective-permute-start | bytes 3145736 | tf_op jit(solution)/shard_map/ppermute | solution.py:36
  199.8 61.4 %collective-permute-start.16 = (f32[2,2,256,256]{3,2,1,0:T(8,128)S(1)}, f32[2,2,256,256]{3,2,1,0:T(8,128)S(1)}, u32[]{:S(2)}, u32[]{:S(2)}) collective-permute-start(f32[2,2,256,256]{3,2,1,0:T(8,128)S(1)} %get-tuple-element.44), channel_id=1, source_target_pairs={{0,1},{1,2},{2,3},{3,4},{4,5},{5,6},{6,7},{7,8},{8,9},{9,10},{10,1... | collective-permute-start | bytes 3145736 | tf_op jit(solution)/shard_map/ppermute | solution.py:36
  238.7 25.3 %collective-permute-start.15 = (f32[2,256,256]{2,1,0:T(8,128)S(1)}, f32[2,256,256]{2,1,0:T(8,128)S(1)}, u32[]{:S(2)}, u32[]{:S(2)}) collective-permute-start(f32[2,256,256]{2,1,0:T(8,128)S(1)} %get-tuple-element.42), channel_id=1, source_target_pairs={{0,16},{16,32},{32,48},{48,64},{64,80},{80,96},{96,112},{112,128},... | collective-permute-start | bytes 1572872 | tf_op jit(solution)/shard_map/ppermute | solution.py:36
  261.3 18.9 %collective-permute-start.17 = (f32[2,256,256]{2,1,0:T(8,128)S(1)}, f32[2,256,256]{2,1,0:T(8,128)S(1)}, u32[]{:S(2)}, u32[]{:S(2)}) collective-permute-start(f32[2,256,256]{2,1,0:T(8,128)S(1)} %get-tuple-element.46), channel_id=1, source_target_pairs={{0,16},{16,32},{32,48},{48,64},{64,80},{80,96},{96,112},{112,128},... | collective-permute-start | bytes 1572872 | tf_op jit(solution)/shard_map/ppermute | solution.py:36
where the time goes:
time: 286 us; the launch traced here: 281 us
  waiting for transfers between devices  208 us (73%)
  starting transfers between devices  59.8 us (21%)
  Pallas kernels  7.61 us (3%)
    ppermute x18, waiting for transfers between devices, shifted(): lax.ppermute(value, axis, [(source, source + steps) for source in range(f...  208 us
    ppermute x18, starting transfers between devices, shifted(): lax.ppermute(value, axis, [(source, source + steps) for source in range(f...  59.8 us
    pallas_call x7, Pallas kernels, call(): pl.pallas_call(body, out_shape=outs, in_specs=[SMEM] * len(scalars) + [VM...  7.61 us
  transfers between devices with their start and end apart: 18, of which 14 were waited for; matrix products, arithmetic and copies ran while one was open for 1% of the time, Pallas kernels for 2%

commit v1 on v0

--- a/solution.py
+++ b/solution.py
@@ -91,6 +91,13 @@
     )
 
 
+def four(tiles):
+    if len(tiles) == 4:
+        return tiles
+    mine, theirs = tiles
+    return mine.at[0], theirs.at[0], mine.at[1], theirs.at[1]
+
+
 def masks(off_ref, iteration, slot):
     row = off_ref[iteration, slot, 0]
     col = off_ref[iteration, slot, 1]
@@ -150,7 +157,10 @@
     lax.fori_loop(0, ITERS * SLOTS, tile_loop, 0)
 
 
-def first_kernel(iteration, off_ref, cnt_ref, own, rgt, low, dia, rolled, prop, tables, mid_ref):
+def first_kernel(iteration, off_ref, cnt_ref, rolled, prop, tables, *refs):
+    *tiles, mid_ref = refs
+    own, rgt, low, dia = four(tiles)
+
     def body(slot, carry):
         below, right = masks(off_ref, iteration, slot)
         one_re = picked(below, right, own, rgt, low, dia, 0)
@@ -168,8 +178,9 @@
     lax.fori_loop(0, cnt_ref[iteration], body, 0)
 
 
-def second_kernel(iteration, off_ref, cnt_ref, own, rgt, low, dia, mid_ref, ampl, tables,
-                  stay, move, carry_ref):
+def second_kernel(iteration, off_ref, cnt_ref, mid_ref, ampl, tables, *refs):
+    *tiles, stay, move, carry_ref = refs
+    own, rgt, low, dia = four(tiles)
     stay[...] = jnp.zeros_like(stay)
     move[...] = jnp.zeros_like(move)
 
@@ -215,6 +226,17 @@
     lax.fori_loop(0, cnt_ref[iteration], body, 0)
 
 
+def update_kernel(above, below, from_above, from_below, *refs):
+    *tiles, mine = refs
+    mine[0] = tiles[0][...] - step_size * (above[...] + from_above[...])
+    mine[1] = tiles[1][...] - step_size * (from_below[...] + below[...])
+
+
+def last_kernel(one, two, above1, above2, from_above1, from_above2, out):
+    out[0] = one[0] - step_size * (above1[...] + from_above1[...])
+    out[1] = two[0] - step_size * (above2[...] + from_above2[...])
+
+
 SMEM = pl.BlockSpec(memory_space=pltpu.SMEM)
 VMEM = pl.BlockSpec(memory_space=pltpu.VMEM)
 LIMIT = 24 * 1024 * 1024
@@ -224,7 +246,7 @@
     return jax.ShapeDtypeStruct(shape, jnp.float32)
 
 
-def call(body, scalars, arrays, outs, scratch=()):
+def call(body, scalars, arrays, outs, scratch=(), flops=4 * 10**9):
     args = [*scalars, *arrays]
     return pl.pallas_call(
         body,
@@ -233,7 +255,7 @@
         out_specs=[VMEM] * len(outs),
         scratch_shapes=scratch,
         compiler_params=pltpu.CompilerParams(vmem_limit_bytes=LIMIT),
-        cost_estimate=pl.CostEstimate(flops=4 * 10**9, bytes_accessed=8 * 2**20, transcendentals=0),
+        cost_estimate=pl.CostEstimate(flops=flops, bytes_accessed=8 * 2**20, transcendentals=0),
     )(*args)
 
 
@@ -264,35 +286,36 @@
     )
     pair = f32(2, 2, SIDE, SIDE)
 
+    tiles = [[own[s], rgt[s], low[s], dia[s]] for s in (0, 1)]
+
     for iteration in range(ITERS):
         def bind(kernel, iteration=iteration):
             return lambda *refs: kernel(iteration, *refs)
 
         scalars = [offsets, counts]
-        (mid,) = call(bind(first_kernel), scalars,
-                      [own[0], rgt[0], low[0], dia[0], rolled, prop, tables], [pair])
+        (mid,) = call(bind(first_kernel), scalars, [rolled, prop, tables, *tiles[0]], [pair])
         stay2, move2, carry = call(bind(second_kernel), scalars,
-                                   [own[1], rgt[1], low[1], dia[1], mid, ampl, tables], [pair] * 3)
+                                   [mid, ampl, tables, *tiles[1]], [pair] * 3)
         stay1, move1 = call(bind(third_kernel), scalars,
                             [carry, rolled, prop, tables], [pair] * 2)
         stay, move = [stay1, stay2], [move1, move2]
-        last = iteration == ITERS - 1
-        came, above, below = [None, None], [None, None], [None, None]
+        above, below, came = [None, None], [None, None], [None, None]
         for s in (1, 0):
             came[s] = shifted(move[s], "tx", 1)
             sums = (stay[s][0] + came[s][0], stay[s][1] + came[s][1])
             above[s], below[s] = lax.optimization_barrier(sums)
+        from_above = [None, None]
         for s in (1, 0):
-            from_above = shifted(below[s], "ty", 1)
-            if last:
-                own[s] = own[s] - step_size * (above[s] + from_above)
+            from_above[s] = shifted(below[s], "ty", 1)
+            if iteration == ITERS - 1:
                 continue
             from_below = shifted(above[s], "ty", -1)
-            own[s] = own[s] - step_size * (above[s] + from_above)
-            low[s] = low[s] - step_size * (from_below + below[s])
-            both = shifted(jnp.stack([own[s], low[s]]), "tx", -1)
-            rgt[s], dia[s] = both[0], both[1]
-    return jnp.stack(own)
+            held = [tiles[s][0], tiles[s][2]]
+            (mine,) = call(update_kernel, [],
+                           [above[s], below[s], from_above[s], from_below, *held], [pair], flops=10**6)
+            tiles[s] = [mine, shifted(mine, "tx", -1)]
+    (out,) = call(last_kernel, [], [tiles[0][0], tiles[1][0], *above, *from_above], [pair], flops=10**6)
+    return out
 
 
 def solution(mesh):

time: 286 us -> 271 us (0.948)
  the two profiles are of different devices: /device:TPU:172 before, /device:TPU:23 now
where the time goes in v1:
time: 271 us; the launch traced here: 270 us
  waiting for transfers between devices  172 us (63%)
  starting transfers between devices  75.2 us (28%)
  Pallas kernels  19.5 us (7%)
    ppermute x18, waiting for transfers between devices, shifted(): lax.ppermute(value, axis, [(source, source + steps) for source in range(f...  172 us
    ppermute x18, starting transfers between devices, shifted(): lax.ppermute(value, axis, [(source, source + steps) for source in range(f...  75.2 us
    pallas_call x10, Pallas kernels, call(): pl.pallas_call(body, out_shape=outs, in_specs=[SMEM] * len(scalars) + [VM...  19.5 us
  transfers between devices with their start and end apart: 18, of which 14 were waited for; matrix products, arithmetic and copies ran while one was open for 1% of the time, Pallas kernels for 3%

profile of v1, /device:TPU:23, one launch (start us, length us, event | category | flops | bytes accessed | tf_op | source)
XLA Modules:
  0.0 270.1 jit_solution(11596447119990229813)
XLA Ops:
  0.0 0.0 copy-start.5
  0.0 0.0 copy-start.2
  0.0 0.0 copy-start.1
  0.0 1.4 slice_bitcast_fusion
  1.5 7.8 %collective-permute-start.1 = (f32[2,256,256]{2,1,0:T(8,128)S(1)}, f32[2,256,256]{2,1,0:T(8,128)S(1)}, u32[]{:S(2)}, u32[]{:S(2)}) collective-permute-start(f32[2,256,256]{2,1,0:T(8,128)S(1)} %get-tuple-element.56.refs_5_.refs_0_), channel_id=1, source_target_pairs={{16,0},{32,16},{48,32},{64,48},{80,64},{96,80},{112,96},{128,112},... | collective-permute-start | bytes 1572872 | tf_op jit(solution)/shard_map/ppermute | solution.py:36
  9.3 3.1 %collective-permute-start.4 = (f32[2,256,256]{2,1,0:T(8,128)S(1)}, f32[2,256,256]{2,1,0:T(8,128)S(1)}, u32[]{:S(2)}, u32[]{:S(2)}) collective-permute-start(f32[2,256,256]{2,1,0:T(8,128)S(1)} %get-tuple-element.55.refs_5_.refs_0_), channel_id=1, source_target_pairs={{16,0},{32,16},{48,32},{64,48},{80,64},{96,80},{112,96},{128,112},... | collective-permute-start | bytes 1572872 | tf_op jit(solution)/shard_map/ppermute | solution.py:36
  12.4 3.1 %collective-permute-start.3 = (f32[2,256,256]{2,1,0:T(8,128)S(1)}, f32[2,256,256]{2,1,0:T(8,128)S(1)}, u32[]{:S(2)}, u32[]{:S(2)}) collective-permute-start(f32[2,256,256]{2,1,0:T(8,128)S(1)} %get-tuple-element.55.refs_5_.refs_0_), channel_id=1, source_target_pairs={{1,0},{2,1},{3,2},{4,3},{5,4},{6,5},{7,6},{8,7},{9,8},{10,9},{11,1... | collective-permute-start | bytes 1572872 | tf_op jit(solution)/shard_map/ppermute | solution.py:36
  15.5 2.1 collective-permute-start
  17.6 20.0 %collective-permute-done.1.refs_7_.refs_1_ = f32[2,256,256]{2,1,0:T(8,128)S(1)} collective-permute-done((f32[2,256,256]{2,1,0:T(8,128)S(1)}, f32[2,256,256]{2,1,0:T(8,128)S(1)}, u32[]{:S(2)}, u32[]{:S(2)}) %collective-permute-start.1) | collective-permute-done | bytes 524320 | tf_op jit(solution)/shard_map/ppermute | solution.py:36
  37.6 5.2 %collective-permute-start.2 = (f32[2,256,256]{2,1,0:T(8,128)S(1)}, f32[2,256,256]{2,1,0:T(8,128)S(1)}, u32[]{:S(2)}, u32[]{:S(2)}) collective-permute-start(f32[2,256,256]{2,1,0:T(8,128)S(1)} %collective-permute-done.1.refs_7_.refs_1_), channel_id=1, source_target_pairs={{1,0},{2,1},{3,2},{4,3},{5,4},{6,5},{7,6},{8,7},{9,8},{10,9},{11,1... | collective-permute-start | bytes 1572872 | tf_op jit(solution)/shard_map/ppermute | solution.py:36
  42.8 0.0 copy-done.6
  42.9 1.0 fusion.8
  43.8 8.1 %collective-permute-done.4.refs_7_.refs_1_ = f32[2,256,256]{2,1,0:T(8,128)S(1)} collective-permute-done((f32[2,256,256]{2,1,0:T(8,128)S(1)}, f32[2,256,256]{2,1,0:T(8,128)S(1)}, u32[]{:S(2)}, u32[]{:S(2)}) %collective-permute-start.4) | collective-permute-done | bytes 524320 | tf_op jit(solution)/shard_map/ppermute | solution.py:36
  51.9 5.1 %collective-permute-start.5 = (f32[2,256,256]{2,1,0:T(8,128)S(1)}, f32[2,256,256]{2,1,0:T(8,128)S(1)}, u32[]{:S(2)}, u32[]{:S(2)}) collective-permute-start(f32[2,256,256]{2,1,0:T(8,128)S(1)} %collective-permute-done.4.refs_7_.refs_1_), channel_id=1, source_target_pairs={{1,0},{2,1},{3,2},{4,3},{5,4},{6,5},{7,6},{8,7},{9,8},{10,9},{11,1... | collective-permute-start | bytes 1572872 | tf_op jit(solution)/shard_map/ppermute | solution.py:36
  57.0 0.0 copy-done.5
  57.0 0.0 copy-done
  57.1 0.0 copy-done.2
  57.1 0.0 copy-done.1
  57.1 0.0 copy-start.3
  57.1 0.0 copy-start.4
  57.1 3.6 %shard_map.82 = (f32[2,2,2,256,256]{4,3,2,1,0:T(8,128)S(1)}, f32[2,2,256,128]{3,2,1,0:T(8,128)S(1)}, f32[2,2,2,256,128]{4,3,2,1,0:T(8,128)S(1)}) custom-call(s32[2,2,2]{2,1,0:T(2,128)S(1)} %bitcast.24, f32[2,256,256]{2,1,0:T(8,128)S(1)} %copy-done.1, f32[256,256]{1,0:T(8,128)S(1)} %get-tuple-element.58.cos_ref, f32[256,256]{1,0:T(8,128)S(1)} %get-tuple-element.57.sin_ref, ...), custom_call_target="tpu_custom_call" | custom-call | flops 4000000000 | bytes 8388608 | tf_op jit(solution)/shard_map/pallas_call | solution.py:251
  60.7 5.0 %collective-permute-done.refs_6_ = f32[2,256,256]{2,1,0:T(8,128)S(1)} collective-permute-done((f32[2,256,256]{2,1,0:T(8,128)S(1)}, f32[2,256,256]{2,1,0:T(8,128)S(1)}, u32[]{:S(2)}, u32[]{:S(2)}) %collective-permute-start) | collective-permute-done | bytes 524320 | tf_op jit(solution)/shard_map/ppermute | solution.py:36
  65.7 5.6 %collective-permute-done.2.refs_8_ = f32[2,256,256]{2,1,0:T(8,128)S(1)} collective-permute-done((f32[2,256,256]{2,1,0:T(8,128)S(1)}, f32[2,256,256]{2,1,0:T(8,128)S(1)}, u32[]{:S(2)}, u32[]{:S(2)}) %collective-permute-start.2) | collective-permute-done | bytes 524320 | tf_op jit(solution)/shard_map/ppermute | solution.py:36
  71.3 0.0 copy-done.3
  71.3 0.0 copy-done.4
  71.3 2.1 shard_map.83.refs_2_
  73.4 0.0 collective-permute-done.3.refs_6_
  73.4 3.5 %collective-permute-done.5.refs_8_ = f32[2,256,256]{2,1,0:T(8,128)S(1)} collective-permute-done((f32[2,256,256]{2,1,0:T(8,128)S(1)}, f32[2,256,256]{2,1,0:T(8,128)S(1)}, u32[]{:S(2)}, u32[]{:S(2)}) %collective-permute-start.5) | collective-permute-done | bytes 524320 | tf_op jit(solution)/shard_map/ppermute | solution.py:36
  76.9 2.8 %shard_map.84 = (f32[2,2,256,256]{3,2,1,0:T(8,128)S(1)}, f32[2,2,256,256]{3,2,1,0:T(8,128)S(1)}, f32[2,2,256,256]{3,2,1,0:T(8,128)S(1)}) custom-call(s32[2,2,2]{2,1,0:T(2,128)S(1)} %bitcast.26, s32[2]{0:T(128)S(1)} %bitcast.32, f32[2,2,256,256]{3,2,1,0:T(8,128)S(1)} %shard_map.83.refs_2_, f32[2,2,2,256,128]{4,3,2,1,0:T(8,128)S(1)} %get-tuple-element.28.refs_3_, ...), custom_call_target="tpu_custom_call" | custom-call | flops 4000000000 | bytes 8388608 | tf_op jit(solution)/shard_map/pallas_call | solution.py:251
  79.7 2.3 shard_map.85
  82.1 5.4 %collective-permute-start.6 = (f32[2,2,256,256]{3,2,1,0:T(8,128)S(1)}, f32[2,2,256,256]{3,2,1,0:T(8,128)S(1)}, u32[]{:S(2)}, u32[]{:S(2)}) collective-permute-start(f32[2,2,256,256]{3,2,1,0:T(8,128)S(1)} %get-tuple-element.31), channel_id=1, source_target_pairs={{0,1},{1,2},{2,3},{3,4},{4,5},{5,6},{6,7},{7,8},{8,9},{9,10},{10,1... | collective-permute-start | bytes 3145736 | tf_op jit(solution)/shard_map/ppermute | solution.py:36
  87.5 1.9 collective-permute-start.9
  89.4 9.8 %collective-permute-done.6 = f32[2,2,256,256]{3,2,1,0:T(8,128)S(1)} collective-permute-done((f32[2,2,256,256]{3,2,1,0:T(8,128)S(1)}, f32[2,2,256,256]{3,2,1,0:T(8,128)S(1)}, u32[]{:S(2)}, u32[]{:S(2)}) %collective-permute-start.6) | collective-permute-done | bytes 1048608 | tf_op jit(solution)/shard_map/ppermute | solution.py:36
  99.2 0.2 fusion.6
  99.4 18.1 %collective-permute-start.8 = (f32[2,256,256]{2,1,0:T(8,128)S(1)}, f32[2,256,256]{2,1,0:T(8,128)S(1)}, u32[]{:S(2)}, u32[]{:S(2)}) collective-permute-start(f32[2,256,256]{2,1,0:T(8,128)S(1)} %get-tuple-element.32.above), channel_id=1, source_target_pairs={{16,0},{32,16},{48,32},{64,48},{80,64},{96,80},{112,96},{128,112},... | collective-permute-start | bytes 1572872 | tf_op jit(solution)/shard_map/ppermute | solution.py:36
  117.6 1.9 collective-permute-start.7
  119.5 14.7 %collective-permute-done.9 = f32[2,2,256,256]{3,2,1,0:T(8,128)S(1)} collective-permute-done((f32[2,2,256,256]{3,2,1,0:T(8,128)S(1)}, f32[2,2,256,256]{3,2,1,0:T(8,128)S(1)}, u32[]{:S(2)}, u32[]{:S(2)}) %collective-permute-start.9) | collective-permute-done | bytes 1048608 | tf_op jit(solution)/shard_map/ppermute | solution.py:36
  134.2 0.1 fusion.4
  134.3 7.0 %collective-permute-start.11 = (f32[2,256,256]{2,1,0:T(8,128)S(1)}, f32[2,256,256]{2,1,0:T(8,128)S(1)}, u32[]{:S(2)}, u32[]{:S(2)}) collective-permute-start(f32[2,256,256]{2,1,0:T(8,128)S(1)} %get-tuple-element.36.above), channel_id=1, source_target_pairs={{16,0},{32,16},{48,32},{64,48},{80,64},{96,80},{112,96},{128,112},... | collective-permute-start | bytes 1572872 | tf_op jit(solution)/shard_map/ppermute | solution.py:36
  141.3 1.9 collective-permute-start.10
  143.3 0.0 collective-permute-done.8.from_below
  143.3 7.7 %collective-permute-done.7.from_above = f32[2,256,256]{2,1,0:T(8,128)S(1)} collective-permute-done((f32[2,256,256]{2,1,0:T(8,128)S(1)}, f32[2,256,256]{2,1,0:T(8,128)S(1)}, u32[]{:S(2)}, u32[]{:S(2)}) %collective-permute-start.7) | collective-permute-done | bytes 524320 | tf_op jit(solution)/shard_map/ppermute | solution.py:36
  151.0 0.2 shard_map.86.refs_5_.one
  151.2 1.9 collective-permute-start.12
  153.1 0.0 collective-permute-done.11.from_below
  153.1 14.7 %collective-permute-done.10.from_above = f32[2,256,256]{2,1,0:T(8,128)S(1)} collective-permute-done((f32[2,256,256]{2,1,0:T(8,128)S(1)}, f32[2,256,256]{2,1,0:T(8,128)S(1)}, u32[]{:S(2)}, u32[]{:S(2)}) %collective-permute-start.10) | collective-permute-done | bytes 524320 | tf_op jit(solution)/shard_map/ppermute | solution.py:36
  167.8 0.2 shard_map.87.refs_5_.two
  168.0 1.9 collective-permute-start.13
  170.0 0.0 collective-permute-done.12.refs_6_
  170.0 2.1 shard_map.88.refs_2_
  172.1 12.1 %collective-permute-done.13.refs_6_ = f32[2,2,256,256]{3,2,1,0:T(8,128)S(1)} collective-permute-done((f32[2,2,256,256]{3,2,1,0:T(8,128)S(1)}, f32[2,2,256,256]{3,2,1,0:T(8,128)S(1)}, u32[]{:S(2)}, u32[]{:S(2)}) %collective-permute-start.13) | collective-permute-done | bytes 1048608 | tf_op jit(solution)/shard_map/ppermute | solution.py:36
  184.2 2.7 %shard_map.89 = (f32[2,2,256,256]{3,2,1,0:T(8,128)S(1)}, f32[2,2,256,256]{3,2,1,0:T(8,128)S(1)}, f32[2,2,256,256]{3,2,1,0:T(8,128)S(1)}) custom-call(s32[2,2,2]{2,1,0:T(2,128)S(1)} %bitcast.29, s32[2]{0:T(128)S(1)} %bitcast.35, f32[2,2,256,256]{3,2,1,0:T(8,128)S(1)} %shard_map.88.refs_2_, f32[2,2,2,256,128]{4,3,2,1,0:T(8,128)S(1)} %get-tuple-element.28.refs_3_, ...), custom_call_target="tpu_custom_call" | custom-call | flops 4000000000 | bytes 8388608 | tf_op jit(solution)/shard_map/pallas_call | solution.py:251
  186.9 2.3 shard_map.90
  189.2 1.9 collective-permute-start.14
  191.1 1.9 collective-permute-start.15
  193.1 28.4 %collective-permute-done.14 = f32[2,2,256,256]{3,2,1,0:T(8,128)S(1)} collective-permute-done((f32[2,2,256,256]{3,2,1,0:T(8,128)S(1)}, f32[2,2,256,256]{3,2,1,0:T(8,128)S(1)}, u32[]{:S(2)}, u32[]{:S(2)}) %collective-permute-start.14) | collective-permute-done | bytes 1048608 | tf_op jit(solution)/shard_map/ppermute | solution.py:36
  221.4 0.2 fusion.2
  221.6 1.9 collective-permute-start.16
  223.5 18.6 %collective-permute-done.15 = f32[2,2,256,256]{3,2,1,0:T(8,128)S(1)} collective-permute-done((f32[2,2,256,256]{3,2,1,0:T(8,128)S(1)}, f32[2,2,256,256]{3,2,1,0:T(8,128)S(1)}, u32[]{:S(2)}, u32[]{:S(2)}) %collective-permute-start.15) | collective-permute-done | bytes 1048608 | tf_op jit(solution)/shard_map/ppermute | solution.py:36
  242.2 0.1 fusion
  242.3 2.8 %collective-permute-start.17 = (f32[2,256,256]{2,1,0:T(8,128)S(1)}, f32[2,256,256]{2,1,0:T(8,128)S(1)}, u32[]{:S(2)}, u32[]{:S(2)}) collective-permute-start(f32[2,256,256]{2,1,0:T(8,128)S(1)} %get-tuple-element.46), channel_id=1, source_target_pairs={{0,16},{16,32},{32,48},{48,64},{64,80},{80,96},{96,112},{112,128},... | collective-permute-start | bytes 1572872 | tf_op jit(solution)/shard_map/ppermute | solution.py:36
  245.1 12.5 %collective-permute-done.16.from_above1 = f32[2,256,256]{2,1,0:T(8,128)S(1)} collective-permute-done((f32[2,256,256]{2,1,0:T(8,128)S(1)}, f32[2,256,256]{2,1,0:T(8,128)S(1)}, u32[]{:S(2)}, u32[]{:S(2)}) %collective-permute-start.16) | collective-permute-done | bytes 524320 | tf_op jit(solution)/shard_map/ppermute | solution.py:36
  257.6 11.2 %collective-permute-done.17.from_above2 = f32[2,256,256]{2,1,0:T(8,128)S(1)} collective-permute-done((f32[2,256,256]{2,1,0:T(8,128)S(1)}, f32[2,256,256]{2,1,0:T(8,128)S(1)}, u32[]{:S(2)}, u32[]{:S(2)}) %collective-permute-start.17) | collective-permute-done | bytes 524320 | tf_op jit(solution)/shard_map/ppermute | solution.py:36
  268.9 1.2 shard_map.91
  (2 shorter events, 0.0 us)
Async XLA Ops:
  0.0 57.0 %copy-start.5 = (bf16[2,256,256]{2,1,0:T(8,128)(2,1)S(1)}, bf16[2,256,256]{2,1,0:T(8,128)(2,1)}, u32[]{:S(2)}) copy-start(bf16[2,256,256]{2,1,0:T(8,128)(2,1)} %constant.5.clone.perm_ref) | copy-start | bytes 786436
  0.0 42.8 %copy-start.6 = (f32[256,256]{1,0:T(8,128)S(1)}, f32[256,256]{1,0:T(8,128)}, u32[]{:S(2)}) copy-start(f32[256,256]{1,0:T(8,128)} %param.10) | copy-start | bytes 786436
  0.0 57.0 %copy-start = (f32[2,1,1,2,256,256]{5,4,3,2,1,0:T(8,128)S(1)}, f32[2,1,1,2,256,256]{5,4,3,2,1,0:T(8,128)}, u32[]{:S(2)}) copy-start(f32[2,1,1,2,256,256]{5,4,3,2,1,0:T(8,128)} %param.13) | copy-start | bytes 3145732
  0.0 57.1 %copy-start.2 = (s32[2,1,1,2,2]{4,3,2,1,0:T(2,128)S(1)}, s32[2,1,1,2,2]{4,3,2,1,0:T(2,128)}, u32[]{:S(2)}) copy-start(s32[2,1,1,2,2]{4,3,2,1,0:T(2,128)} %param.11) | copy-start | bytes 100
  0.0 57.1 %copy-start.1 = (f32[2,256,256]{2,1,0:T(8,128)S(1)}, f32[2,256,256]{2,1,0:T(8,128)}, u32[]{:S(2)}) copy-start(f32[2,256,256]{2,1,0:T(8,128)} %probe_ref.1) | copy-start | bytes 1572868
  1.5 36.2 %collective-permute-start.1 = (f32[2,256,256]{2,1,0:T(8,128)S(1)}, f32[2,256,256]{2,1,0:T(8,128)S(1)}, u32[]{:S(2)}, u32[]{:S(2)}) collective-permute-start(f32[2,256,256]{2,1,0:T(8,128)S(1)} %get-tuple-element.56.refs_5_.refs_0_), channel_id=1, source_target_pairs={{16,0},{32,16},{48,32},{64,48},{80,64},{96,80},{112,96},{128,112},... | collective-permute-start | bytes 1572872 | tf_op jit(solution)/shard_map/ppermute | solution.py:36
  9.3 42.6 %collective-permute-start.4 = (f32[2,256,256]{2,1,0:T(8,128)S(1)}, f32[2,256,256]{2,1,0:T(8,128)S(1)}, u32[]{:S(2)}, u32[]{:S(2)}) collective-permute-start(f32[2,256,256]{2,1,0:T(8,128)S(1)} %get-tuple-element.55.refs_5_.refs_0_), channel_id=1, source_target_pairs={{16,0},{32,16},{48,32},{64,48},{80,64},{96,80},{112,96},{128,112},... | collective-permute-start | bytes 1572872 | tf_op jit(solution)/shard_map/ppermute | solution.py:36
  12.4 61.0 %collective-permute-start.3 = (f32[2,256,256]{2,1,0:T(8,128)S(1)}, f32[2,256,256]{2,1,0:T(8,128)S(1)}, u32[]{:S(2)}, u32[]{:S(2)}) collective-permute-start(f32[2,256,256]{2,1,0:T(8,128)S(1)} %get-tuple-element.55.refs_5_.refs_0_), channel_id=1, source_target_pairs={{1,0},{2,1},{3,2},{4,3},{5,4},{6,5},{7,6},{8,7},{9,8},{10,9},{11,1... | collective-permute-start | bytes 1572872 | tf_op jit(solution)/shard_map/ppermute | solution.py:36
  15.5 50.2 %collective-permute-start = (f32[2,256,256]{2,1,0:T(8,128)S(1)}, f32[2,256,256]{2,1,0:T(8,128)S(1)}, u32[]{:S(2)}, u32[]{:S(2)}) collective-permute-start(f32[2,256,256]{2,1,0:T(8,128)S(1)} %get-tuple-element.56.refs_5_.refs_0_), channel_id=1, source_target_pairs={{1,0},{2,1},{3,2},{4,3},{5,4},{6,5},{7,6},{8,7},{9,8},{10,9},{11,1... | collective-permute-start | bytes 1572872 | tf_op jit(solution)/shard_map/ppermute | solution.py:36
  37.6 33.7 %collective-permute-start.2 = (f32[2,256,256]{2,1,0:T(8,128)S(1)}, f32[2,256,256]{2,1,0:T(8,128)S(1)}, u32[]{:S(2)}, u32[]{:S(2)}) collective-permute-start(f32[2,256,256]{2,1,0:T(8,128)S(1)} %collective-permute-done.1.refs_7_.refs_1_), channel_id=1, source_target_pairs={{1,0},{2,1},{3,2},{4,3},{5,4},{6,5},{7,6},{8,7},{9,8},{10,9},{11,1... | collective-permute-start | bytes 1572872 | tf_op jit(solution)/shard_map/ppermute | solution.py:36
  51.9 25.1 %collective-permute-start.5 = (f32[2,256,256]{2,1,0:T(8,128)S(1)}, f32[2,256,256]{2,1,0:T(8,128)S(1)}, u32[]{:S(2)}, u32[]{:S(2)}) collective-permute-start(f32[2,256,256]{2,1,0:T(8,128)S(1)} %collective-permute-done.4.refs_7_.refs_1_), channel_id=1, source_target_pairs={{1,0},{2,1},{3,2},{4,3},{5,4},{6,5},{7,6},{8,7},{9,8},{10,9},{11,1... | collective-permute-start | bytes 1572872 | tf_op jit(solution)/shard_map/ppermute | solution.py:36
  57.1 14.3 %copy-start.3 = (s32[2,1,1]{0,2,1:T(1,128)S(1)}, s32[2,1,1]{0,2,1:T(1,128)}, u32[]{:S(2)}) copy-start(s32[2,1,1]{0,2,1:T(1,128)} %param.12) | copy-start | bytes 28
  57.1 14.2 %copy-start.4 = (bf16[2,2,2,256,256]{4,3,2,1,0:T(8,128)(2,1)S(1)}, bf16[2,2,2,256,256]{4,3,2,1,0:T(8,128)(2,1)}, u32[]{:S(2)}) copy-start(bf16[2,2,2,256,256]{4,3,2,1,0:T(8,128)(2,1)} %constant.4.clone.refs_4_.refs_5_) | copy-start | bytes 3145732
  82.1 17.2 %collective-permute-start.6 = (f32[2,2,256,256]{3,2,1,0:T(8,128)S(1)}, f32[2,2,256,256]{3,2,1,0:T(8,128)S(1)}, u32[]{:S(2)}, u32[]{:S(2)}) collective-permute-start(f32[2,2,256,256]{3,2,1,0:T(8,128)S(1)} %get-tuple-element.31), channel_id=1, source_target_pairs={{0,1},{1,2},{2,3},{3,4},{4,5},{5,6},{6,7},{7,8},{8,9},{9,10},{10,1... | collective-permute-start | bytes 3145736 | tf_op jit(solution)/shard_map/ppermute | solution.py:36
  87.5 46.7 %collective-permute-start.9 = (f32[2,2,256,256]{3,2,1,0:T(8,128)S(1)}, f32[2,2,256,256]{3,2,1,0:T(8,128)S(1)}, u32[]{:S(2)}, u32[]{:S(2)}) collective-permute-start(f32[2,2,256,256]{3,2,1,0:T(8,128)S(1)} %get-tuple-element.35), channel_id=1, source_target_pairs={{0,1},{1,2},{2,3},{3,4},{4,5},{5,6},{6,7},{7,8},{8,9},{9,10},{10,1... | collective-permute-start | bytes 3145736 | tf_op jit(solution)/shard_map/ppermute | solution.py:36
  99.4 43.8 %collective-permute-start.8 = (f32[2,256,256]{2,1,0:T(8,128)S(1)}, f32[2,256,256]{2,1,0:T(8,128)S(1)}, u32[]{:S(2)}, u32[]{:S(2)}) collective-permute-start(f32[2,256,256]{2,1,0:T(8,128)S(1)} %get-tuple-element.32.above), channel_id=1, source_target_pairs={{16,0},{32,16},{48,32},{64,48},{80,64},{96,80},{112,96},{128,112},... | collective-permute-start | bytes 1572872 | tf_op jit(solution)/shard_map/ppermute | solution.py:36
  117.6 33.4 %collective-permute-start.7 = (f32[2,256,256]{2,1,0:T(8,128)S(1)}, f32[2,256,256]{2,1,0:T(8,128)S(1)}, u32[]{:S(2)}, u32[]{:S(2)}) collective-permute-start(f32[2,256,256]{2,1,0:T(8,128)S(1)} %get-tuple-element.33.below), channel_id=1, source_target_pairs={{0,16},{16,32},{32,48},{48,64},{64,80},{80,96},{96,112},{112,128},... | collective-permute-start | bytes 1572872 | tf_op jit(solution)/shard_map/ppermute | solution.py:36
  134.3 18.8 %collective-permute-start.11 = (f32[2,256,256]{2,1,0:T(8,128)S(1)}, f32[2,256,256]{2,1,0:T(8,128)S(1)}, u32[]{:S(2)}, u32[]{:S(2)}) collective-permute-start(f32[2,256,256]{2,1,0:T(8,128)S(1)} %get-tuple-element.36.above), channel_id=1, source_target_pairs={{16,0},{32,16},{48,32},{64,48},{80,64},{96,80},{112,96},{128,112},... | collective-permute-start | bytes 1572872 | tf_op jit(solution)/shard_map/ppermute | solution.py:36
  141.3 26.5 %collective-permute-start.10 = (f32[2,256,256]{2,1,0:T(8,128)S(1)}, f32[2,256,256]{2,1,0:T(8,128)S(1)}, u32[]{:S(2)}, u32[]{:S(2)}) collective-permute-start(f32[2,256,256]{2,1,0:T(8,128)S(1)} %get-tuple-element.37.below), channel_id=1, source_target_pairs={{0,16},{16,32},{32,48},{48,64},{64,80},{80,96},{96,112},{112,128},... | collective-permute-start | bytes 1572872 | tf_op jit(solution)/shard_map/ppermute | solution.py:36
  151.2 18.8 %collective-permute-start.12 = (f32[2,2,256,256]{3,2,1,0:T(8,128)S(1)}, f32[2,2,256,256]{3,2,1,0:T(8,128)S(1)}, u32[]{:S(2)}, u32[]{:S(2)}) collective-permute-start(f32[2,2,256,256]{3,2,1,0:T(8,128)S(1)} %shard_map.86.refs_5_.one), channel_id=1, source_target_pairs={{1,0},{2,1},{3,2},{4,3},{5,4},{6,5},{7,6},{8,7},{9,8},{10,9},{11,1... | collective-permute-start | bytes 3145736 | tf_op jit(solution)/shard_map/ppermute | solution.py:36
  168.0 16.1 %collective-permute-start.13 = (f32[2,2,256,256]{3,2,1,0:T(8,128)S(1)}, f32[2,2,256,256]{3,2,1,0:T(8,128)S(1)}, u32[]{:S(2)}, u32[]{:S(2)}) collective-permute-start(f32[2,2,256,256]{3,2,1,0:T(8,128)S(1)} %shard_map.87.refs_5_.two), channel_id=1, source_target_pairs={{1,0},{2,1},{3,2},{4,3},{5,4},{6,5},{7,6},{8,7},{9,8},{10,9},{11,1... | collective-permute-start | bytes 3145736 | tf_op jit(solution)/shard_map/ppermute | solution.py:36
  189.2 32.2 %collective-permute-start.14 = (f32[2,2,256,256]{3,2,1,0:T(8,128)S(1)}, f32[2,2,256,256]{3,2,1,0:T(8,128)S(1)}, u32[]{:S(2)}, u32[]{:S(2)}) collective-permute-start(f32[2,2,256,256]{3,2,1,0:T(8,128)S(1)} %get-tuple-element.40), channel_id=1, source_target_pairs={{0,1},{1,2},{2,3},{3,4},{4,5},{5,6},{6,7},{7,8},{8,9},{9,10},{10,1... | collective-permute-start | bytes 3145736 | tf_op jit(solution)/shard_map/ppermute | solution.py:36
  191.1 51.0 %collective-permute-start.15 = (f32[2,2,256,256]{3,2,1,0:T(8,128)S(1)}, f32[2,2,256,256]{3,2,1,0:T(8,128)S(1)}, u32[]{:S(2)}, u32[]{:S(2)}) collective-permute-start(f32[2,2,256,256]{3,2,1,0:T(8,128)S(1)} %get-tuple-element.43), channel_id=1, source_target_pairs={{0,1},{1,2},{2,3},{3,4},{4,5},{5,6},{6,7},{7,8},{8,9},{9,10},{10,1... | collective-permute-start | bytes 3145736 | tf_op jit(solution)/shard_map/ppermute | solution.py:36
  221.6 36.0 %collective-permute-start.16 = (f32[2,256,256]{2,1,0:T(8,128)S(1)}, f32[2,256,256]{2,1,0:T(8,128)S(1)}, u32[]{:S(2)}, u32[]{:S(2)}) collective-permute-start(f32[2,256,256]{2,1,0:T(8,128)S(1)} %get-tuple-element.45), channel_id=1, source_target_pairs={{0,16},{16,32},{32,48},{48,64},{64,80},{80,96},{96,112},{112,128},... | collective-permute-start | bytes 1572872 | tf_op jit(solution)/shard_map/ppermute | solution.py:36
  242.3 26.6 %collective-permute-start.17 = (f32[2,256,256]{2,1,0:T(8,128)S(1)}, f32[2,256,256]{2,1,0:T(8,128)S(1)}, u32[]{:S(2)}, u32[]{:S(2)}) collective-permute-start(f32[2,256,256]{2,1,0:T(8,128)S(1)} %get-tuple-element.46), channel_id=1, source_target_pairs={{0,16},{16,32},{32,48},{48,64},{64,80},{80,96},{96,112},{112,128},... | collective-permute-start | bytes 1572872 | tf_op jit(solution)/shard_map/ppermute | solution.py:36

commit v2 on v1

--- a/solution.py
+++ b/solution.py
@@ -34,6 +34,19 @@
     count = lax.axis_size(axis)
     first, last = (max(0, -steps), min(count, count - steps))
     return lax.ppermute(value, axis, [(source, source + steps) for source in range(first, last)])
+
+
+def around(value, steps, sizes):
+    rows, cols = sizes
+    first, second = [], []
+    for row in range(max(0, -steps), min(rows, rows - steps)):
+        for col in range(cols):
+            z = (2 * (row % 4) + col // 2 % 2 - 3 * steps) % 8
+            relay = (row // 4 * 4 + z // 2) * cols + col // 4 * 4 + z % 2 * 2 + col % 2
+            first.append((row * cols + col, relay))
+            second.append((relay, (row + steps) * cols + col))
+    value = lax.ppermute(value, ("ty", "tx"), first)
+    return lax.ppermute(value, ("ty", "tx"), second)
 
 
 def split(value):
@@ -232,9 +245,19 @@
     mine[1] = tiles[1][...] - step_size * (from_below[...] + below[...])
 
 
-def last_kernel(one, two, above1, above2, from_above1, from_above2, out):
+def sums_kernel(stay, came, above, *below):
+    above[...] = stay[0] + came[0]
+    if len(below) == 1:
+        below[0][...] = stay[1] + came[1]
+    else:
+        for plane in range(2):
+            below[plane][...] = stay[1, plane] + came[1, plane]
+
+
+def last_kernel(one, two, above1, above2, near2, far2, from_above1, out):
     out[0] = one[0] - step_size * (above1[...] + from_above1[...])
-    out[1] = two[0] - step_size * (above2[...] + from_above2[...])
+    out[1, 0] = two[0, 0] - step_size * (above2[0] + near2[...])
+    out[1, 1] = two[0, 1] - step_size * (above2[1] + far2[...])
 
 
 SMEM = pl.BlockSpec(memory_space=pltpu.SMEM)
@@ -270,13 +293,14 @@
     counts = probe_counts.reshape(ITERS)
     measured = amplitudes.reshape(ITERS, SLOTS, SIDE, SIDE)
 
+    sizes = lax.axis_size("ty"), lax.axis_size("tx")
     own = [object_tiles[0], object_tiles[1]]
-    low, rgt, dia = [None, None], [None, None], [None, None]
-    for s in (0, 1):
-        low[s] = shifted(own[s], "ty", -1)
-        rgt[s] = shifted(own[s], "tx", -1)
-    for s in (0, 1):
-        dia[s] = shifted(low[s], "tx", -1)
+    low0 = shifted(own[0], "ty", -1)
+    far = around(object_tiles[1, 1], -1, sizes)
+    rgt = [shifted(own[s], "tx", -1) for s in (0, 1)]
+    near = shifted(object_tiles[1, 0], "ty", -1)
+    low = [low0, jnp.stack([near, far])]
+    dia = [shifted(low[s], "tx", -1) for s in (0, 1)]
 
     rolled, prop, ampl = call(
         prepare_kernel, [offsets],
@@ -299,20 +323,26 @@
         stay1, move1 = call(bind(third_kernel), scalars,
                             [carry, rolled, prop, tables], [pair] * 2)
         stay, move = [stay1, stay2], [move1, move2]
-        above, below, came = [None, None], [None, None], [None, None]
+        above, below, came, from_above = [None, None], [None, None], [None, None], []
+        last = iteration == ITERS - 1
         for s in (1, 0):
             came[s] = shifted(move[s], "tx", 1)
-            sums = (stay[s][0] + came[s][0], stay[s][1] + came[s][1])
-            above[s], below[s] = lax.optimization_barrier(sums)
-        from_above = [None, None]
+            cut = last and s == 1
+            outs = [f32(2, SIDE, SIDE)] + ([f32(SIDE, SIDE)] * 2 if cut else [f32(2, SIDE, SIDE)])
+            above[s], *below[s] = call(sums_kernel, [], [stay[s], came[s]], outs, flops=10**6)
         for s in (1, 0):
-            from_above[s] = shifted(below[s], "ty", 1)
-            if iteration == ITERS - 1:
+            if last and s == 1:
+                far = around(below[s][1], 1, sizes)
+                from_above += [shifted(below[s][0], "ty", 1), far]
+                continue
+            fallen = shifted(below[s][0], "ty", 1)
+            if last:
+                from_above.append(fallen)
                 continue
             from_below = shifted(above[s], "ty", -1)
             held = [tiles[s][0], tiles[s][2]]
             (mine,) = call(update_kernel, [],
-                           [above[s], below[s], from_above[s], from_below, *held], [pair], flops=10**6)
+                           [above[s], below[s][0], fallen, from_below, *held], [pair], flops=10**6)
             tiles[s] = [mine, shifted(mine, "tx", -1)]
     (out,) = call(last_kernel, [], [tiles[0][0], tiles[1][0], *above, *from_above], [pair], flops=10**6)
     return out

time: 271 us -> 279 us (1.030)
  the two profiles are of different devices: /device:TPU:23 before, /device:TPU:29 now
where the time goes in v2:
time: 279 us; the launch traced here: 278 us
  starting transfers between devices  156 us (56%)
  waiting for transfers between devices  98.4 us (35%)
  Pallas kernels  20.2 us (7%)
    ppermute x18, starting transfers between devices, shifted(): lax.ppermute(value, axis, [(source, source + steps) for source in range(f...  134 us
    ppermute x2, waiting for transfers between devices, around(): value = lax.ppermute(value, ('ty', 'tx'), first)  38.2 us
    ppermute x18, waiting for transfers between devices, shifted(): lax.ppermute(value, axis, [(source, source + steps) for source in range(f...  33 us
    ppermute x2, waiting for transfers between devices, around(): return lax.ppermute(value, ('ty', 'tx'), second)  27.2 us
    pallas_call x14, Pallas kernels, call(): pl.pallas_call(body, out_shape=outs, in_specs=[SMEM] * len(scalars) + [VM...  20.2 us
    ppermute x2, starting transfers between devices, around(): value = lax.ppermute(value, ('ty', 'tx'), first)  18.1 us
  transfers between devices with their start and end apart: 22, of which 10 were waited for; matrix products, arithmetic and copies ran while one was open for 0% of the time, Pallas kernels for 3%

profile of v2, /device:TPU:29, one launch (start us, length us, event | category | flops | bytes accessed | tf_op | source)
XLA Modules:
  0.0 277.9 jit_solution(11712784112978237145)
XLA Ops:
  0.0 1.4 slice_bitcast_fusion
  1.5 8.1 %collective-permute-start.1 = (f32[2,256,256]{2,1,0:T(8,128)S(1)}, f32[2,256,256]{2,1,0:T(8,128)S(1)}, u32[]{:S(2)}, u32[]{:S(2)}) collective-permute-start(f32[2,256,256]{2,1,0:T(8,128)S(1)} %get-tuple-element.52.refs_5_.refs_0_), channel_id=1, source_target_pairs={{16,0},{32,16},{48,32},{64,48},{80,64},{96,80},{112,96},{128,112},... | collective-permute-start | bytes 1572872 | tf_op jit(solution)/shard_map/ppermute | solution.py:36
  9.6 1.9 collective-permute-start.5
  11.6 5.8 %collective-permute-start.4 = (f32[256,256]{1,0:T(8,128)S(1)}, f32[256,256]{1,0:T(8,128)S(1)}, u32[]{:S(2)}, u32[]{:S(2)}) collective-permute-start(f32[256,256]{1,0:T(8,128)S(1)} %get-tuple-element.49), channel_id=1, source_target_pairs={{16,0},{32,16},{48,32},{64,48},{80,64},{96,80},{112,96},{128,112},... | collective-permute-start | bytes 786440 | tf_op jit(solution)/shard_map/ppermute | solution.py:36
  17.4 14.6 %collective-permute-done.5 = f32[256,256]{1,0:T(8,128)S(1)} collective-permute-done((f32[256,256]{1,0:T(8,128)S(1)}, f32[256,256]{1,0:T(8,128)S(1)}, u32[]{:S(2)}, u32[]{:S(2)}) %collective-permute-start.5) | collective-permute-done | bytes 262176 | tf_op jit(solution)/shard_map/ppermute | solution.py:48
  32.0 1.9 collective-permute-start.6
  33.9 2.8 %collective-permute-start = (f32[2,256,256]{2,1,0:T(8,128)S(1)}, f32[2,256,256]{2,1,0:T(8,128)S(1)}, u32[]{:S(2)}, u32[]{:S(2)}) collective-permute-start(f32[2,256,256]{2,1,0:T(8,128)S(1)} %get-tuple-element.52.refs_5_.refs_0_), channel_id=1, source_target_pairs={{1,0},{2,1},{3,2},{4,3},{5,4},{6,5},{7,6},{8,7},{9,8},{10,9},{11,1... | collective-permute-start | bytes 1572872 | tf_op jit(solution)/shard_map/ppermute | solution.py:36
  36.7 4.2 %collective-permute-start.3 = (f32[2,256,256]{2,1,0:T(8,128)S(1)}, f32[2,256,256]{2,1,0:T(8,128)S(1)}, u32[]{:S(2)}, u32[]{:S(2)}) collective-permute-start(f32[2,256,256]{2,1,0:T(8,128)S(1)} %get-tuple-element.51.refs_5_.refs_0_), channel_id=1, source_target_pairs={{1,0},{2,1},{3,2},{4,3},{5,4},{6,5},{7,6},{8,7},{9,8},{10,9},{11,1... | collective-permute-start | bytes 1572872 | tf_op jit(solution)/shard_map/ppermute | solution.py:36
  40.9 0.0 collective-permute-done.1.refs_7_.refs_1_
  40.9 2.9 %collective-permute-start.2 = (f32[2,256,256]{2,1,0:T(8,128)S(1)}, f32[2,256,256]{2,1,0:T(8,128)S(1)}, u32[]{:S(2)}, u32[]{:S(2)}) collective-permute-start(f32[2,256,256]{2,1,0:T(8,128)S(1)} %collective-permute-done.1.refs_7_.refs_1_), channel_id=1, source_target_pairs={{1,0},{2,1},{3,2},{4,3},{5,4},{6,5},{7,6},{8,7},{9,8},{10,9},{11,1... | collective-permute-start | bytes 1572872 | tf_op jit(solution)/shard_map/ppermute | solution.py:36
  43.8 0.0 copy-done.7
  43.8 1.0 fusion
  44.8 0.0 collective-permute-done.4
  44.8 8.8 %collective-permute-done.6 = f32[256,256]{1,0:T(8,128)S(1)} collective-permute-done((f32[256,256]{1,0:T(8,128)S(1)}, f32[256,256]{1,0:T(8,128)S(1)}, u32[]{:S(2)}, u32[]{:S(2)}) %collective-permute-start.6) | collective-permute-done | bytes 262176 | tf_op jit(solution)/shard_map/ppermute | solution.py:49
  53.6 3.2 %collective-permute-start.7 = (f32[2,256,256]{2,1,0:T(8,128)S(1)}, f32[2,256,256]{2,1,0:T(8,128)S(1)}, u32[]{:S(2)}, u32[]{:S(2)}) collective-permute-start(f32[2,256,256]{2,1,0:T(8,128)S(1)} %pad_maximum_fusion.refs_7_.refs_1_), channel_id=1, source_target_pairs={{1,0},{2,1},{3,2},{4,3},{5,4},{6,5},{7,6},{8,7},{9,8},{10,9},{11,1... | collective-permute-start | bytes 1572872 | tf_op jit(solution)/shard_map/ppermute | solution.py:36
  56.9 0.0 copy-start.3
  56.9 0.0 copy-start.4
  56.9 3.6 %shard_map.82 = (f32[2,2,2,256,256]{4,3,2,1,0:T(8,128)S(1)}, f32[2,2,256,128]{3,2,1,0:T(8,128)S(1)}, f32[2,2,2,256,128]{4,3,2,1,0:T(8,128)S(1)}) custom-call(s32[2,2,2]{2,1,0:T(2,128)S(1)} %bitcast.14, f32[2,256,256]{2,1,0:T(8,128)S(1)} %copy-done.1, f32[256,256]{1,0:T(8,128)S(1)} %get-tuple-element.54.cos_ref, f32[256,256]{1,0:T(8,128)S(1)} %get-tuple-element.53.sin_ref, ...), custom_call_target="tpu_custom_call" | custom-call | flops 4000000000 | bytes 8388608 | tf_op jit(solution)/shard_map/pallas_call | solution.py:274
  60.6 0.0 collective-permute-done.refs_6_
  60.6 0.0 collective-permute-done.2.refs_8_
  60.6 0.0 copy-done.3
  60.6 3.6 %shard_map.83.refs_2_ = f32[2,2,256,256]{3,2,1,0:T(8,128)S(1)} custom-call(s32[2,2,2]{2,1,0:T(2,128)S(1)} %bitcast.15, s32[2]{0:T(128)S(1)} %bitcast.21, f32[2,2,2,256,256]{4,3,2,1,0:T(8,128)S(1)} %get-tuple-element.27.refs_2_.refs_3_, f32[2,2,256,128]{3,2,1,0:T(8,128)S(1)} %get-tuple-element.28.refs_3_.refs_4_, bf16[2,2,2,256,256]{4,3,2,1,0:T(8,128)(2,1)S(1)} %copy-done.4, ...), custom_call_target="tpu_custom_call" | custom-call | flops 4000000000 | bytes 8388608 | tf_op jit(solution)/shard_map/pallas_call | solution.py:274
  64.2 0.0 collective-permute-done.3.refs_6_
  64.2 1.9 collective-permute-done.7.refs_8_
  66.0 4.8 %shard_map.84 = (f32[2,2,256,256]{3,2,1,0:T(8,128)S(1)}, f32[2,2,256,256]{3,2,1,0:T(8,128)S(1)}, f32[2,2,256,256]{3,2,1,0:T(8,128)S(1)}) custom-call(s32[2,2,2]{2,1,0:T(2,128)S(1)} %bitcast.16, s32[2]{0:T(128)S(1)} %bitcast.22, f32[2,2,256,256]{3,2,1,0:T(8,128)S(1)} %shard_map.83.refs_2_, f32[2,2,2,256,128]{4,3,2,1,0:T(8,128)S(1)} %get-tuple-element.29.refs_3_, ...), custom_call_target="tpu_custom_call" | custom-call | flops 4000000000 | bytes 8388608 | tf_op jit(solution)/shard_map/pallas_call | solution.py:274
  70.9 4.0 %shard_map.85 = (f32[2,2,256,256]{3,2,1,0:T(8,128)S(1)}, f32[2,2,256,256]{3,2,1,0:T(8,128)S(1)}) custom-call(s32[2,2,2]{2,1,0:T(2,128)S(1)} %bitcast.17, s32[2]{0:T(128)S(1)} %bitcast.23, f32[2,2,256,256]{3,2,1,0:T(8,128)S(1)} %get-tuple-element.30.refs_2_, f32[2,2,2,256,256]{4,3,2,1,0:T(8,128)S(1)} %get-tuple-element.27.refs_2_.refs_3_, ...), custom_call_target="tpu_custom_call" | custom-call | flops 4000000000 | bytes 8388608 | tf_op jit(solution)/shard_map/pallas_call | solution.py:274
  74.8 1.9 collective-permute-start.8
  76.8 3.0 %collective-permute-start.11 = (f32[2,2,256,256]{3,2,1,0:T(8,128)S(1)}, f32[2,2,256,256]{3,2,1,0:T(8,128)S(1)}, u32[]{:S(2)}, u32[]{:S(2)}) collective-permute-start(f32[2,2,256,256]{3,2,1,0:T(8,128)S(1)} %get-tuple-element.36), channel_id=1, source_target_pairs={{0,1},{1,2},{2,3},{3,4},{4,5},{5,6},{6,7},{7,8},{8,9},{9,10},{10,1... | collective-permute-start | bytes 3145736 | tf_op jit(solution)/shard_map/ppermute | solution.py:36
  79.8 8.7 %collective-permute-done.8.came = f32[2,2,256,256]{3,2,1,0:T(8,128)S(1)} collective-permute-done((f32[2,2,256,256]{3,2,1,0:T(8,128)S(1)}, f32[2,2,256,256]{3,2,1,0:T(8,128)S(1)}, u32[]{:S(2)}, u32[]{:S(2)}) %collective-permute-start.8) | collective-permute-done | bytes 1048608 | tf_op jit(solution)/shard_map/ppermute | solution.py:36
  88.5 0.1 shard_map.86
  88.6 1.9 collective-permute-start.10
  90.5 4.3 %collective-permute-start.9 = (f32[2,256,256]{2,1,0:T(8,128)S(1)}, f32[2,256,256]{2,1,0:T(8,128)S(1)}, u32[]{:S(2)}, u32[]{:S(2)}) collective-permute-start(f32[2,256,256]{2,1,0:T(8,128)S(1)} %get-tuple-element.34.below), channel_id=1, source_target_pairs={{0,16},{16,32},{32,48},{48,64},{64,80},{80,96},{96,112},{112,128},... | collective-permute-start | bytes 1572872 | tf_op jit(solution)/shard_map/ppermute | solution.py:36
  94.8 4.9 %collective-permute-done.11.came = f32[2,2,256,256]{3,2,1,0:T(8,128)S(1)} collective-permute-done((f32[2,2,256,256]{3,2,1,0:T(8,128)S(1)}, f32[2,2,256,256]{3,2,1,0:T(8,128)S(1)}, u32[]{:S(2)}, u32[]{:S(2)}) %collective-permute-start.11) | collective-permute-done | bytes 1048608 | tf_op jit(solution)/shard_map/ppermute | solution.py:36
  99.7 0.1 shard_map.88
  99.9 2.4 collective-permute-start.13
  102.2 5.4 %collective-permute-start.12 = (f32[2,256,256]{2,1,0:T(8,128)S(1)}, f32[2,256,256]{2,1,0:T(8,128)S(1)}, u32[]{:S(2)}, u32[]{:S(2)}) collective-permute-start(f32[2,256,256]{2,1,0:T(8,128)S(1)} %get-tuple-element.38.below), channel_id=1, source_target_pairs={{0,16},{16,32},{32,48},{48,64},{64,80},{80,96},{96,112},{112,128},... | collective-permute-start | bytes 1572872 | tf_op jit(solution)/shard_map/ppermute | solution.py:36
  107.7 0.0 collective-permute-done.10.from_below
  107.7 4.3 %collective-permute-done.9.from_above = f32[2,256,256]{2,1,0:T(8,128)S(1)} collective-permute-done((f32[2,256,256]{2,1,0:T(8,128)S(1)}, f32[2,256,256]{2,1,0:T(8,128)S(1)}, u32[]{:S(2)}, u32[]{:S(2)}) %collective-permute-start.9) | collective-permute-done | bytes 524320 | tf_op jit(solution)/shard_map/ppermute | solution.py:36
  112.0 0.2 shard_map.87.refs_5_.one
  112.2 40.5 %collective-permute-start.14 = (f32[2,2,256,256]{3,2,1,0:T(8,128)S(1)}, f32[2,2,256,256]{3,2,1,0:T(8,128)S(1)}, u32[]{:S(2)}, u32[]{:S(2)}) collective-permute-start(f32[2,2,256,256]{3,2,1,0:T(8,128)S(1)} %shard_map.87.refs_5_.one), channel_id=1, source_target_pairs={{1,0},{2,1},{3,2},{4,3},{5,4},{6,5},{7,6},{8,7},{9,8},{10,9},{11,1... | collective-permute-start | bytes 3145736 | tf_op jit(solution)/shard_map/ppermute | solution.py:36
  152.8 0.0 collective-permute-done.13.from_below
  152.8 0.0 collective-permute-done.12.from_above
  152.8 0.2 shard_map.89.refs_5_.two
  153.0 14.2 %collective-permute-start.15 = (f32[2,2,256,256]{3,2,1,0:T(8,128)S(1)}, f32[2,2,256,256]{3,2,1,0:T(8,128)S(1)}, u32[]{:S(2)}, u32[]{:S(2)}) collective-permute-start(f32[2,2,256,256]{3,2,1,0:T(8,128)S(1)} %shard_map.89.refs_5_.two), channel_id=1, source_target_pairs={{1,0},{2,1},{3,2},{4,3},{5,4},{6,5},{7,6},{8,7},{9,8},{10,9},{11,1... | collective-permute-start | bytes 3145736 | tf_op jit(solution)/shard_map/ppermute | solution.py:36
  167.2 0.0 collective-permute-done.14.refs_6_
  167.2 0.6 shard_map.90.refs_2_
  167.8 7.7 %collective-permute-done.15.refs_6_ = f32[2,2,256,256]{3,2,1,0:T(8,128)S(1)} collective-permute-done((f32[2,2,256,256]{3,2,1,0:T(8,128)S(1)}, f32[2,2,256,256]{3,2,1,0:T(8,128)S(1)}, u32[]{:S(2)}, u32[]{:S(2)}) %collective-permute-start.15) | collective-permute-done | bytes 1048608 | tf_op jit(solution)/shard_map/ppermute | solution.py:36
  175.5 0.7 shard_map.91
  176.2 1.9 collective-permute-start.17
  178.2 0.7 shard_map.92
  178.9 18.4 %collective-permute-start.16 = (f32[2,2,256,256]{3,2,1,0:T(8,128)S(1)}, f32[2,2,256,256]{3,2,1,0:T(8,128)S(1)}, u32[]{:S(2)}, u32[]{:S(2)}) collective-permute-start(f32[2,2,256,256]{3,2,1,0:T(8,128)S(1)} %get-tuple-element.41), channel_id=1, source_target_pairs={{0,1},{1,2},{2,3},{3,4},{4,5},{5,6},{6,7},{7,8},{8,9},{9,10},{10,1... | collective-permute-start | bytes 3145736 | tf_op jit(solution)/shard_map/ppermute | solution.py:36
  197.3 5.6 %collective-permute-done.17.came = f32[2,2,256,256]{3,2,1,0:T(8,128)S(1)} collective-permute-done((f32[2,2,256,256]{3,2,1,0:T(8,128)S(1)}, f32[2,2,256,256]{3,2,1,0:T(8,128)S(1)}, u32[]{:S(2)}, u32[]{:S(2)}) %collective-permute-start.17) | collective-permute-done | bytes 1048608 | tf_op jit(solution)/shard_map/ppermute | solution.py:36
  202.9 0.1 shard_map.94
  203.0 16.2 %collective-permute-start.19 = (f32[256,256]{1,0:T(8,128)S(1)}, f32[256,256]{1,0:T(8,128)S(1)}, u32[]{:S(2)}, u32[]{:S(2)}) collective-permute-start(f32[256,256]{1,0:T(8,128)S(1)} %get-tuple-element.47), channel_id=1, source_target_pairs={{0,34},{1,35},{2,48},{3,49},{4,38},{5,39},{6,52},{7,53},{8,42},{9,... | collective-permute-start | bytes 786440 | tf_op jit(solution)/shard_map/ppermute | solution.py:48
  219.2 0.0 collective-permute-done.16.came
  219.2 0.1 shard_map.93
  219.3 11.5 %collective-permute-start.21 = (f32[2,256,256]{2,1,0:T(8,128)S(1)}, f32[2,256,256]{2,1,0:T(8,128)S(1)}, u32[]{:S(2)}, u32[]{:S(2)}) collective-permute-start(f32[2,256,256]{2,1,0:T(8,128)S(1)} %get-tuple-element.48), channel_id=1, source_target_pairs={{0,16},{16,32},{32,48},{48,64},{64,80},{80,96},{96,112},{112,128},... | collective-permute-start | bytes 1572872 | tf_op jit(solution)/shard_map/ppermute | solution.py:36
  230.9 1.9 collective-permute-start.18
  232.8 23.6 %collective-permute-done.19 = f32[256,256]{1,0:T(8,128)S(1)} collective-permute-done((f32[256,256]{1,0:T(8,128)S(1)}, f32[256,256]{1,0:T(8,128)S(1)}, u32[]{:S(2)}, u32[]{:S(2)}) %collective-permute-start.19) | collective-permute-done | bytes 262176 | tf_op jit(solution)/shard_map/ppermute | solution.py:48
  256.4 1.9 collective-permute-start.20
  258.3 0.0 collective-permute-done.18.near2
  258.3 0.0 collective-permute-done.21.from_above1
  258.3 18.4 %collective-permute-done.20.far2 = f32[256,256]{1,0:T(8,128)S(1)} collective-permute-done((f32[256,256]{1,0:T(8,128)S(1)}, f32[256,256]{1,0:T(8,128)S(1)}, u32[]{:S(2)}, u32[]{:S(2)}) %collective-permute-start.20) | collective-permute-done | bytes 262176 | tf_op jit(solution)/shard_map/ppermute | solution.py:49
  276.7 1.2 shard_map.95
  (14 shorter events, 0.1 us)
Async XLA Ops:
  0.0 56.9 %copy-start.5 = (bf16[2,256,256]{2,1,0:T(8,128)(2,1)S(1)}, bf16[2,256,256]{2,1,0:T(8,128)(2,1)}, u32[]{:S(2)}) copy-start(bf16[2,256,256]{2,1,0:T(8,128)(2,1)} %constant.5.clone.perm_ref) | copy-start | bytes 786436
  0.0 9.6 %copy-start.6 = (f32[2,2,256,256]{3,2,1,0:T(8,128)S(1)}, f32[2,2,256,256]{3,2,1,0:T(8,128)}, u32[]{:S(2)}) copy-start(f32[2,2,256,256]{3,2,1,0:T(8,128)} %param.8) | copy-start | bytes 3145732
  0.0 43.8 %copy-start.7 = (f32[256,256]{1,0:T(8,128)S(1)}, f32[256,256]{1,0:T(8,128)}, u32[]{:S(2)}) copy-start(f32[256,256]{1,0:T(8,128)} %param.10) | copy-start | bytes 786436
  0.0 56.9 %copy-start = (f32[2,1,1,2,256,256]{5,4,3,2,1,0:T(8,128)S(1)}, f32[2,1,1,2,256,256]{5,4,3,2,1,0:T(8,128)}, u32[]{:S(2)}) copy-start(f32[2,1,1,2,256,256]{5,4,3,2,1,0:T(8,128)} %param.13) | copy-start | bytes 3145732
  0.0 56.9 %copy-start.2 = (s32[2,1,1,2,2]{4,3,2,1,0:T(2,128)S(1)}, s32[2,1,1,2,2]{4,3,2,1,0:T(2,128)}, u32[]{:S(2)}) copy-start(s32[2,1,1,2,2]{4,3,2,1,0:T(2,128)} %param.11) | copy-start | bytes 100
  0.0 56.9 %copy-start.1 = (f32[2,256,256]{2,1,0:T(8,128)S(1)}, f32[2,256,256]{2,1,0:T(8,128)}, u32[]{:S(2)}) copy-start(f32[2,256,256]{2,1,0:T(8,128)} %probe_ref.1) | copy-start | bytes 1572868
  1.5 39.5 %collective-permute-start.1 = (f32[2,256,256]{2,1,0:T(8,128)S(1)}, f32[2,256,256]{2,1,0:T(8,128)S(1)}, u32[]{:S(2)}, u32[]{:S(2)}) collective-permute-start(f32[2,256,256]{2,1,0:T(8,128)S(1)} %get-tuple-element.52.refs_5_.refs_0_), channel_id=1, source_target_pairs={{16,0},{32,16},{48,32},{64,48},{80,64},{96,80},{112,96},{128,112},... | collective-permute-start | bytes 1572872 | tf_op jit(solution)/shard_map/ppermute | solution.py:36
  9.6 22.3 %collective-permute-start.5 = (f32[256,256]{1,0:T(8,128)S(1)}, f32[256,256]{1,0:T(8,128)S(1)}, u32[]{:S(2)}, u32[]{:S(2)}) collective-permute-start(f32[256,256]{1,0:T(8,128)S(1)} %get-tuple-element.50), channel_id=1, source_target_pairs={{16,34},{17,35},{18,48},{19,49},{20,38},{21,39},{22,52},{23,53},{2... | collective-permute-start | bytes 786440 | tf_op jit(solution)/shard_map/ppermute | solution.py:48
  11.6 33.2 %collective-permute-start.4 = (f32[256,256]{1,0:T(8,128)S(1)}, f32[256,256]{1,0:T(8,128)S(1)}, u32[]{:S(2)}, u32[]{:S(2)}) collective-permute-start(f32[256,256]{1,0:T(8,128)S(1)} %get-tuple-element.49), channel_id=1, source_target_pairs={{16,0},{32,16},{48,32},{64,48},{80,64},{96,80},{112,96},{128,112},... | collective-permute-start | bytes 786440 | tf_op jit(solution)/shard_map/ppermute | solution.py:36
  32.0 21.6 %collective-permute-start.6 = (f32[256,256]{1,0:T(8,128)S(1)}, f32[256,256]{1,0:T(8,128)S(1)}, u32[]{:S(2)}, u32[]{:S(2)}) collective-permute-start(f32[256,256]{1,0:T(8,128)S(1)} %collective-permute-done.5), channel_id=1, source_target_pairs={{34,0},{35,1},{48,2},{49,3},{38,4},{39,5},{52,6},{53,7},{42,8},{43... | collective-permute-start | bytes 786440 | tf_op jit(solution)/shard_map/ppermute | solution.py:49
  33.9 26.7 %collective-permute-start = (f32[2,256,256]{2,1,0:T(8,128)S(1)}, f32[2,256,256]{2,1,0:T(8,128)S(1)}, u32[]{:S(2)}, u32[]{:S(2)}) collective-permute-start(f32[2,256,256]{2,1,0:T(8,128)S(1)} %get-tuple-element.52.refs_5_.refs_0_), channel_id=1, source_target_pairs={{1,0},{2,1},{3,2},{4,3},{5,4},{6,5},{7,6},{8,7},{9,8},{10,9},{11,1... | collective-permute-start | bytes 1572872 | tf_op jit(solution)/shard_map/ppermute | solution.py:36
  36.7 27.4 %collective-permute-start.3 = (f32[2,256,256]{2,1,0:T(8,128)S(1)}, f32[2,256,256]{2,1,0:T(8,128)S(1)}, u32[]{:S(2)}, u32[]{:S(2)}) collective-permute-start(f32[2,256,256]{2,1,0:T(8,128)S(1)} %get-tuple-element.51.refs_5_.refs_0_), channel_id=1, source_target_pairs={{1,0},{2,1},{3,2},{4,3},{5,4},{6,5},{7,6},{8,7},{9,8},{10,9},{11,1... | collective-permute-start | bytes 1572872 | tf_op jit(solution)/shard_map/ppermute | solution.py:36
  40.9 19.6 %collective-permute-start.2 = (f32[2,256,256]{2,1,0:T(8,128)S(1)}, f32[2,256,256]{2,1,0:T(8,128)S(1)}, u32[]{:S(2)}, u32[]{:S(2)}) collective-permute-start(f32[2,256,256]{2,1,0:T(8,128)S(1)} %collective-permute-done.1.refs_7_.refs_1_), channel_id=1, source_target_pairs={{1,0},{2,1},{3,2},{4,3},{5,4},{6,5},{7,6},{8,7},{9,8},{10,9},{11,1... | collective-permute-start | bytes 1572872 | tf_op jit(solution)/shard_map/ppermute | solution.py:36
  53.6 12.4 %collective-permute-start.7 = (f32[2,256,256]{2,1,0:T(8,128)S(1)}, f32[2,256,256]{2,1,0:T(8,128)S(1)}, u32[]{:S(2)}, u32[]{:S(2)}) collective-permute-start(f32[2,256,256]{2,1,0:T(8,128)S(1)} %pad_maximum_fusion.refs_7_.refs_1_), channel_id=1, source_target_pairs={{1,0},{2,1},{3,2},{4,3},{5,4},{6,5},{7,6},{8,7},{9,8},{10,9},{11,1... | collective-permute-start | bytes 1572872 | tf_op jit(solution)/shard_map/ppermute | solution.py:36
  56.9 3.7 %copy-start.3 = (s32[2,1,1]{0,2,1:T(1,128)S(1)}, s32[2,1,1]{0,2,1:T(1,128)}, u32[]{:S(2)}) copy-start(s32[2,1,1]{0,2,1:T(1,128)} %param.12) | copy-start | bytes 28
  56.9 3.7 %copy-start.4 = (bf16[2,2,2,256,256]{4,3,2,1,0:T(8,128)(2,1)S(1)}, bf16[2,2,2,256,256]{4,3,2,1,0:T(8,128)(2,1)}, u32[]{:S(2)}) copy-start(bf16[2,2,2,256,256]{4,3,2,1,0:T(8,128)(2,1)} %constant.4.clone.refs_4_.refs_5_) | copy-start | bytes 3145732
  74.8 13.7 %collective-permute-start.8 = (f32[2,2,256,256]{3,2,1,0:T(8,128)S(1)}, f32[2,2,256,256]{3,2,1,0:T(8,128)S(1)}, u32[]{:S(2)}, u32[]{:S(2)}) collective-permute-start(f32[2,2,256,256]{3,2,1,0:T(8,128)S(1)} %get-tuple-element.32), channel_id=1, source_target_pairs={{0,1},{1,2},{2,3},{3,4},{4,5},{5,6},{6,7},{7,8},{8,9},{9,10},{10,1... | collective-permute-start | bytes 3145736 | tf_op jit(solution)/shard_map/ppermute | solution.py:36
  76.8 23.0 %collective-permute-start.11 = (f32[2,2,256,256]{3,2,1,0:T(8,128)S(1)}, f32[2,2,256,256]{3,2,1,0:T(8,128)S(1)}, u32[]{:S(2)}, u32[]{:S(2)}) collective-permute-start(f32[2,2,256,256]{3,2,1,0:T(8,128)S(1)} %get-tuple-element.36), channel_id=1, source_target_pairs={{0,1},{1,2},{2,3},{3,4},{4,5},{5,6},{6,7},{7,8},{8,9},{9,10},{10,1... | collective-permute-start | bytes 3145736 | tf_op jit(solution)/shard_map/ppermute | solution.py:36
  88.6 19.1 %collective-permute-start.10 = (f32[2,256,256]{2,1,0:T(8,128)S(1)}, f32[2,256,256]{2,1,0:T(8,128)S(1)}, u32[]{:S(2)}, u32[]{:S(2)}) collective-permute-start(f32[2,256,256]{2,1,0:T(8,128)S(1)} %get-tuple-element.33.above), channel_id=1, source_target_pairs={{16,0},{32,16},{48,32},{64,48},{80,64},{96,80},{112,96},{128,112},... | collective-permute-start | bytes 1572872 | tf_op jit(solution)/shard_map/ppermute | solution.py:36
  90.5 21.5 %collective-permute-start.9 = (f32[2,256,256]{2,1,0:T(8,128)S(1)}, f32[2,256,256]{2,1,0:T(8,128)S(1)}, u32[]{:S(2)}, u32[]{:S(2)}) collective-permute-start(f32[2,256,256]{2,1,0:T(8,128)S(1)} %get-tuple-element.34.below), channel_id=1, source_target_pairs={{0,16},{16,32},{32,48},{48,64},{64,80},{80,96},{96,112},{112,128},... | collective-permute-start | bytes 1572872 | tf_op jit(solution)/shard_map/ppermute | solution.py:36
  99.9 52.9 %collective-permute-start.13 = (f32[2,256,256]{2,1,0:T(8,128)S(1)}, f32[2,256,256]{2,1,0:T(8,128)S(1)}, u32[]{:S(2)}, u32[]{:S(2)}) collective-permute-start(f32[2,256,256]{2,1,0:T(8,128)S(1)} %get-tuple-element.37.above), channel_id=1, source_target_pairs={{16,0},{32,16},{48,32},{64,48},{80,64},{96,80},{112,96},{128,112},... | collective-permute-start | bytes 1572872 | tf_op jit(solution)/shard_map/ppermute | solution.py:36
  102.2 50.5 %collective-permute-start.12 = (f32[2,256,256]{2,1,0:T(8,128)S(1)}, f32[2,256,256]{2,1,0:T(8,128)S(1)}, u32[]{:S(2)}, u32[]{:S(2)}) collective-permute-start(f32[2,256,256]{2,1,0:T(8,128)S(1)} %get-tuple-element.38.below), channel_id=1, source_target_pairs={{0,16},{16,32},{32,48},{48,64},{64,80},{80,96},{96,112},{112,128},... | collective-permute-start | bytes 1572872 | tf_op jit(solution)/shard_map/ppermute | solution.py:36
  112.2 55.0 %collective-permute-start.14 = (f32[2,2,256,256]{3,2,1,0:T(8,128)S(1)}, f32[2,2,256,256]{3,2,1,0:T(8,128)S(1)}, u32[]{:S(2)}, u32[]{:S(2)}) collective-permute-start(f32[2,2,256,256]{3,2,1,0:T(8,128)S(1)} %shard_map.87.refs_5_.one), channel_id=1, source_target_pairs={{1,0},{2,1},{3,2},{4,3},{5,4},{6,5},{7,6},{8,7},{9,8},{10,9},{11,1... | collective-permute-start | bytes 3145736 | tf_op jit(solution)/shard_map/ppermute | solution.py:36
  153.0 22.5 %collective-permute-start.15 = (f32[2,2,256,256]{3,2,1,0:T(8,128)S(1)}, f32[2,2,256,256]{3,2,1,0:T(8,128)S(1)}, u32[]{:S(2)}, u32[]{:S(2)}) collective-permute-start(f32[2,2,256,256]{3,2,1,0:T(8,128)S(1)} %shard_map.89.refs_5_.two), channel_id=1, source_target_pairs={{1,0},{2,1},{3,2},{4,3},{5,4},{6,5},{7,6},{8,7},{9,8},{10,9},{11,1... | collective-permute-start | bytes 3145736 | tf_op jit(solution)/shard_map/ppermute | solution.py:36
  176.2 26.6 %collective-permute-start.17 = (f32[2,2,256,256]{3,2,1,0:T(8,128)S(1)}, f32[2,2,256,256]{3,2,1,0:T(8,128)S(1)}, u32[]{:S(2)}, u32[]{:S(2)}) collective-permute-start(f32[2,2,256,256]{3,2,1,0:T(8,128)S(1)} %get-tuple-element.44), channel_id=1, source_target_pairs={{0,1},{1,2},{2,3},{3,4},{4,5},{5,6},{6,7},{7,8},{8,9},{9,10},{10,1... | collective-permute-start | bytes 3145736 | tf_op jit(solution)/shard_map/ppermute | solution.py:36
  178.9 40.3 %collective-permute-start.16 = (f32[2,2,256,256]{3,2,1,0:T(8,128)S(1)}, f32[2,2,256,256]{3,2,1,0:T(8,128)S(1)}, u32[]{:S(2)}, u32[]{:S(2)}) collective-permute-start(f32[2,2,256,256]{3,2,1,0:T(8,128)S(1)} %get-tuple-element.41), channel_id=1, source_target_pairs={{0,1},{1,2},{2,3},{3,4},{4,5},{5,6},{6,7},{7,8},{8,9},{9,10},{10,1... | collective-permute-start | bytes 3145736 | tf_op jit(solution)/shard_map/ppermute | solution.py:36
  203.0 53.4 %collective-permute-start.19 = (f32[256,256]{1,0:T(8,128)S(1)}, f32[256,256]{1,0:T(8,128)S(1)}, u32[]{:S(2)}, u32[]{:S(2)}) collective-permute-start(f32[256,256]{1,0:T(8,128)S(1)} %get-tuple-element.47), channel_id=1, source_target_pairs={{0,34},{1,35},{2,48},{3,49},{4,38},{5,39},{6,52},{7,53},{8,42},{9,... | collective-permute-start | bytes 786440 | tf_op jit(solution)/shard_map/ppermute | solution.py:48
  219.3 39.0 %collective-permute-start.21 = (f32[2,256,256]{2,1,0:T(8,128)S(1)}, f32[2,256,256]{2,1,0:T(8,128)S(1)}, u32[]{:S(2)}, u32[]{:S(2)}) collective-permute-start(f32[2,256,256]{2,1,0:T(8,128)S(1)} %get-tuple-element.48), channel_id=1, source_target_pairs={{0,16},{16,32},{32,48},{48,64},{64,80},{80,96},{96,112},{112,128},... | collective-permute-start | bytes 1572872 | tf_op jit(solution)/shard_map/ppermute | solution.py:36
  230.9 27.5 %collective-permute-start.18 = (f32[256,256]{1,0:T(8,128)S(1)}, f32[256,256]{1,0:T(8,128)S(1)}, u32[]{:S(2)}, u32[]{:S(2)}) collective-permute-start(f32[256,256]{1,0:T(8,128)S(1)} %get-tuple-element.46), channel_id=1, source_target_pairs={{0,16},{16,32},{32,48},{48,64},{64,80},{80,96},{96,112},{112,128},... | collective-permute-start | bytes 786440 | tf_op jit(solution)/shard_map/ppermute | solution.py:36
  256.4 20.4 %collective-permute-start.20 = (f32[256,256]{1,0:T(8,128)S(1)}, f32[256,256]{1,0:T(8,128)S(1)}, u32[]{:S(2)}, u32[]{:S(2)}) collective-permute-start(f32[256,256]{1,0:T(8,128)S(1)} %collective-permute-done.19), channel_id=1, source_target_pairs={{34,16},{35,17},{48,18},{49,19},{38,20},{39,21},{52,22},{53,23},{4... | collective-permute-start | bytes 786440 | tf_op jit(solution)/shard_map/ppermute | solution.py:49

commit v3 on v2

--- a/solution.py
+++ b/solution.py
@@ -36,17 +36,39 @@
     return lax.ppermute(value, axis, [(source, source + steps) for source in range(first, last)])
 
 
+def moved(value, target, sizes):
+    rows, cols = sizes
+    pairs = []
+    for row in range(rows):
+        for col in range(cols):
+            new_row, new_col = target(row, col)
+            if 0 <= new_row < rows and 0 <= new_col < cols:
+                pairs.append((row * cols + col, new_row * cols + new_col))
+    return lax.ppermute(value, ("ty", "tx"), pairs)
+
+
+NOWHERE = (-1, -1)
+
+
+def diagonal_back(row, col):
+    return (row - 1, col - 1) if col % 4 == 0 else (row, col - 1)
+
+
+def diagonal_on(row, col):
+    return (row + 1, col + 1) if col % 4 == 3 else (row, col + 1)
+
+
 def around(value, steps, sizes):
     rows, cols = sizes
-    first, second = [], []
-    for row in range(max(0, -steps), min(rows, rows - steps)):
-        for col in range(cols):
-            z = (2 * (row % 4) + col // 2 % 2 - 3 * steps) % 8
-            relay = (row // 4 * 4 + z // 2) * cols + col // 4 * 4 + z % 2 * 2 + col % 2
-            first.append((row * cols + col, relay))
-            second.append((relay, (row + steps) * cols + col))
-    value = lax.ppermute(value, ("ty", "tx"), first)
-    return lax.ppermute(value, ("ty", "tx"), second)
+
+    def relay(row, col):
+        z = (2 * (row % 4) + col // 2 % 2 - 3 * steps) % 8
+        return row // 4 * 4 + z // 2, col // 4 * 4 + z % 2 * 2 + col % 2
+
+    spots = [(r, c) for r in range(rows) for c in range(cols) if 0 <= r + steps < rows]
+    ends = {relay(*spot): (spot[0] + steps, spot[1]) for spot in spots}
+    value = moved(value, lambda r, c: relay(r, c) if (r, c) in spots else NOWHERE, sizes)
+    return moved(value, lambda r, c: ends.get((r, c), NOWHERE), sizes)
 
 
 def split(value):
@@ -104,13 +126,6 @@
     )
 
 
-def four(tiles):
-    if len(tiles) == 4:
-        return tiles
-    mine, theirs = tiles
-    return mine.at[0], theirs.at[0], mine.at[1], theirs.at[1]
-
-
 def masks(off_ref, iteration, slot):
     row = off_ref[iteration, slot, 0]
     col = off_ref[iteration, slot, 1]
@@ -125,14 +140,14 @@
     return jnp.where(below, lower, upper)
 
 
-def placed(below, right, value, plane, stay, move):
+def placed(below, right, value, plane, stay, side, diag):
     zero = jnp.zeros_like(value)
     left_part = jnp.where(right, zero, value)
     right_part = jnp.where(right, value, zero)
     stay[0, plane] += jnp.where(below, zero, left_part)
     stay[1, plane] += jnp.where(below, left_part, zero)
-    move[0, plane] += jnp.where(below, zero, right_part)
-    move[1, plane] += jnp.where(below, right_part, zero)
+    side[plane] += jnp.where(below, zero, right_part)
+    diag[plane] += jnp.where(below, right_part, zero)
 
 
 def prepare_kernel(off_ref, probe_ref, cos_ref, sin_ref, amp_ref, perm_ref,
@@ -172,7 +187,7 @@
 
 def first_kernel(iteration, off_ref, cnt_ref, rolled, prop, tables, *refs):
     *tiles, mid_ref = refs
-    own, rgt, low, dia = four(tiles)
+    own, rgt, low, dia = tiles
 
     def body(slot, carry):
         below, right = masks(off_ref, iteration, slot)
@@ -192,10 +207,11 @@
 
 
 def second_kernel(iteration, off_ref, cnt_ref, mid_ref, ampl, tables, *refs):
-    *tiles, stay, move, carry_ref = refs
-    own, rgt, low, dia = four(tiles)
+    own, rgt, low, dia, stay, *moves, carry_ref = refs
+    side, diag = moves if len(moves) == 2 else (moves[0].at[0], moves[0].at[1])
     stay[...] = jnp.zeros_like(stay)
-    move[...] = jnp.zeros_like(move)
+    side[...] = jnp.zeros_like(side)
+    diag[...] = jnp.zeros_like(diag)
 
     def body(slot, carry):
         below, right = masks(off_ref, iteration, slot)
@@ -209,8 +225,8 @@
             factor = 1.0 - ampl[iteration, slot, q] * lax.rsqrt(re * re + im * im + soft_floor)
             chi.append(lanes_cat(re * factor, im * factor))
         b_re, b_im = inverse(tables, *chi)
-        placed(below, right, m_re * b_re + m_im * b_im, 0, stay, move)
-        placed(below, right, m_re * b_im - m_im * b_re, 1, stay, move)
+        placed(below, right, m_re * b_re + m_im * b_im, 0, stay, side, diag)
+        placed(below, right, m_re * b_im - m_im * b_re, 1, stay, side, diag)
         carry_ref[slot, 0] = two_re * b_re + two_im * b_im
         carry_ref[slot, 1] = two_re * b_im - two_im * b_re
         return carry
@@ -218,9 +234,11 @@
     lax.fori_loop(0, cnt_ref[iteration], body, 0)
 
 
-def third_kernel(iteration, off_ref, cnt_ref, carry_ref, rolled, prop, tables, stay, move):
+def third_kernel(iteration, off_ref, cnt_ref, carry_ref, rolled, prop, tables, stay, *moves):
+    side, diag = moves if len(moves) == 2 else (moves[0].at[0], moves[0].at[1])
     stay[...] = jnp.zeros_like(stay)
-    move[...] = jnp.zeros_like(move)
+    side[...] = jnp.zeros_like(side)
+    diag[...] = jnp.zeros_like(diag)
 
     def body(slot, carry):
         below, right = masks(off_ref, iteration, slot)
@@ -232,20 +250,22 @@
             turned.append(lanes_cat(re * h_re + im * h_im, im * h_re - re * h_im))
         e_re, e_im = inverse(tables, *turned)
         p_re, p_im = rolled[iteration, slot, 0], rolled[iteration, slot, 1]
-        placed(below, right, p_re * e_re + p_im * e_im, 0, stay, move)
-        placed(below, right, p_re * e_im - p_im * e_re, 1, stay, move)
+        placed(below, right, p_re * e_re + p_im * e_im, 0, stay, side, diag)
+        placed(below, right, p_re * e_im - p_im * e_re, 1, stay, side, diag)
         return carry
 
     lax.fori_loop(0, cnt_ref[iteration], body, 0)
 
 
-def update_kernel(above, below, from_above, from_below, *refs):
-    *tiles, mine = refs
-    mine[0] = tiles[0][...] - step_size * (above[...] + from_above[...])
-    mine[1] = tiles[1][...] - step_size * (from_below[...] + below[...])
-
-
-def sums_kernel(stay, came, above, *below):
+def sums_kernel(first, stay, side, diag, above, below):
+    for plane in range(2):
+        zero = jnp.zeros((SIDE, SIDE), jnp.float32)
+        extra = diag[plane]
+        above[plane] = stay[0, plane] + side[plane] + jnp.where(first[0] > 0, extra, zero)
+        below[plane] = stay[1, plane] + jnp.where(first[0] > 0, zero, extra)
+
+
+def fall_kernel(stay, came, above, *below):
     above[...] = stay[0] + came[0]
     if len(below) == 1:
         below[0][...] = stay[1] + came[1]
@@ -254,15 +274,24 @@
             below[plane][...] = stay[1, plane] + came[1, plane]
 
 
-def last_kernel(one, two, above1, above2, near2, far2, from_above1, out):
-    out[0] = one[0] - step_size * (above1[...] + from_above1[...])
-    out[1, 0] = two[0, 0] - step_size * (above2[0] + near2[...])
-    out[1, 1] = two[0, 1] - step_size * (above2[1] + far2[...])
+def update_kernel(first, above, below, from_above, from_below, old, old_low, own, low, send):
+    for plane in range(2):
+        one = old[plane] - step_size * (above[plane] + from_above[plane])
+        two = old_low[plane] - step_size * (from_below[plane] + below[plane])
+        own[plane] = one
+        low[plane] = two
+        send[plane] = jnp.where(first[0] > 0, one, two)
+
+
+def last_kernel(one, two, above1, above2, near2, far2, fallen1, out):
+    out[0] = one[...] - step_size * (above1[...] + fallen1[...])
+    out[1, 0] = two[0] - step_size * (above2[0] + near2[...])
+    out[1, 1] = two[1] - step_size * (above2[1] + far2[...])
 
 
 SMEM = pl.BlockSpec(memory_space=pltpu.SMEM)
 VMEM = pl.BlockSpec(memory_space=pltpu.VMEM)
-LIMIT = 24 * 1024 * 1024
+LIMIT = 12 * 1024 * 1024
 
 
 def f32(*shape):
@@ -294,6 +323,9 @@
     measured = amplitudes.reshape(ITERS, SLOTS, SIDE, SIDE)
 
     sizes = lax.axis_size("ty"), lax.axis_size("tx")
+    sizes = lax.axis_size("ty"), lax.axis_size("tx")
+    column = lax.axis_index("tx") % 4
+    first = (column == 0).astype(jnp.int32).reshape(1)
     own = [object_tiles[0], object_tiles[1]]
     low0 = shifted(own[0], "ty", -1)
     far = around(object_tiles[1, 1], -1, sizes)
@@ -308,7 +340,7 @@
         [f32(ITERS, SLOTS, 2, SIDE, SIDE), f32(2, 2, SIDE, HALF), f32(ITERS, SLOTS, 2, SIDE, HALF)],
         [pltpu.VMEM((2, 2 * SIDE, SIDE), jnp.float32)],
     )
-    pair = f32(2, 2, SIDE, SIDE)
+    pair, tile = f32(2, 2, SIDE, SIDE), f32(2, SIDE, SIDE)
 
     tiles = [[own[s], rgt[s], low[s], dia[s]] for s in (0, 1)]
 
@@ -318,34 +350,42 @@
 
         scalars = [offsets, counts]
         (mid,) = call(bind(first_kernel), scalars, [rolled, prop, tables, *tiles[0]], [pair])
-        stay2, move2, carry = call(bind(second_kernel), scalars,
-                                   [mid, ampl, tables, *tiles[1]], [pair] * 3)
-        stay1, move1 = call(bind(third_kernel), scalars,
-                            [carry, rolled, prop, tables], [pair] * 2)
-        stay, move = [stay1, stay2], [move1, move2]
-        above, below, came, from_above = [None, None], [None, None], [None, None], []
         last = iteration == ITERS - 1
+        moves = [pair] if last else [tile, tile]
+        stay2, *moves2, carry = call(bind(second_kernel), scalars,
+                                     [mid, ampl, tables, *tiles[1]], [pair, *moves, pair])
+        stay1, *moves1 = call(bind(third_kernel), scalars,
+                              [carry, rolled, prop, tables], [pair, *moves])
+        stay = [stay1, stay2]
+        if last:
+            came = [None, None]
+            for s in (1, 0):
+                came[s] = shifted([moves1, moves2][s][0], "tx", 1)
+            above2, near, far = call(fall_kernel, [], [stay[1], came[1]],
+                                     [tile, f32(SIDE, SIDE), f32(SIDE, SIDE)], flops=10**6)
+            above1, fallen = call(fall_kernel, [], [stay[0], came[0]], [tile, tile], flops=10**6)
+            far = around(far, 1, sizes)
+            near = shifted(near, "ty", 1)
+            fallen = shifted(fallen, "ty", 1)
+            (out,) = call(last_kernel, [], [tiles[0][0], tiles[1][0], above1, above2, near, far, fallen],
+                          [pair], flops=10**6)
+            return out
+        side, diag = [moves1[0], moves2[0]], [moves1[1], moves2[1]]
         for s in (1, 0):
-            came[s] = shifted(move[s], "tx", 1)
-            cut = last and s == 1
-            outs = [f32(2, SIDE, SIDE)] + ([f32(SIDE, SIDE)] * 2 if cut else [f32(2, SIDE, SIDE)])
-            above[s], *below[s] = call(sums_kernel, [], [stay[s], came[s]], outs, flops=10**6)
+            diag[s] = moved(diag[s], diagonal_on, sizes)
+        above, below = [None, None], [None, None]
         for s in (1, 0):
-            if last and s == 1:
-                far = around(below[s][1], 1, sizes)
-                from_above += [shifted(below[s][0], "ty", 1), far]
-                continue
-            fallen = shifted(below[s][0], "ty", 1)
-            if last:
-                from_above.append(fallen)
-                continue
-            from_below = shifted(above[s], "ty", -1)
-            held = [tiles[s][0], tiles[s][2]]
-            (mine,) = call(update_kernel, [],
-                           [above[s], below[s][0], fallen, from_below, *held], [pair], flops=10**6)
-            tiles[s] = [mine, shifted(mine, "tx", -1)]
-    (out,) = call(last_kernel, [], [tiles[0][0], tiles[1][0], *above, *from_above], [pair], flops=10**6)
-    return out
+            side[s] = shifted(side[s], "tx", 1)
+            above[s], below[s] = call(sums_kernel, [first], [stay[s], side[s], diag[s]],
+                                      [tile, tile], flops=10**6)
+        for s in (1, 0):
+            fallen = shifted(below[s], "ty", 1)
+            risen = shifted(above[s], "ty", -1)
+            own, low, send = call(update_kernel, [first],
+                                  [above[s], below[s], fallen, risen, tiles[s][0], tiles[s][2]],
+                                  [tile] * 3, flops=10**6)
+            tiles[s] = [own, shifted(own, "tx", -1), low,
+                        moved(send, diagonal_back, sizes)]
 
 
 def solution(mesh):

time: 279 us -> 254 us (0.910)
  the two profiles are of different devices: /device:TPU:29 before, /device:TPU:82 now
where the time goes in v3:
time: 254 us; the launch traced here: 253 us
  waiting for transfers between devices  127 us (50%)
  starting transfers between devices  86.2 us (34%)
  Pallas kernels  34.5 us (14%)
  local copies, waits for them, and re-layouts  4.7 us (2%)
    ppermute x18, waiting for transfers between devices, shifted(): lax.ppermute(value, axis, [(source, source + steps) for source in range(f...  90.7 us
    ppermute x18, starting transfers between devices, shifted(): lax.ppermute(value, axis, [(source, source + steps) for source in range(f...  53.5 us
    ppermute x8, waiting for transfers between devices, moved(): return lax.ppermute(value, ('ty', 'tx'), pairs)  36.3 us
    pallas_call x14, Pallas kernels, call(): pl.pallas_call(body, out_shape=outs, in_specs=[SMEM] * len(scalars) + [VM...  34.5 us
    ppermute x8, starting transfers between devices, moved(): return lax.ppermute(value, ('ty', 'tx'), pairs)  32.7 us
  transfers between devices with their start and end apart: 26, of which 18 were waited for; matrix products, arithmetic and copies ran while one was open for 0% of the time, Pallas kernels for 7%

profile of v3, /device:TPU:82, one launch (start us, length us, event | category | flops | bytes accessed | tf_op | source)
XLA Modules:
  0.0 253.0 jit_solution(345300217403594688)
XLA Ops:
  0.0 1.4 slice_bitcast_fusion
  1.5 1.9 collective-permute-start.1
  3.5 7.4 %collective-permute-start.5 = (f32[256,256]{1,0:T(8,128)S(1)}, f32[256,256]{1,0:T(8,128)S(1)}, u32[]{:S(2)}, u32[]{:S(2)}) collective-permute-start(f32[256,256]{1,0:T(8,128)S(1)} %get-tuple-element.66), channel_id=1, source_target_pairs={{16,34},{17,35},{18,48},{19,49},{20,38},{21,39},{22,52},{23,53},{2... | collective-permute-start | bytes 786440 | tf_op jit(solution)/shard_map/ppermute | solution.py:47
  10.8 2.3 collective-permute-start.4
  13.1 14.5 %collective-permute-done.5 = f32[256,256]{1,0:T(8,128)S(1)} collective-permute-done((f32[256,256]{1,0:T(8,128)S(1)}, f32[256,256]{1,0:T(8,128)S(1)}, u32[]{:S(2)}, u32[]{:S(2)}) %collective-permute-start.5) | collective-permute-done | bytes 262176 | tf_op jit(solution)/shard_map/ppermute | solution.py:47
  27.7 6.3 %collective-permute-start.6 = (f32[256,256]{1,0:T(8,128)S(1)}, f32[256,256]{1,0:T(8,128)S(1)}, u32[]{:S(2)}, u32[]{:S(2)}) collective-permute-start(f32[256,256]{1,0:T(8,128)S(1)} %collective-permute-done.5), channel_id=1, source_target_pairs={{0,18},{1,19},{2,32},{3,33},{4,22},{5,23},{6,36},{7,37},{8,26},{9,... | collective-permute-start | bytes 786440 | tf_op jit(solution)/shard_map/ppermute | solution.py:47
  34.0 1.9 collective-permute-start
  35.9 4.3 %collective-permute-start.3 = (f32[2,256,256]{2,1,0:T(8,128)S(1)}, f32[2,256,256]{2,1,0:T(8,128)S(1)}, u32[]{:S(2)}, u32[]{:S(2)}) collective-permute-start(f32[2,256,256]{2,1,0:T(8,128)S(1)} %get-tuple-element.67.refs_5_.old), channel_id=1, source_target_pairs={{1,0},{2,1},{3,2},{4,3},{5,4},{6,5},{7,6},{8,7},{9,8},{10,9},{11,1... | collective-permute-start | bytes 1572872 | tf_op jit(solution)/shard_map/ppermute | solution.py:36
  40.3 1.9 collective-permute-start.2
  42.2 1.0 fusion
  43.2 6.5 %collective-permute-done.6 = f32[256,256]{1,0:T(8,128)S(1)} collective-permute-done((f32[256,256]{1,0:T(8,128)S(1)}, f32[256,256]{1,0:T(8,128)S(1)}, u32[]{:S(2)}, u32[]{:S(2)}) %collective-permute-start.6) | collective-permute-done | bytes 262176 | tf_op jit(solution)/shard_map/ppermute | solution.py:47
  49.8 1.9 collective-permute-start.7
  51.8 0.0 copy-start.8
  51.8 3.6 %shard_map.82 = (f32[2,2,2,256,256]{4,3,2,1,0:T(8,128)S(1)}, f32[2,2,256,128]{3,2,1,0:T(8,128)S(1)}, f32[2,2,2,256,128]{4,3,2,1,0:T(8,128)S(1)}) custom-call(s32[2,2,2]{2,1,0:T(2,128)S(1)} %bitcast.15, f32[2,256,256]{2,1,0:T(8,128)S(1)} %copy-done.5, f32[256,256]{1,0:T(8,128)S(1)} %get-tuple-element.70.cos_ref, f32[256,256]{1,0:T(8,128)S(1)} %get-tuple-element.69.sin_ref, ...), custom_call_target="tpu_custom_call" | custom-call | flops 4000000000 | bytes 8388608 | tf_op jit(solution)/shard_map/pallas_call | solution.py:303
  55.4 11.1 %collective-permute-done.2.refs_8_ = f32[2,256,256]{2,1,0:T(8,128)S(1)} collective-permute-done((f32[2,256,256]{2,1,0:T(8,128)S(1)}, f32[2,256,256]{2,1,0:T(8,128)S(1)}, u32[]{:S(2)}, u32[]{:S(2)}) %collective-permute-start.2) | collective-permute-done | bytes 524320 | tf_op jit(solution)/shard_map/ppermute | solution.py:36
  66.6 3.7 %shard_map.83.refs_2_ = f32[2,2,256,256]{3,2,1,0:T(8,128)S(1)} custom-call(s32[2,2,2]{2,1,0:T(2,128)S(1)} %bitcast.16, s32[2]{0:T(128)S(1)} %bitcast.22, f32[2,2,2,256,256]{4,3,2,1,0:T(8,128)S(1)} %get-tuple-element.35.refs_2_.refs_3_, f32[2,2,256,128]{3,2,1,0:T(8,128)S(1)} %get-tuple-element.36.refs_3_.refs_4_, bf16[2,2,2,256,256]{4,3,2,1,0:T(8,128)(2,1)S(1)} %copy-done.8, ...), custom_call_target="tpu_custom_call" | custom-call | flops 4000000000 | bytes 8388608 | tf_op jit(solution)/shard_map/pallas_call | solution.py:303
  70.3 1.9 collective-permute-done.7.refs_8_
  72.2 5.6 %shard_map.84 = (f32[2,2,256,256]{3,2,1,0:T(8,128)S(1)}, f32[2,256,256]{2,1,0:T(8,128)}, f32[2,256,256]{2,1,0:T(8,128)}, f32[2,2,256,256]{3,2,1,0:T(8,128)S(1)}) custom-call(s32[2,2,2]{2,1,0:T(2,128)S(1)} %bitcast.17, s32[2]{0:T(128)S(1)} %bitcast.23, f32[2,2,256,256]{3,2,1,0:T(8,128)S(1)} %shard_map.83.refs_2_, ...), custom_call_target="tpu_custom_call" | custom-call | flops 4000000000 | bytes 8388608 | tf_op jit(solution)/shard_map/pallas_call | solution.py:303
  77.8 4.9 %shard_map.85 = (f32[2,2,256,256]{3,2,1,0:T(8,128)S(1)}, f32[2,256,256]{2,1,0:T(8,128)}, f32[2,256,256]{2,1,0:T(8,128)}) custom-call(s32[2,2,2]{2,1,0:T(2,128)S(1)} %bitcast.18, s32[2]{0:T(128)S(1)} %bitcast.24, f32[2,2,256,256]{3,2,1,0:T(8,128)S(1)} %get-tuple-element.38.refs_2_, f32[2,2,2,256,256]{4,3,2,1,0:T(8,128)S(1)} %get-tuple-element.35.refs_2_.refs_3_, ...), custom_call_target="tpu_custom_call" | custom-call | flops 4000000000 | bytes 8388608 | tf_op jit(solution)/shard_map/pallas_call | solution.py:303
  82.7 1.0 copy-done
  83.7 1.9 collective-permute-start.8
  85.6 1.9 collective-permute-start.9
  87.5 1.9 collective-permute-start.12
  89.5 5.1 %collective-permute-start.13 = (f32[2,256,256]{2,1,0:T(8,128)}, f32[2,256,256]{2,1,0:T(8,128)}, u32[]{:S(2)}, u32[]{:S(2)}) collective-permute-start(f32[2,256,256]{2,1,0:T(8,128)} %get-tuple-element.47), channel_id=1, source_target_pairs={{0,1},{1,2},{2,3},{3,20},{4,5},{5,6},{6,7},{7,24},{8,9},{9,10},{10... | collective-permute-start | bytes 1572872 | tf_op jit(solution)/shard_map/ppermute | solution.py:47
  94.5 4.9 %collective-permute-done.8.side = f32[2,256,256]{2,1,0:T(8,128)} collective-permute-done((f32[2,256,256]{2,1,0:T(8,128)}, f32[2,256,256]{2,1,0:T(8,128)}, u32[]{:S(2)}, u32[]{:S(2)}) %collective-permute-start.8) | collective-permute-done | bytes 524320 | tf_op jit(solution)/shard_map/ppermute | solution.py:36
  99.4 3.5 %collective-permute-done.9.diag = f32[2,256,256]{2,1,0:T(8,128)} collective-permute-done((f32[2,256,256]{2,1,0:T(8,128)}, f32[2,256,256]{2,1,0:T(8,128)}, u32[]{:S(2)}, u32[]{:S(2)}) %collective-permute-start.9) | collective-permute-done | bytes 524320 | tf_op jit(solution)/shard_map/ppermute | solution.py:47
  102.9 1.2 copy-done.1
  104.2 1.4 shard_map.86
  105.6 5.1 %collective-permute-start.11 = (f32[2,256,256]{2,1,0:T(8,128)S(1)}, f32[2,256,256]{2,1,0:T(8,128)S(1)}, u32[]{:S(2)}, u32[]{:S(2)}) collective-permute-start(f32[2,256,256]{2,1,0:T(8,128)S(1)} %get-tuple-element.42.above), channel_id=1, source_target_pairs={{16,0},{32,16},{48,32},{64,48},{80,64},{96,80},{112,96},{128,112},... | collective-permute-start | bytes 1572872 | tf_op jit(solution)/shard_map/ppermute | solution.py:36
  110.6 2.9 %collective-permute-start.10 = (f32[2,256,256]{2,1,0:T(8,128)S(1)}, f32[2,256,256]{2,1,0:T(8,128)S(1)}, u32[]{:S(2)}, u32[]{:S(2)}) collective-permute-start(f32[2,256,256]{2,1,0:T(8,128)S(1)} %get-tuple-element.43.below), channel_id=1, source_target_pairs={{0,16},{16,32},{32,48},{48,64},{64,80},{80,96},{96,112},{112,128},... | collective-permute-start | bytes 1572872 | tf_op jit(solution)/shard_map/ppermute | solution.py:36
  113.5 18.5 %collective-permute-done.12.side = f32[2,256,256]{2,1,0:T(8,128)S(1)} collective-permute-done((f32[2,256,256]{2,1,0:T(8,128)}, f32[2,256,256]{2,1,0:T(8,128)S(1)}, u32[]{:S(2)}, u32[]{:S(2)}) %collective-permute-start.12) | collective-permute-done | bytes 524320 | tf_op jit(solution)/shard_map/ppermute | solution.py:36
  132.0 3.1 %collective-permute-done.13.diag = f32[2,256,256]{2,1,0:T(8,128)} collective-permute-done((f32[2,256,256]{2,1,0:T(8,128)}, f32[2,256,256]{2,1,0:T(8,128)}, u32[]{:S(2)}, u32[]{:S(2)}) %collective-permute-start.13) | collective-permute-done | bytes 524320 | tf_op jit(solution)/shard_map/ppermute | solution.py:47
  135.1 1.2 shard_map.88
  136.3 1.9 collective-permute-start.15
  138.2 6.0 %collective-permute-start.14 = (f32[2,256,256]{2,1,0:T(8,128)S(1)}, f32[2,256,256]{2,1,0:T(8,128)S(1)}, u32[]{:S(2)}, u32[]{:S(2)}) collective-permute-start(f32[2,256,256]{2,1,0:T(8,128)S(1)} %get-tuple-element.49.below), channel_id=1, source_target_pairs={{0,16},{16,32},{32,48},{48,64},{64,80},{80,96},{96,112},{112,128},... | collective-permute-start | bytes 1572872 | tf_op jit(solution)/shard_map/ppermute | solution.py:36
  144.3 2.2 collective-permute-done.10.from_above
  146.5 0.2 shard_map.87
  146.7 0.0 copy-start.9
  146.7 2.2 collective-permute-start.17
  148.9 2.9 %collective-permute-start.16 = (f32[2,256,256]{2,1,0:T(8,128)S(1)}, f32[2,256,256]{2,1,0:T(8,128)S(1)}, u32[]{:S(2)}, u32[]{:S(2)}) collective-permute-start(f32[2,256,256]{2,1,0:T(8,128)S(1)} %get-tuple-element.44.refs_5_.one), channel_id=1, source_target_pairs={{1,0},{2,1},{3,2},{4,3},{5,4},{6,5},{7,6},{8,7},{9,8},{10,9},{11,1... | collective-permute-start | bytes 1572872 | tf_op jit(solution)/shard_map/ppermute | solution.py:36
  151.8 0.1 collective-permute-done.15.from_below
  151.9 1.2 collective-permute-done.14.from_above
  153.1 0.2 shard_map.89
  153.3 6.0 %collective-permute-start.19 = (f32[2,256,256]{2,1,0:T(8,128)S(1)}, f32[2,256,256]{2,1,0:T(8,128)S(1)}, u32[]{:S(2)}, u32[]{:S(2)}) collective-permute-start(f32[2,256,256]{2,1,0:T(8,128)S(1)} %get-tuple-element.54), channel_id=1, source_target_pairs={{1,0},{2,1},{3,2},{5,4},{6,5},{7,6},{9,8},{10,9},{11,10},{13,12},{... | collective-permute-start | bytes 1572872 | tf_op jit(solution)/shard_map/ppermute | solution.py:47
  159.3 1.9 collective-permute-start.18
  161.2 4.0 %collective-permute-done.16.refs_6_ = f32[2,256,256]{2,1,0:T(8,128)S(1)} collective-permute-done((f32[2,256,256]{2,1,0:T(8,128)S(1)}, f32[2,256,256]{2,1,0:T(8,128)S(1)}, u32[]{:S(2)}, u32[]{:S(2)}) %collective-permute-start.16) | collective-permute-done | bytes 524320 | tf_op jit(solution)/shard_map/ppermute | solution.py:36
  165.2 3.6 %shard_map.90.refs_2_ = f32[2,2,256,256]{3,2,1,0:T(8,128)S(1)} custom-call(s32[2,2,2]{2,1,0:T(2,128)S(1)} %bitcast.19, s32[2]{0:T(128)S(1)} %bitcast.25, f32[2,2,2,256,256]{4,3,2,1,0:T(8,128)S(1)} %copy-done.12, f32[2,2,256,128]{3,2,1,0:T(8,128)S(1)} %copy-done.16, bf16[2,2,2,256,256]{4,3,2,1,0:T(8,128)(2,1)S(1)} %copy-done.9, ...), custom_call_target="tpu_custom_call" | custom-call | flops 4000000000 | bytes 8388608 | tf_op jit(solution)/shard_map/pallas_call | solution.py:303
  168.8 1.8 collective-permute-done.19.refs_8_
  170.6 4.6 %collective-permute-done.18.refs_6_ = f32[2,256,256]{2,1,0:T(8,128)S(1)} collective-permute-done((f32[2,256,256]{2,1,0:T(8,128)S(1)}, f32[2,256,256]{2,1,0:T(8,128)S(1)}, u32[]{:S(2)}, u32[]{:S(2)}) %collective-permute-start.18) | collective-permute-done | bytes 524320 | tf_op jit(solution)/shard_map/ppermute | solution.py:36
  175.2 4.7 %shard_map.91 = (f32[2,2,256,256]{3,2,1,0:T(8,128)S(1)}, f32[2,2,256,256]{3,2,1,0:T(8,128)S(1)}, f32[2,2,256,256]{3,2,1,0:T(8,128)S(1)}) custom-call(s32[2,2,2]{2,1,0:T(2,128)S(1)} %bitcast.20, s32[2]{0:T(128)S(1)} %bitcast.26, f32[2,2,256,256]{3,2,1,0:T(8,128)S(1)} %shard_map.90.refs_2_, f32[2,2,2,256,128]{4,3,2,1,0:T(8,128)S(1)} %copy-done.14, ...), custom_call_target="tpu_custom_call" | custom-call | flops 4000000000 | bytes 8388608 | tf_op jit(solution)/shard_map/pallas_call | solution.py:303
  179.9 1.9 collective-permute-start.21
  181.9 4.0 %shard_map.92 = (f32[2,2,256,256]{3,2,1,0:T(8,128)S(1)}, f32[2,2,256,256]{3,2,1,0:T(8,128)S(1)}) custom-call(s32[2,2,2]{2,1,0:T(2,128)S(1)} %bitcast.21, s32[2]{0:T(128)S(1)} %bitcast.27, f32[2,2,256,256]{3,2,1,0:T(8,128)S(1)} %get-tuple-element.55.refs_2_, f32[2,2,2,256,256]{4,3,2,1,0:T(8,128)S(1)} %copy-done.12, f32[2,2,256,128]{3,2,1,0:T(8,128)S(1)} %copy-done.16, ...), custom_call_target="tpu_custom_call" | custom-call | flops 4000000000 | bytes 8388608 | tf_op jit(solution)/shard_map/pallas_call | solution.py:303
  185.9 1.9 collective-permute-start.20
  187.8 9.2 %collective-permute-done.21.came = f32[2,2,256,256]{3,2,1,0:T(8,128)S(1)} collective-permute-done((f32[2,2,256,256]{3,2,1,0:T(8,128)S(1)}, f32[2,2,256,256]{3,2,1,0:T(8,128)S(1)}, u32[]{:S(2)}, u32[]{:S(2)}) %collective-permute-start.21) | collective-permute-done | bytes 1048608 | tf_op jit(solution)/shard_map/ppermute | solution.py:36
  197.0 0.1 shard_map.94
  197.1 1.9 collective-permute-start.23
  199.0 28.1 %collective-permute-done.20.came = f32[2,2,256,256]{3,2,1,0:T(8,128)S(1)} collective-permute-done((f32[2,2,256,256]{3,2,1,0:T(8,128)S(1)}, f32[2,2,256,256]{3,2,1,0:T(8,128)S(1)}, u32[]{:S(2)}, u32[]{:S(2)}) %collective-permute-start.20) | collective-permute-done | bytes 1048608 | tf_op jit(solution)/shard_map/ppermute | solution.py:36
  227.1 0.1 shard_map.93
  227.2 1.9 collective-permute-start.25
  229.2 8.9 %collective-permute-start.22 = (f32[256,256]{1,0:T(8,128)S(1)}, f32[256,256]{1,0:T(8,128)S(1)}, u32[]{:S(2)}, u32[]{:S(2)}) collective-permute-start(f32[256,256]{1,0:T(8,128)S(1)} %get-tuple-element.62), channel_id=1, source_target_pairs={{0,16},{16,32},{32,48},{48,64},{64,80},{80,96},{96,112},{112,128},... | collective-permute-start | bytes 786440 | tf_op jit(solution)/shard_map/ppermute | solution.py:36
  238.1 1.9 collective-permute-start.24
  240.0 4.9 %collective-permute-done.22.near2 = f32[256,256]{1,0:T(8,128)S(1)} collective-permute-done((f32[256,256]{1,0:T(8,128)S(1)}, f32[256,256]{1,0:T(8,128)S(1)}, u32[]{:S(2)}, u32[]{:S(2)}) %collective-permute-start.22) | collective-permute-done | bytes 262176 | tf_op jit(solution)/shard_map/ppermute | solution.py:36
  244.9 6.8 %collective-permute-done.24.far2 = f32[256,256]{1,0:T(8,128)S(1)} collective-permute-done((f32[256,256]{1,0:T(8,128)S(1)}, f32[256,256]{1,0:T(8,128)S(1)}, u32[]{:S(2)}, u32[]{:S(2)}) %collective-permute-start.24) | collective-permute-done | bytes 262176 | tf_op jit(solution)/shard_map/ppermute | solution.py:47
  251.8 1.2 shard_map.95
  (44 shorter events, 0.2 us)
Async XLA Ops:
  0.0 51.7 %copy-start.10 = (bf16[2,256,256]{2,1,0:T(8,128)(2,1)S(1)}, bf16[2,256,256]{2,1,0:T(8,128)(2,1)}, u32[]{:S(2)}) copy-start(bf16[2,256,256]{2,1,0:T(8,128)(2,1)} %constant.23.clone.perm_ref) | copy-start | bytes 786436
  0.0 3.4 %copy-start.17 = (f32[2,2,256,256]{3,2,1,0:T(8,128)S(1)}, f32[2,2,256,256]{3,2,1,0:T(8,128)}, u32[]{:S(2)}) copy-start(f32[2,2,256,256]{3,2,1,0:T(8,128)} %param.8) | copy-start | bytes 3145732
  0.0 42.2 %copy-start.18 = (f32[256,256]{1,0:T(8,128)S(1)}, f32[256,256]{1,0:T(8,128)}, u32[]{:S(2)}) copy-start(f32[256,256]{1,0:T(8,128)} %param.10) | copy-start | bytes 786436
  0.0 51.7 %copy-start.4 = (f32[2,1,1,2,256,256]{5,4,3,2,1,0:T(8,128)S(1)}, f32[2,1,1,2,256,256]{5,4,3,2,1,0:T(8,128)}, u32[]{:S(2)}) copy-start(f32[2,1,1,2,256,256]{5,4,3,2,1,0:T(8,128)} %param.13) | copy-start | bytes 3145732
  0.0 51.7 %copy-start.6 = (s32[2,1,1,2,2]{4,3,2,1,0:T(2,128)S(1)}, s32[2,1,1,2,2]{4,3,2,1,0:T(2,128)}, u32[]{:S(2)}) copy-start(s32[2,1,1,2,2]{4,3,2,1,0:T(2,128)} %param.11) | copy-start | bytes 100
  0.0 51.7 %copy-start.5 = (f32[2,256,256]{2,1,0:T(8,128)S(1)}, f32[2,256,256]{2,1,0:T(8,128)}, u32[]{:S(2)}) copy-start(f32[2,256,256]{2,1,0:T(8,128)} %probe_ref.1) | copy-start | bytes 1572868
  1.5 38.8 %collective-permute-start.1 = (f32[2,256,256]{2,1,0:T(8,128)S(1)}, f32[2,256,256]{2,1,0:T(8,128)S(1)}, u32[]{:S(2)}, u32[]{:S(2)}) collective-permute-start(f32[2,256,256]{2,1,0:T(8,128)S(1)} %get-tuple-element.68.refs_5_.old), channel_id=1, source_target_pairs={{16,0},{32,16},{48,32},{64,48},{80,64},{96,80},{112,96},{128,112},... | collective-permute-start | bytes 1572872 | tf_op jit(solution)/shard_map/ppermute | solution.py:36
  3.5 24.2 %collective-permute-start.5 = (f32[256,256]{1,0:T(8,128)S(1)}, f32[256,256]{1,0:T(8,128)S(1)}, u32[]{:S(2)}, u32[]{:S(2)}) collective-permute-start(f32[256,256]{1,0:T(8,128)S(1)} %get-tuple-element.66), channel_id=1, source_target_pairs={{16,34},{17,35},{18,48},{19,49},{20,38},{21,39},{22,52},{23,53},{2... | collective-permute-start | bytes 786440 | tf_op jit(solution)/shard_map/ppermute | solution.py:47
  10.8 32.4 %collective-permute-start.4 = (f32[256,256]{1,0:T(8,128)S(1)}, f32[256,256]{1,0:T(8,128)S(1)}, u32[]{:S(2)}, u32[]{:S(2)}) collective-permute-start(f32[256,256]{1,0:T(8,128)S(1)} %get-tuple-element.65), channel_id=1, source_target_pairs={{16,0},{32,16},{48,32},{64,48},{80,64},{96,80},{112,96},{128,112},... | collective-permute-start | bytes 786440 | tf_op jit(solution)/shard_map/ppermute | solution.py:36
  27.7 22.1 %collective-permute-start.6 = (f32[256,256]{1,0:T(8,128)S(1)}, f32[256,256]{1,0:T(8,128)S(1)}, u32[]{:S(2)}, u32[]{:S(2)}) collective-permute-start(f32[256,256]{1,0:T(8,128)S(1)} %collective-permute-done.5), channel_id=1, source_target_pairs={{0,18},{1,19},{2,32},{3,33},{4,22},{5,23},{6,36},{7,37},{8,26},{9,... | collective-permute-start | bytes 786440 | tf_op jit(solution)/shard_map/ppermute | solution.py:47
  34.0 21.4 %collective-permute-start = (f32[2,256,256]{2,1,0:T(8,128)S(1)}, f32[2,256,256]{2,1,0:T(8,128)S(1)}, u32[]{:S(2)}, u32[]{:S(2)}) collective-permute-start(f32[2,256,256]{2,1,0:T(8,128)S(1)} %get-tuple-element.68.refs_5_.old), channel_id=1, source_target_pairs={{1,0},{2,1},{3,2},{4,3},{5,4},{6,5},{7,6},{8,7},{9,8},{10,9},{11,1... | collective-permute-start | bytes 1572872 | tf_op jit(solution)/shard_map/ppermute | solution.py:36
  35.9 34.4 %collective-permute-start.3 = (f32[2,256,256]{2,1,0:T(8,128)S(1)}, f32[2,256,256]{2,1,0:T(8,128)S(1)}, u32[]{:S(2)}, u32[]{:S(2)}) collective-permute-start(f32[2,256,256]{2,1,0:T(8,128)S(1)} %get-tuple-element.67.refs_5_.old), channel_id=1, source_target_pairs={{1,0},{2,1},{3,2},{4,3},{5,4},{6,5},{7,6},{8,7},{9,8},{10,9},{11,1... | collective-permute-start | bytes 1572872 | tf_op jit(solution)/shard_map/ppermute | solution.py:36
  40.3 26.3 %copy-start.2 = (f32[2,256,256]{2,1,0:T(8,128)}, f32[2,256,256]{2,1,0:T(8,128)S(1)}, u32[]{:S(2)}) copy-start(f32[2,256,256]{2,1,0:T(8,128)S(1)} %collective-permute-done.1.refs_7_.old_low) | copy-start | bytes 1572868
  40.3 26.3 %collective-permute-start.2 = (f32[2,256,256]{2,1,0:T(8,128)S(1)}, f32[2,256,256]{2,1,0:T(8,128)S(1)}, u32[]{:S(2)}, u32[]{:S(2)}) collective-permute-start(f32[2,256,256]{2,1,0:T(8,128)S(1)} %collective-permute-done.1.refs_7_.old_low), channel_id=1, source_target_pairs={{1,0},{2,1},{3,2},{4,3},{5,4},{6,5},{7,6},{8,7},{9,8},{10,9},{11,1... | collective-permute-start | bytes 1572872 | tf_op jit(solution)/shard_map/ppermute | solution.py:36
  49.8 22.4 %collective-permute-start.7 = (f32[2,256,256]{2,1,0:T(8,128)S(1)}, f32[2,256,256]{2,1,0:T(8,128)S(1)}, u32[]{:S(2)}, u32[]{:S(2)}) collective-permute-start(f32[2,256,256]{2,1,0:T(8,128)S(1)} %pad_maximum_fusion.refs_7_.old_low), channel_id=1, source_target_pairs={{1,0},{2,1},{3,2},{4,3},{5,4},{6,5},{7,6},{8,7},{9,8},{10,9},{11,1... | collective-permute-start | bytes 1572872 | tf_op jit(solution)/shard_map/ppermute | solution.py:36
  51.7 14.9 %copy-start.7 = (s32[2,1,1]{0,2,1:T(1,128)S(1)}, s32[2,1,1]{0,2,1:T(1,128)}, u32[]{:S(2)}) copy-start(s32[2,1,1]{0,2,1:T(1,128)} %param.12) | copy-start | bytes 28
  51.8 14.8 %copy-start.8 = (bf16[2,2,2,256,256]{4,3,2,1,0:T(8,128)(2,1)S(1)}, bf16[2,2,2,256,256]{4,3,2,1,0:T(8,128)(2,1)}, u32[]{:S(2)}) copy-start(bf16[2,2,2,256,256]{4,3,2,1,0:T(8,128)(2,1)} %constant.22.clone.refs_4_.refs_5_) | copy-start | bytes 3145732
  55.4 16.8 %copy-start.13 = (f32[2,2,2,256,128]{4,3,2,1,0:T(8,128)}, f32[2,2,2,256,128]{4,3,2,1,0:T(8,128)S(1)}, u32[]{:S(2)}) copy-start(f32[2,2,2,256,128]{4,3,2,1,0:T(8,128)S(1)} %get-tuple-element.37.refs_3_) | copy-start | bytes 3145732
  55.4 22.4 %copy-start.11 = (f32[2,2,2,256,256]{4,3,2,1,0:T(8,128)}, f32[2,2,2,256,256]{4,3,2,1,0:T(8,128)S(1)}, u32[]{:S(2)}) copy-start(f32[2,2,2,256,256]{4,3,2,1,0:T(8,128)S(1)} %get-tuple-element.35.refs_2_.refs_3_) | copy-start | bytes 6291460
  55.4 22.4 %copy-start.15 = (f32[2,2,256,128]{3,2,1,0:T(8,128)}, f32[2,2,256,128]{3,2,1,0:T(8,128)S(1)}, u32[]{:S(2)}) copy-start(f32[2,2,256,128]{3,2,1,0:T(8,128)S(1)} %get-tuple-element.36.refs_3_.refs_4_) | copy-start | bytes 1572868
  82.7 1.0 copy-start
  83.7 15.7 %collective-permute-start.8 = (f32[2,256,256]{2,1,0:T(8,128)}, f32[2,256,256]{2,1,0:T(8,128)}, u32[]{:S(2)}, u32[]{:S(2)}) collective-permute-start(f32[2,256,256]{2,1,0:T(8,128)} %get-tuple-element.40), channel_id=1, source_target_pairs={{0,1},{1,2},{2,3},{3,4},{4,5},{5,6},{6,7},{7,8},{8,9},{9,10},{10,1... | collective-permute-start | bytes 1572872 | tf_op jit(solution)/shard_map/ppermute | solution.py:36
  85.6 17.3 %collective-permute-start.9 = (f32[2,256,256]{2,1,0:T(8,128)}, f32[2,256,256]{2,1,0:T(8,128)}, u32[]{:S(2)}, u32[]{:S(2)}) collective-permute-start(f32[2,256,256]{2,1,0:T(8,128)} %get-tuple-element.41), channel_id=1, source_target_pairs={{0,1},{1,2},{2,3},{3,20},{4,5},{5,6},{6,7},{7,24},{8,9},{9,10},{10... | collective-permute-start | bytes 1572872 | tf_op jit(solution)/shard_map/ppermute | solution.py:47
  87.5 44.5 %collective-permute-start.12 = (f32[2,256,256]{2,1,0:T(8,128)}, f32[2,256,256]{2,1,0:T(8,128)S(1)}, u32[]{:S(2)}, u32[]{:S(2)}) collective-permute-start(f32[2,256,256]{2,1,0:T(8,128)} %get-tuple-element.46), channel_id=1, source_target_pairs={{0,1},{1,2},{2,3},{3,4},{4,5},{5,6},{6,7},{7,8},{8,9},{9,10},{10,1... | collective-permute-start | bytes 1572872 | tf_op jit(solution)/shard_map/ppermute | solution.py:36
  89.5 45.7 %collective-permute-start.13 = (f32[2,256,256]{2,1,0:T(8,128)}, f32[2,256,256]{2,1,0:T(8,128)}, u32[]{:S(2)}, u32[]{:S(2)}) collective-permute-start(f32[2,256,256]{2,1,0:T(8,128)} %get-tuple-element.47), channel_id=1, source_target_pairs={{0,1},{1,2},{2,3},{3,20},{4,5},{5,6},{6,7},{7,24},{8,9},{9,10},{10... | collective-permute-start | bytes 1572872 | tf_op jit(solution)/shard_map/ppermute | solution.py:47
  102.9 1.2 copy-start.1
  104.2 42.3 %copy-start.3 = (f32[2,256,256]{2,1,0:T(8,128)S(1)}, f32[2,256,256]{2,1,0:T(8,128)}, u32[]{:S(2)}) copy-start(f32[2,256,256]{2,1,0:T(8,128)} %copy-done.2) | copy-start | bytes 1572868
  105.6 38.7 %collective-permute-start.11 = (f32[2,256,256]{2,1,0:T(8,128)S(1)}, f32[2,256,256]{2,1,0:T(8,128)S(1)}, u32[]{:S(2)}, u32[]{:S(2)}) collective-permute-start(f32[2,256,256]{2,1,0:T(8,128)S(1)} %get-tuple-element.42.above), channel_id=1, source_target_pairs={{16,0},{32,16},{48,32},{64,48},{80,64},{96,80},{112,96},{128,112},... | collective-permute-start | bytes 1572872 | tf_op jit(solution)/shard_map/ppermute | solution.py:36
  110.6 35.9 %collective-permute-start.10 = (f32[2,256,256]{2,1,0:T(8,128)S(1)}, f32[2,256,256]{2,1,0:T(8,128)S(1)}, u32[]{:S(2)}, u32[]{:S(2)}) collective-permute-start(f32[2,256,256]{2,1,0:T(8,128)S(1)} %get-tuple-element.43.below), channel_id=1, source_target_pairs={{0,16},{16,32},{32,48},{48,64},{64,80},{80,96},{96,112},{112,128},... | collective-permute-start | bytes 1572872 | tf_op jit(solution)/shard_map/ppermute | solution.py:36
  136.3 15.6 %collective-permute-start.15 = (f32[2,256,256]{2,1,0:T(8,128)S(1)}, f32[2,256,256]{2,1,0:T(8,128)S(1)}, u32[]{:S(2)}, u32[]{:S(2)}) collective-permute-start(f32[2,256,256]{2,1,0:T(8,128)S(1)} %get-tuple-element.48.above), channel_id=1, source_target_pairs={{16,0},{32,16},{48,32},{64,48},{80,64},{96,80},{112,96},{128,112},... | collective-permute-start | bytes 1572872 | tf_op jit(solution)/shard_map/ppermute | solution.py:36
  138.2 14.9 %collective-permute-start.14 = (f32[2,256,256]{2,1,0:T(8,128)S(1)}, f32[2,256,256]{2,1,0:T(8,128)S(1)}, u32[]{:S(2)}, u32[]{:S(2)}) collective-permute-start(f32[2,256,256]{2,1,0:T(8,128)S(1)} %get-tuple-element.49.below), channel_id=1, source_target_pairs={{0,16},{16,32},{32,48},{48,64},{64,80},{80,96},{96,112},{112,128},... | collective-permute-start | bytes 1572872 | tf_op jit(solution)/shard_map/ppermute | solution.py:36
  146.5 18.7 %copy-start.16 = (f32[2,2,256,128]{3,2,1,0:T(8,128)S(1)}, f32[2,2,256,128]{3,2,1,0:T(8,128)}, u32[]{:S(2)}) copy-start(f32[2,2,256,128]{3,2,1,0:T(8,128)} %copy-done.15) | copy-start | bytes 1572868
  146.7 18.5 %copy-start.9 = (bf16[2,2,2,256,256]{4,3,2,1,0:T(8,128)(2,1)S(1)}, bf16[2,2,2,256,256]{4,3,2,1,0:T(8,128)(2,1)}, u32[]{:S(2)}) copy-start(bf16[2,2,2,256,256]{4,3,2,1,0:T(8,128)(2,1)} %constant.22.clone.refs_4_.refs_5_) | copy-start | bytes 3145732
  146.7 18.5 %copy-start.12 = (f32[2,2,2,256,256]{4,3,2,1,0:T(8,128)S(1)}, f32[2,2,2,256,256]{4,3,2,1,0:T(8,128)}, u32[]{:S(2)}) copy-start(f32[2,2,2,256,256]{4,3,2,1,0:T(8,128)} %copy-done.11) | copy-start | bytes 6291460
  146.7 14.5 %collective-permute-start.17 = (f32[2,256,256]{2,1,0:T(8,128)S(1)}, f32[2,256,256]{2,1,0:T(8,128)S(1)}, u32[]{:S(2)}, u32[]{:S(2)}) collective-permute-start(f32[2,256,256]{2,1,0:T(8,128)S(1)} %get-tuple-element.52), channel_id=1, source_target_pairs={{1,0},{2,1},{3,2},{5,4},{6,5},{7,6},{9,8},{10,9},{11,10},{13,12},{... | collective-permute-start | bytes 1572872 | tf_op jit(solution)/shard_map/ppermute | solution.py:47
  148.9 16.3 %collective-permute-start.16 = (f32[2,256,256]{2,1,0:T(8,128)S(1)}, f32[2,256,256]{2,1,0:T(8,128)S(1)}, u32[]{:S(2)}, u32[]{:S(2)}) collective-permute-start(f32[2,256,256]{2,1,0:T(8,128)S(1)} %get-tuple-element.44.refs_5_.one), channel_id=1, source_target_pairs={{1,0},{2,1},{3,2},{4,3},{5,4},{6,5},{7,6},{8,7},{9,8},{10,9},{11,1... | collective-permute-start | bytes 1572872 | tf_op jit(solution)/shard_map/ppermute | solution.py:36
  153.3 17.3 %collective-permute-start.19 = (f32[2,256,256]{2,1,0:T(8,128)S(1)}, f32[2,256,256]{2,1,0:T(8,128)S(1)}, u32[]{:S(2)}, u32[]{:S(2)}) collective-permute-start(f32[2,256,256]{2,1,0:T(8,128)S(1)} %get-tuple-element.54), channel_id=1, source_target_pairs={{1,0},{2,1},{3,2},{5,4},{6,5},{7,6},{9,8},{10,9},{11,10},{13,12},{... | collective-permute-start | bytes 1572872 | tf_op jit(solution)/shard_map/ppermute | solution.py:47
  159.3 15.9 %collective-permute-start.18 = (f32[2,256,256]{2,1,0:T(8,128)S(1)}, f32[2,256,256]{2,1,0:T(8,128)S(1)}, u32[]{:S(2)}, u32[]{:S(2)}) collective-permute-start(f32[2,256,256]{2,1,0:T(8,128)S(1)} %get-tuple-element.50.refs_5_.two), channel_id=1, source_target_pairs={{1,0},{2,1},{3,2},{4,3},{5,4},{6,5},{7,6},{8,7},{9,8},{10,9},{11,1... | collective-permute-start | bytes 1572872 | tf_op jit(solution)/shard_map/ppermute | solution.py:36
  165.2 10.0 %copy-start.14 = (f32[2,2,2,256,128]{4,3,2,1,0:T(8,128)S(1)}, f32[2,2,2,256,128]{4,3,2,1,0:T(8,128)}, u32[]{:S(2)}) copy-start(f32[2,2,2,256,128]{4,3,2,1,0:T(8,128)} %copy-done.13) | copy-start | bytes 3145732
  179.9 17.0 %collective-permute-start.21 = (f32[2,2,256,256]{3,2,1,0:T(8,128)S(1)}, f32[2,2,256,256]{3,2,1,0:T(8,128)S(1)}, u32[]{:S(2)}, u32[]{:S(2)}) collective-permute-start(f32[2,2,256,256]{3,2,1,0:T(8,128)S(1)} %get-tuple-element.60), channel_id=1, source_target_pairs={{0,1},{1,2},{2,3},{3,4},{4,5},{5,6},{6,7},{7,8},{8,9},{9,10},{10,1... | collective-permute-start | bytes 3145736 | tf_op jit(solution)/shard_map/ppermute | solution.py:36
  185.9 41.2 %collective-permute-start.20 = (f32[2,2,256,256]{3,2,1,0:T(8,128)S(1)}, f32[2,2,256,256]{3,2,1,0:T(8,128)S(1)}, u32[]{:S(2)}, u32[]{:S(2)}) collective-permute-start(f32[2,2,256,256]{3,2,1,0:T(8,128)S(1)} %get-tuple-element.57), channel_id=1, source_target_pairs={{0,1},{1,2},{2,3},{3,4},{4,5},{5,6},{6,7},{7,8},{8,9},{9,10},{10,1... | collective-permute-start | bytes 3145736 | tf_op jit(solution)/shard_map/ppermute | solution.py:36
  197.1 41.0 %collective-permute-start.23 = (f32[256,256]{1,0:T(8,128)S(1)}, f32[256,256]{1,0:T(8,128)S(1)}, u32[]{:S(2)}, u32[]{:S(2)}) collective-permute-start(f32[256,256]{1,0:T(8,128)S(1)} %get-tuple-element.63), channel_id=1, source_target_pairs={{0,34},{1,35},{2,48},{3,49},{4,38},{5,39},{6,52},{7,53},{8,42},{9,... | collective-permute-start | bytes 786440 | tf_op jit(solution)/shard_map/ppermute | solution.py:47
  227.2 17.7 %collective-permute-start.25 = (f32[2,256,256]{2,1,0:T(8,128)S(1)}, f32[2,256,256]{2,1,0:T(8,128)S(1)}, u32[]{:S(2)}, u32[]{:S(2)}) collective-permute-start(f32[2,256,256]{2,1,0:T(8,128)S(1)} %get-tuple-element.64), channel_id=1, source_target_pairs={{0,16},{16,32},{32,48},{48,64},{64,80},{80,96},{96,112},{112,128},... | collective-permute-start | bytes 1572872 | tf_op jit(solution)/shard_map/ppermute | solution.py:36
  229.2 15.8 %collective-permute-start.22 = (f32[256,256]{1,0:T(8,128)S(1)}, f32[256,256]{1,0:T(8,128)S(1)}, u32[]{:S(2)}, u32[]{:S(2)}) collective-permute-start(f32[256,256]{1,0:T(8,128)S(1)} %get-tuple-element.62), channel_id=1, source_target_pairs={{0,16},{16,32},{32,48},{48,64},{64,80},{80,96},{96,112},{112,128},... | collective-permute-start | bytes 786440 | tf_op jit(solution)/shard_map/ppermute | solution.py:36
  238.1 13.7 %collective-permute-start.24 = (f32[256,256]{1,0:T(8,128)S(1)}, f32[256,256]{1,0:T(8,128)S(1)}, u32[]{:S(2)}, u32[]{:S(2)}) collective-permute-start(f32[256,256]{1,0:T(8,128)S(1)} %collective-permute-done.23), channel_id=1, source_target_pairs={{0,34},{1,35},{2,48},{3,49},{4,38},{5,39},{6,52},{7,53},{8,42},{9,... | collective-permute-start | bytes 786440 | tf_op jit(solution)/shard_map/ppermute | solution.py:47

commit v4 on v3

--- a/solution.py
+++ b/solution.py
@@ -150,10 +150,10 @@
     diag[plane] += jnp.where(below, right_part, zero)
 
 
-def prepare_kernel(off_ref, probe_ref, cos_ref, sin_ref, amp_ref, perm_ref,
+def prepare_kernel(off_ref, probe_ref, angle_ref, amp_ref, perm_ref,
                    rolled_ref, prop_ref, ampl_ref, twice):
     def reorder(src):
-        rest = src[...]
+        rest = src
         total = None
         for _ in range(3):
             part = rest.astype(jnp.bfloat16)
@@ -174,14 +174,14 @@
             start = pl.multiple_of(SIDE - 8 - row // 8 * 8, 8)
             turned = pltpu.roll(twice[plane, pl.ds(start, SIDE + 8), :], row % 8, 0)
             rolled_ref[it, slot, plane] = pltpu.roll(turned[8:], col, 1)
-        put(ampl_ref.at[it, slot], reorder(amp_ref.at[it, slot]))
+        put(ampl_ref.at[it, slot], reorder(amp_ref[it, slot]))
         return carry
 
     for plane in range(2):
         twice[plane, :SIDE] = probe_ref[plane]
         twice[plane, SIDE:] = probe_ref[plane]
-    put(prop_ref.at[0], reorder(cos_ref))
-    put(prop_ref.at[1], reorder(sin_ref))
+    put(prop_ref.at[0], reorder(jnp.cos(angle_ref[...])))
+    put(prop_ref.at[1], reorder(jnp.sin(angle_ref[...])))
     lax.fori_loop(0, ITERS * SLOTS, tile_loop, 0)
 
 
@@ -257,12 +257,21 @@
     lax.fori_loop(0, cnt_ref[iteration], body, 0)
 
 
-def sums_kernel(first, stay, side, diag, above, below):
+def leading():
+    return lax.rem(lax.axis_index("tx"), 4) == 0
+
+
+def join_kernel(near, far, both):
+    both[0] = near[...]
+    both[1] = far[...]
+
+
+def sums_kernel(stay, side, diag, above, below):
     for plane in range(2):
         zero = jnp.zeros((SIDE, SIDE), jnp.float32)
         extra = diag[plane]
-        above[plane] = stay[0, plane] + side[plane] + jnp.where(first[0] > 0, extra, zero)
-        below[plane] = stay[1, plane] + jnp.where(first[0] > 0, zero, extra)
+        above[plane] = stay[0, plane] + side[plane] + jnp.where(leading(), extra, zero)
+        below[plane] = stay[1, plane] + jnp.where(leading(), zero, extra)
 
 
 def fall_kernel(stay, came, above, *below):
@@ -274,13 +283,13 @@
             below[plane][...] = stay[1, plane] + came[1, plane]
 
 
-def update_kernel(first, above, below, from_above, from_below, old, old_low, own, low, send):
+def update_kernel(above, below, from_above, from_below, old, old_low, own, low, send):
     for plane in range(2):
         one = old[plane] - step_size * (above[plane] + from_above[plane])
         two = old_low[plane] - step_size * (from_below[plane] + below[plane])
         own[plane] = one
         low[plane] = two
-        send[plane] = jnp.where(first[0] > 0, one, two)
+        send[plane] = jnp.where(leading(), one, two)
 
 
 def last_kernel(one, two, above1, above2, near2, far2, fallen1, out):
@@ -324,19 +333,18 @@
 
     sizes = lax.axis_size("ty"), lax.axis_size("tx")
     sizes = lax.axis_size("ty"), lax.axis_size("tx")
-    column = lax.axis_index("tx") % 4
-    first = (column == 0).astype(jnp.int32).reshape(1)
     own = [object_tiles[0], object_tiles[1]]
     low0 = shifted(own[0], "ty", -1)
     far = around(object_tiles[1, 1], -1, sizes)
     rgt = [shifted(own[s], "tx", -1) for s in (0, 1)]
     near = shifted(object_tiles[1, 0], "ty", -1)
-    low = [low0, jnp.stack([near, far])]
+    (low1,) = call(join_kernel, [], [near, far], [f32(2, SIDE, SIDE)], flops=10**6)
+    low = [low0, low1]
     dia = [shifted(low[s], "tx", -1) for s in (0, 1)]
 
     rolled, prop, ampl = call(
         prepare_kernel, [offsets],
-        [probe_field, jnp.cos(prop_angle), jnp.sin(prop_angle), measured, perm],
+        [probe_field, prop_angle, measured, perm],
         [f32(ITERS, SLOTS, 2, SIDE, SIDE), f32(2, 2, SIDE, HALF), f32(ITERS, SLOTS, 2, SIDE, HALF)],
         [pltpu.VMEM((2, 2 * SIDE, SIDE), jnp.float32)],
     )
@@ -376,12 +384,12 @@
         above, below = [None, None], [None, None]
         for s in (1, 0):
             side[s] = shifted(side[s], "tx", 1)
-            above[s], below[s] = call(sums_kernel, [first], [stay[s], side[s], diag[s]],
+            above[s], below[s] = call(sums_kernel, [], [stay[s], side[s], diag[s]],
                                       [tile, tile], flops=10**6)
         for s in (1, 0):
             fallen = shifted(below[s], "ty", 1)
             risen = shifted(above[s], "ty", -1)
-            own, low, send = call(update_kernel, [first],
+            own, low, send = call(update_kernel, [],
                                   [above[s], below[s], fallen, risen, tiles[s][0], tiles[s][2]],
                                   [tile] * 3, flops=10**6)
             tiles[s] = [own, shifted(own, "tx", -1), low,

time: 254 us -> 253 us (level)
  the two profiles are of different devices: /device:TPU:82 before, /device:TPU:17 now
where the time goes in v4:
time: 253 us; the launch traced here: 252 us
  waiting for transfers between devices  133 us (53%)
  starting transfers between devices  99.9 us (39%)
  Pallas kernels  16.7 us (7%)
    ppermute x8, waiting for transfers between devices, moved(): return lax.ppermute(value, ('ty', 'tx'), pairs)  72.5 us
    ppermute x18, starting transfers between devices, shifted(): lax.ppermute(value, axis, [(source, source + steps) for source in range(f...  63.5 us
    ppermute x18, waiting for transfers between devices, shifted(): lax.ppermute(value, axis, [(source, source + steps) for source in range(f...  60.6 us
    ppermute x8, starting transfers between devices, moved(): return lax.ppermute(value, ('ty', 'tx'), pairs)  36.4 us
    pallas_call x15, Pallas kernels, call(): pl.pallas_call(body, out_shape=outs, in_specs=[SMEM] * len(scalars) + [VM...  16.7 us
  transfers between devices with their start and end apart: 26, of which 13 were waited for; matrix products, arithmetic and copies ran while one was open for 0% of the time, Pallas kernels for 4%

profile of v4, /device:TPU:17, one launch (start us, length us, event | category | flops | bytes accessed | tf_op | source)
XLA Modules:
  0.0 251.7 jit_solution(987931441328045312)
XLA Ops:
  0.0 1.4 slice_bitcast_fusion
  1.5 7.8 %collective-permute-start.1 = (f32[2,256,256]{2,1,0:T(8,128)S(1)}, f32[2,256,256]{2,1,0:T(8,128)S(1)}, u32[]{:S(2)}, u32[]{:S(2)}) collective-permute-start(f32[2,256,256]{2,1,0:T(8,128)S(1)} %get-tuple-element.68.refs_5_.old), channel_id=1, source_target_pairs={{16,0},{32,16},{48,32},{64,48},{80,64},{96,80},{112,96},{128,112},... | collective-permute-start | bytes 1572872 | tf_op jit(solution)/shard_map/ppermute | solution.py:36
  9.4 1.9 collective-permute-start.5
  11.3 5.8 %collective-permute-start.4 = (f32[256,256]{1,0:T(8,128)S(1)}, f32[256,256]{1,0:T(8,128)S(1)}, u32[]{:S(2)}, u32[]{:S(2)}) collective-permute-start(f32[256,256]{1,0:T(8,128)S(1)} %get-tuple-element.66), channel_id=1, source_target_pairs={{16,0},{32,16},{48,32},{64,48},{80,64},{96,80},{112,96},{128,112},... | collective-permute-start | bytes 786440 | tf_op jit(solution)/shard_map/ppermute | solution.py:36
  17.1 15.2 %collective-permute-done.5 = f32[256,256]{1,0:T(8,128)S(1)} collective-permute-done((f32[256,256]{1,0:T(8,128)S(1)}, f32[256,256]{1,0:T(8,128)S(1)}, u32[]{:S(2)}, u32[]{:S(2)}) %collective-permute-start.5) | collective-permute-done | bytes 262176 | tf_op jit(solution)/shard_map/ppermute | solution.py:47
  32.3 1.9 collective-permute-start.6
  34.2 2.5 collective-permute-start
  36.7 0.0 collective-permute-done.1.refs_7_.old_low
  36.7 2.1 collective-permute-start.2
  38.9 1.9 collective-permute-start.3
  40.8 0.0 collective-permute-done.4.near
  40.8 13.0 %collective-permute-done.6.far = f32[256,256]{1,0:T(8,128)S(1)} collective-permute-done((f32[256,256]{1,0:T(8,128)S(1)}, f32[256,256]{1,0:T(8,128)S(1)}, u32[]{:S(2)}, u32[]{:S(2)}) %collective-permute-start.6) | collective-permute-done | bytes 262176 | tf_op jit(solution)/shard_map/ppermute | solution.py:47
  53.8 3.2 %collective-permute-start.7 = (f32[2,256,256]{2,1,0:T(8,128)S(1)}, f32[2,256,256]{2,1,0:T(8,128)S(1)}, u32[]{:S(2)}, u32[]{:S(2)}) collective-permute-start(f32[2,256,256]{2,1,0:T(8,128)S(1)} %shard_map.84.refs_7_.old_low), channel_id=1, source_target_pairs={{1,0},{2,1},{3,2},{4,3},{5,4},{6,5},{7,6},{8,7},{9,8},{10,9},{11,1... | collective-permute-start | bytes 1572872 | tf_op jit(solution)/shard_map/ppermute | solution.py:36
  57.1 0.0 copy-start.4
  57.1 0.0 copy-start.5
  57.1 5.1 %shard_map.82 = (f32[2,2,2,256,256]{4,3,2,1,0:T(8,128)S(1)}, f32[2,2,256,128]{3,2,1,0:T(8,128)S(1)}, f32[2,2,2,256,128]{4,3,2,1,0:T(8,128)S(1)}) custom-call(s32[2,2,2]{2,1,0:T(2,128)S(1)} %bitcast.12, f32[2,256,256]{2,1,0:T(8,128)S(1)} %copy-done.1, f32[256,256]{1,0:T(8,128)S(1)} %copy-done.2, f32[2,2,256,256]{3,2,1,0:T(8,128)S(1)} %bitcast.11, ...), custom_call_target="tpu_custom_call" | custom-call | flops 4000000000 | bytes 8388608 | tf_op jit(solution)/shard_map/pallas_call | solution.py:312
  62.2 0.0 collective-permute-done.refs_6_
  62.2 0.0 collective-permute-done.2.refs_8_
  62.3 0.6 shard_map.83.refs_2_
  62.9 0.0 collective-permute-done.3.refs_6_
  62.9 2.9 %collective-permute-done.7.refs_8_ = f32[2,256,256]{2,1,0:T(8,128)S(1)} collective-permute-done((f32[2,256,256]{2,1,0:T(8,128)S(1)}, f32[2,256,256]{2,1,0:T(8,128)S(1)}, u32[]{:S(2)}, u32[]{:S(2)}) %collective-permute-start.7) | collective-permute-done | bytes 524320 | tf_op jit(solution)/shard_map/ppermute | solution.py:36
  65.7 0.7 shard_map.85
  66.4 0.7 shard_map.86
  67.2 1.9 collective-permute-start.8
  69.1 18.8 %collective-permute-start.9 = (f32[2,256,256]{2,1,0:T(8,128)S(1)}, f32[2,256,256]{2,1,0:T(8,128)S(1)}, u32[]{:S(2)}, u32[]{:S(2)}) collective-permute-start(f32[2,256,256]{2,1,0:T(8,128)S(1)} %get-tuple-element.41), channel_id=1, source_target_pairs={{0,1},{1,2},{2,3},{3,20},{4,5},{5,6},{6,7},{7,24},{8,9},{9,10},{10... | collective-permute-start | bytes 1572872 | tf_op jit(solution)/shard_map/ppermute | solution.py:47
  87.9 1.9 collective-permute-start.12
  89.8 3.9 %collective-permute-start.13 = (f32[2,256,256]{2,1,0:T(8,128)S(1)}, f32[2,256,256]{2,1,0:T(8,128)S(1)}, u32[]{:S(2)}, u32[]{:S(2)}) collective-permute-start(f32[2,256,256]{2,1,0:T(8,128)S(1)} %get-tuple-element.47), channel_id=1, source_target_pairs={{0,1},{1,2},{2,3},{3,20},{4,5},{5,6},{6,7},{7,24},{8,9},{9,10},{10... | collective-permute-start | bytes 1572872 | tf_op jit(solution)/shard_map/ppermute | solution.py:47
  93.7 0.0 collective-permute-done.8.side
  93.7 0.3 collective-permute-done.9.diag
  94.0 0.1 shard_map.87
  94.2 9.4 %collective-permute-start.11 = (f32[2,256,256]{2,1,0:T(8,128)S(1)}, f32[2,256,256]{2,1,0:T(8,128)S(1)}, u32[]{:S(2)}, u32[]{:S(2)}) collective-permute-start(f32[2,256,256]{2,1,0:T(8,128)S(1)} %get-tuple-element.42.above), channel_id=1, source_target_pairs={{16,0},{32,16},{48,32},{64,48},{80,64},{96,80},{112,96},{128,112},... | collective-permute-start | bytes 1572872 | tf_op jit(solution)/shard_map/ppermute | solution.py:36
  103.5 1.9 collective-permute-start.10
  105.5 0.0 collective-permute-done.12.side
  105.5 0.1 shard_map.89
  105.6 8.2 %collective-permute-start.15 = (f32[2,256,256]{2,1,0:T(8,128)S(1)}, f32[2,256,256]{2,1,0:T(8,128)S(1)}, u32[]{:S(2)}, u32[]{:S(2)}) collective-permute-start(f32[2,256,256]{2,1,0:T(8,128)S(1)} %get-tuple-element.48.above), channel_id=1, source_target_pairs={{16,0},{32,16},{48,32},{64,48},{80,64},{96,80},{112,96},{128,112},... | collective-permute-start | bytes 1572872 | tf_op jit(solution)/shard_map/ppermute | solution.py:36
  113.9 2.8 %collective-permute-start.14 = (f32[2,256,256]{2,1,0:T(8,128)S(1)}, f32[2,256,256]{2,1,0:T(8,128)S(1)}, u32[]{:S(2)}, u32[]{:S(2)}) collective-permute-start(f32[2,256,256]{2,1,0:T(8,128)S(1)} %get-tuple-element.49.below), channel_id=1, source_target_pairs={{0,16},{16,32},{32,48},{48,64},{64,80},{80,96},{96,112},{112,128},... | collective-permute-start | bytes 1572872 | tf_op jit(solution)/shard_map/ppermute | solution.py:36
  116.7 8.4 %collective-permute-done.10.from_above = f32[2,256,256]{2,1,0:T(8,128)S(1)} collective-permute-done((f32[2,256,256]{2,1,0:T(8,128)S(1)}, f32[2,256,256]{2,1,0:T(8,128)S(1)}, u32[]{:S(2)}, u32[]{:S(2)}) %collective-permute-start.10) | collective-permute-done | bytes 524320 | tf_op jit(solution)/shard_map/ppermute | solution.py:36
  125.1 0.3 shard_map.88
  125.4 2.0 collective-permute-start.17
  127.4 1.9 collective-permute-start.16
  129.4 16.3 %collective-permute-done.15.from_below = f32[2,256,256]{2,1,0:T(8,128)S(1)} collective-permute-done((f32[2,256,256]{2,1,0:T(8,128)S(1)}, f32[2,256,256]{2,1,0:T(8,128)S(1)}, u32[]{:S(2)}, u32[]{:S(2)}) %collective-permute-start.15) | collective-permute-done | bytes 524320 | tf_op jit(solution)/shard_map/ppermute | solution.py:36
  145.7 11.3 %collective-permute-done.14.from_above = f32[2,256,256]{2,1,0:T(8,128)S(1)} collective-permute-done((f32[2,256,256]{2,1,0:T(8,128)S(1)}, f32[2,256,256]{2,1,0:T(8,128)S(1)}, u32[]{:S(2)}, u32[]{:S(2)}) %collective-permute-start.14) | collective-permute-done | bytes 524320 | tf_op jit(solution)/shard_map/ppermute | solution.py:36
  157.0 0.3 shard_map.90
  157.3 2.3 collective-permute-start.19
  159.6 1.9 collective-permute-start.18
  161.5 0.0 collective-permute-done.17.refs_8_
  161.5 2.1 shard_map.91.refs_2_
  163.6 4.2 %collective-permute-done.19.refs_8_ = f32[2,256,256]{2,1,0:T(8,128)S(1)} collective-permute-done((f32[2,256,256]{2,1,0:T(8,128)S(1)}, f32[2,256,256]{2,1,0:T(8,128)S(1)}, u32[]{:S(2)}, u32[]{:S(2)}) %collective-permute-start.19) | collective-permute-done | bytes 524320 | tf_op jit(solution)/shard_map/ppermute | solution.py:47
  167.8 5.6 %collective-permute-done.18.refs_6_ = f32[2,256,256]{2,1,0:T(8,128)S(1)} collective-permute-done((f32[2,256,256]{2,1,0:T(8,128)S(1)}, f32[2,256,256]{2,1,0:T(8,128)S(1)}, u32[]{:S(2)}, u32[]{:S(2)}) %collective-permute-start.18) | collective-permute-done | bytes 524320 | tf_op jit(solution)/shard_map/ppermute | solution.py:36
  173.4 2.9 %shard_map.92 = (f32[2,2,256,256]{3,2,1,0:T(8,128)S(1)}, f32[2,2,256,256]{3,2,1,0:T(8,128)S(1)}, f32[2,2,256,256]{3,2,1,0:T(8,128)S(1)}) custom-call(s32[2,2,2]{2,1,0:T(2,128)S(1)} %bitcast.17, s32[2]{0:T(128)S(1)} %bitcast.23, f32[2,2,256,256]{3,2,1,0:T(8,128)S(1)} %shard_map.91.refs_2_, f32[2,2,2,256,128]{4,3,2,1,0:T(8,128)S(1)} %get-tuple-element.37.refs_3_, ...), custom_call_target="tpu_custom_call" | custom-call | flops 4000000000 | bytes 8388608 | tf_op jit(solution)/shard_map/pallas_call | solution.py:312
  176.3 1.9 collective-permute-start.21
  178.2 2.3 shard_map.93
  180.6 4.4 %collective-permute-start.20 = (f32[2,2,256,256]{3,2,1,0:T(8,128)S(1)}, f32[2,2,256,256]{3,2,1,0:T(8,128)S(1)}, u32[]{:S(2)}, u32[]{:S(2)}) collective-permute-start(f32[2,2,256,256]{3,2,1,0:T(8,128)S(1)} %get-tuple-element.57), channel_id=1, source_target_pairs={{0,1},{1,2},{2,3},{3,4},{4,5},{5,6},{6,7},{7,8},{8,9},{9,10},{10,1... | collective-permute-start | bytes 3145736 | tf_op jit(solution)/shard_map/ppermute | solution.py:36
  184.9 5.0 %collective-permute-done.21.came = f32[2,2,256,256]{3,2,1,0:T(8,128)S(1)} collective-permute-done((f32[2,2,256,256]{3,2,1,0:T(8,128)S(1)}, f32[2,2,256,256]{3,2,1,0:T(8,128)S(1)}, u32[]{:S(2)}, u32[]{:S(2)}) %collective-permute-start.21) | collective-permute-done | bytes 1048608 | tf_op jit(solution)/shard_map/ppermute | solution.py:36
  189.9 0.1 shard_map.95
  190.1 3.6 %collective-permute-start.23 = (f32[256,256]{1,0:T(8,128)S(1)}, f32[256,256]{1,0:T(8,128)S(1)}, u32[]{:S(2)}, u32[]{:S(2)}) collective-permute-start(f32[256,256]{1,0:T(8,128)S(1)} %get-tuple-element.63), channel_id=1, source_target_pairs={{0,34},{1,35},{2,48},{3,49},{4,38},{5,39},{6,52},{7,53},{8,42},{9,... | collective-permute-start | bytes 786440 | tf_op jit(solution)/shard_map/ppermute | solution.py:47
  193.7 11.0 %collective-permute-done.20.came = f32[2,2,256,256]{3,2,1,0:T(8,128)S(1)} collective-permute-done((f32[2,2,256,256]{3,2,1,0:T(8,128)S(1)}, f32[2,2,256,256]{3,2,1,0:T(8,128)S(1)}, u32[]{:S(2)}, u32[]{:S(2)}) %collective-permute-start.20) | collective-permute-done | bytes 1048608 | tf_op jit(solution)/shard_map/ppermute | solution.py:36
  204.7 0.1 shard_map.94
  204.8 1.9 collective-permute-start.25
  206.7 1.9 collective-permute-start.22
  208.7 32.0 %collective-permute-done.23 = f32[256,256]{1,0:T(8,128)S(1)} collective-permute-done((f32[256,256]{1,0:T(8,128)S(1)}, f32[256,256]{1,0:T(8,128)S(1)}, u32[]{:S(2)}, u32[]{:S(2)}) %collective-permute-start.23) | collective-permute-done | bytes 262176 | tf_op jit(solution)/shard_map/ppermute | solution.py:47
  240.7 1.9 collective-permute-start.24
  242.6 7.9 %collective-permute-done.24.far2 = f32[256,256]{1,0:T(8,128)S(1)} collective-permute-done((f32[256,256]{1,0:T(8,128)S(1)}, f32[256,256]{1,0:T(8,128)S(1)}, u32[]{:S(2)}, u32[]{:S(2)}) %collective-permute-start.24) | collective-permute-done | bytes 262176 | tf_op jit(solution)/shard_map/ppermute | solution.py:47
  250.5 1.2 shard_map.96
  (21 shorter events, 0.1 us)
Async XLA Ops:
  0.0 57.0 %copy-start.6 = (bf16[2,256,256]{2,1,0:T(8,128)(2,1)S(1)}, bf16[2,256,256]{2,1,0:T(8,128)(2,1)}, u32[]{:S(2)}) copy-start(bf16[2,256,256]{2,1,0:T(8,128)(2,1)} %constant.5.clone.perm_ref) | copy-start | bytes 786436
  0.0 9.3 %copy-start.7 = (f32[2,2,256,256]{3,2,1,0:T(8,128)S(1)}, f32[2,2,256,256]{3,2,1,0:T(8,128)}, u32[]{:S(2)}) copy-start(f32[2,2,256,256]{3,2,1,0:T(8,128)} %param.8) | copy-start | bytes 3145732
  0.0 57.0 %copy-start = (f32[2,1,1,2,256,256]{5,4,3,2,1,0:T(8,128)S(1)}, f32[2,1,1,2,256,256]{5,4,3,2,1,0:T(8,128)}, u32[]{:S(2)}) copy-start(f32[2,1,1,2,256,256]{5,4,3,2,1,0:T(8,128)} %param.13) | copy-start | bytes 3145732
  0.0 57.0 %copy-start.3 = (s32[2,1,1,2,2]{4,3,2,1,0:T(2,128)S(1)}, s32[2,1,1,2,2]{4,3,2,1,0:T(2,128)}, u32[]{:S(2)}) copy-start(s32[2,1,1,2,2]{4,3,2,1,0:T(2,128)} %param.11) | copy-start | bytes 100
  0.0 57.0 %copy-start.2 = (f32[256,256]{1,0:T(8,128)S(1)}, f32[256,256]{1,0:T(8,128)}, u32[]{:S(2)}) copy-start(f32[256,256]{1,0:T(8,128)} %angle_ref.1) | copy-start | bytes 786436
  0.0 57.0 %copy-start.1 = (f32[2,256,256]{2,1,0:T(8,128)S(1)}, f32[2,256,256]{2,1,0:T(8,128)}, u32[]{:S(2)}) copy-start(f32[2,256,256]{2,1,0:T(8,128)} %probe_ref.1) | copy-start | bytes 1572868
  1.5 35.2 %collective-permute-start.1 = (f32[2,256,256]{2,1,0:T(8,128)S(1)}, f32[2,256,256]{2,1,0:T(8,128)S(1)}, u32[]{:S(2)}, u32[]{:S(2)}) collective-permute-start(f32[2,256,256]{2,1,0:T(8,128)S(1)} %get-tuple-element.68.refs_5_.old), channel_id=1, source_target_pairs={{16,0},{32,16},{48,32},{64,48},{80,64},{96,80},{112,96},{128,112},... | collective-permute-start | bytes 1572872 | tf_op jit(solution)/shard_map/ppermute | solution.py:36
  9.4 22.9 %collective-permute-start.5 = (f32[256,256]{1,0:T(8,128)S(1)}, f32[256,256]{1,0:T(8,128)S(1)}, u32[]{:S(2)}, u32[]{:S(2)}) collective-permute-start(f32[256,256]{1,0:T(8,128)S(1)} %get-tuple-element.65), channel_id=1, source_target_pairs={{16,34},{17,35},{18,48},{19,49},{20,38},{21,39},{22,52},{23,53},{2... | collective-permute-start | bytes 786440 | tf_op jit(solution)/shard_map/ppermute | solution.py:47
  11.3 29.5 %collective-permute-start.4 = (f32[256,256]{1,0:T(8,128)S(1)}, f32[256,256]{1,0:T(8,128)S(1)}, u32[]{:S(2)}, u32[]{:S(2)}) collective-permute-start(f32[256,256]{1,0:T(8,128)S(1)} %get-tuple-element.66), channel_id=1, source_target_pairs={{16,0},{32,16},{48,32},{64,48},{80,64},{96,80},{112,96},{128,112},... | collective-permute-start | bytes 786440 | tf_op jit(solution)/shard_map/ppermute | solution.py:36
  32.3 21.5 %collective-permute-start.6 = (f32[256,256]{1,0:T(8,128)S(1)}, f32[256,256]{1,0:T(8,128)S(1)}, u32[]{:S(2)}, u32[]{:S(2)}) collective-permute-start(f32[256,256]{1,0:T(8,128)S(1)} %collective-permute-done.5), channel_id=1, source_target_pairs={{0,18},{1,19},{2,32},{3,33},{4,22},{5,23},{6,36},{7,37},{8,26},{9,... | collective-permute-start | bytes 786440 | tf_op jit(solution)/shard_map/ppermute | solution.py:47
  34.2 28.0 %collective-permute-start = (f32[2,256,256]{2,1,0:T(8,128)S(1)}, f32[2,256,256]{2,1,0:T(8,128)S(1)}, u32[]{:S(2)}, u32[]{:S(2)}) collective-permute-start(f32[2,256,256]{2,1,0:T(8,128)S(1)} %get-tuple-element.68.refs_5_.old), channel_id=1, source_target_pairs={{1,0},{2,1},{3,2},{4,3},{5,4},{6,5},{7,6},{8,7},{9,8},{10,9},{11,1... | collective-permute-start | bytes 1572872 | tf_op jit(solution)/shard_map/ppermute | solution.py:36
  36.7 25.5 %collective-permute-start.2 = (f32[2,256,256]{2,1,0:T(8,128)S(1)}, f32[2,256,256]{2,1,0:T(8,128)S(1)}, u32[]{:S(2)}, u32[]{:S(2)}) collective-permute-start(f32[2,256,256]{2,1,0:T(8,128)S(1)} %collective-permute-done.1.refs_7_.old_low), channel_id=1, source_target_pairs={{1,0},{2,1},{3,2},{4,3},{5,4},{6,5},{7,6},{8,7},{9,8},{10,9},{11,1... | collective-permute-start | bytes 1572872 | tf_op jit(solution)/shard_map/ppermute | solution.py:36
  38.9 24.0 %collective-permute-start.3 = (f32[2,256,256]{2,1,0:T(8,128)S(1)}, f32[2,256,256]{2,1,0:T(8,128)S(1)}, u32[]{:S(2)}, u32[]{:S(2)}) collective-permute-start(f32[2,256,256]{2,1,0:T(8,128)S(1)} %get-tuple-element.67.refs_5_.old), channel_id=1, source_target_pairs={{1,0},{2,1},{3,2},{4,3},{5,4},{6,5},{7,6},{8,7},{9,8},{10,9},{11,1... | collective-permute-start | bytes 1572872 | tf_op jit(solution)/shard_map/ppermute | solution.py:36
  53.8 11.9 %collective-permute-start.7 = (f32[2,256,256]{2,1,0:T(8,128)S(1)}, f32[2,256,256]{2,1,0:T(8,128)S(1)}, u32[]{:S(2)}, u32[]{:S(2)}) collective-permute-start(f32[2,256,256]{2,1,0:T(8,128)S(1)} %shard_map.84.refs_7_.old_low), channel_id=1, source_target_pairs={{1,0},{2,1},{3,2},{4,3},{5,4},{6,5},{7,6},{8,7},{9,8},{10,9},{11,1... | collective-permute-start | bytes 1572872 | tf_op jit(solution)/shard_map/ppermute | solution.py:36
  57.1 5.2 %copy-start.4 = (s32[2,1,1]{0,2,1:T(1,128)S(1)}, s32[2,1,1]{0,2,1:T(1,128)}, u32[]{:S(2)}) copy-start(s32[2,1,1]{0,2,1:T(1,128)} %param.12) | copy-start | bytes 28
  57.1 5.2 %copy-start.5 = (bf16[2,2,2,256,256]{4,3,2,1,0:T(8,128)(2,1)S(1)}, bf16[2,2,2,256,256]{4,3,2,1,0:T(8,128)(2,1)}, u32[]{:S(2)}) copy-start(bf16[2,2,2,256,256]{4,3,2,1,0:T(8,128)(2,1)} %constant.4.clone.refs_4_.refs_5_) | copy-start | bytes 3145732
  67.2 26.6 %collective-permute-start.8 = (f32[2,256,256]{2,1,0:T(8,128)S(1)}, f32[2,256,256]{2,1,0:T(8,128)S(1)}, u32[]{:S(2)}, u32[]{:S(2)}) collective-permute-start(f32[2,256,256]{2,1,0:T(8,128)S(1)} %get-tuple-element.40), channel_id=1, source_target_pairs={{0,1},{1,2},{2,3},{3,4},{4,5},{5,6},{6,7},{7,8},{8,9},{9,10},{10,1... | collective-permute-start | bytes 1572872 | tf_op jit(solution)/shard_map/ppermute | solution.py:36
  69.1 24.9 %collective-permute-start.9 = (f32[2,256,256]{2,1,0:T(8,128)S(1)}, f32[2,256,256]{2,1,0:T(8,128)S(1)}, u32[]{:S(2)}, u32[]{:S(2)}) collective-permute-start(f32[2,256,256]{2,1,0:T(8,128)S(1)} %get-tuple-element.41), channel_id=1, source_target_pairs={{0,1},{1,2},{2,3},{3,20},{4,5},{5,6},{6,7},{7,24},{8,9},{9,10},{10... | collective-permute-start | bytes 1572872 | tf_op jit(solution)/shard_map/ppermute | solution.py:47
  87.9 17.6 %collective-permute-start.12 = (f32[2,256,256]{2,1,0:T(8,128)S(1)}, f32[2,256,256]{2,1,0:T(8,128)S(1)}, u32[]{:S(2)}, u32[]{:S(2)}) collective-permute-start(f32[2,256,256]{2,1,0:T(8,128)S(1)} %get-tuple-element.46), channel_id=1, source_target_pairs={{0,1},{1,2},{2,3},{3,4},{4,5},{5,6},{6,7},{7,8},{8,9},{9,10},{10,1... | collective-permute-start | bytes 1572872 | tf_op jit(solution)/shard_map/ppermute | solution.py:36
  89.8 15.6 %collective-permute-start.13 = (f32[2,256,256]{2,1,0:T(8,128)S(1)}, f32[2,256,256]{2,1,0:T(8,128)S(1)}, u32[]{:S(2)}, u32[]{:S(2)}) collective-permute-start(f32[2,256,256]{2,1,0:T(8,128)S(1)} %get-tuple-element.47), channel_id=1, source_target_pairs={{0,1},{1,2},{2,3},{3,20},{4,5},{5,6},{6,7},{7,24},{8,9},{9,10},{10... | collective-permute-start | bytes 1572872 | tf_op jit(solution)/shard_map/ppermute | solution.py:47
  94.2 22.5 %collective-permute-start.11 = (f32[2,256,256]{2,1,0:T(8,128)S(1)}, f32[2,256,256]{2,1,0:T(8,128)S(1)}, u32[]{:S(2)}, u32[]{:S(2)}) collective-permute-start(f32[2,256,256]{2,1,0:T(8,128)S(1)} %get-tuple-element.42.above), channel_id=1, source_target_pairs={{16,0},{32,16},{48,32},{64,48},{80,64},{96,80},{112,96},{128,112},... | collective-permute-start | bytes 1572872 | tf_op jit(solution)/shard_map/ppermute | solution.py:36
  103.5 21.6 %collective-permute-start.10 = (f32[2,256,256]{2,1,0:T(8,128)S(1)}, f32[2,256,256]{2,1,0:T(8,128)S(1)}, u32[]{:S(2)}, u32[]{:S(2)}) collective-permute-start(f32[2,256,256]{2,1,0:T(8,128)S(1)} %get-tuple-element.43.below), channel_id=1, source_target_pairs={{0,16},{16,32},{32,48},{48,64},{64,80},{80,96},{96,112},{112,128},... | collective-permute-start | bytes 1572872 | tf_op jit(solution)/shard_map/ppermute | solution.py:36
  105.6 40.1 %collective-permute-start.15 = (f32[2,256,256]{2,1,0:T(8,128)S(1)}, f32[2,256,256]{2,1,0:T(8,128)S(1)}, u32[]{:S(2)}, u32[]{:S(2)}) collective-permute-start(f32[2,256,256]{2,1,0:T(8,128)S(1)} %get-tuple-element.48.above), channel_id=1, source_target_pairs={{16,0},{32,16},{48,32},{64,48},{80,64},{96,80},{112,96},{128,112},... | collective-permute-start | bytes 1572872 | tf_op jit(solution)/shard_map/ppermute | solution.py:36
  113.9 43.2 %collective-permute-start.14 = (f32[2,256,256]{2,1,0:T(8,128)S(1)}, f32[2,256,256]{2,1,0:T(8,128)S(1)}, u32[]{:S(2)}, u32[]{:S(2)}) collective-permute-start(f32[2,256,256]{2,1,0:T(8,128)S(1)} %get-tuple-element.49.below), channel_id=1, source_target_pairs={{0,16},{16,32},{32,48},{48,64},{64,80},{80,96},{96,112},{112,128},... | collective-permute-start | bytes 1572872 | tf_op jit(solution)/shard_map/ppermute | solution.py:36
  125.4 36.1 %collective-permute-start.17 = (f32[2,256,256]{2,1,0:T(8,128)S(1)}, f32[2,256,256]{2,1,0:T(8,128)S(1)}, u32[]{:S(2)}, u32[]{:S(2)}) collective-permute-start(f32[2,256,256]{2,1,0:T(8,128)S(1)} %get-tuple-element.52), channel_id=1, source_target_pairs={{1,0},{2,1},{3,2},{5,4},{6,5},{7,6},{9,8},{10,9},{11,10},{13,12},{... | collective-permute-start | bytes 1572872 | tf_op jit(solution)/shard_map/ppermute | solution.py:47
  127.4 34.1 %collective-permute-start.16 = (f32[2,256,256]{2,1,0:T(8,128)S(1)}, f32[2,256,256]{2,1,0:T(8,128)S(1)}, u32[]{:S(2)}, u32[]{:S(2)}) collective-permute-start(f32[2,256,256]{2,1,0:T(8,128)S(1)} %get-tuple-element.44.refs_5_.one), channel_id=1, source_target_pairs={{1,0},{2,1},{3,2},{4,3},{5,4},{6,5},{7,6},{8,7},{9,8},{10,9},{11,1... | collective-permute-start | bytes 1572872 | tf_op jit(solution)/shard_map/ppermute | solution.py:36
  157.3 10.5 %collective-permute-start.19 = (f32[2,256,256]{2,1,0:T(8,128)S(1)}, f32[2,256,256]{2,1,0:T(8,128)S(1)}, u32[]{:S(2)}, u32[]{:S(2)}) collective-permute-start(f32[2,256,256]{2,1,0:T(8,128)S(1)} %get-tuple-element.54), channel_id=1, source_target_pairs={{1,0},{2,1},{3,2},{5,4},{6,5},{7,6},{9,8},{10,9},{11,10},{13,12},{... | collective-permute-start | bytes 1572872 | tf_op jit(solution)/shard_map/ppermute | solution.py:47
  159.6 13.8 %collective-permute-start.18 = (f32[2,256,256]{2,1,0:T(8,128)S(1)}, f32[2,256,256]{2,1,0:T(8,128)S(1)}, u32[]{:S(2)}, u32[]{:S(2)}) collective-permute-start(f32[2,256,256]{2,1,0:T(8,128)S(1)} %get-tuple-element.50.refs_5_.two), channel_id=1, source_target_pairs={{1,0},{2,1},{3,2},{4,3},{5,4},{6,5},{7,6},{8,7},{9,8},{10,9},{11,1... | collective-permute-start | bytes 1572872 | tf_op jit(solution)/shard_map/ppermute | solution.py:36
  176.3 13.7 %collective-permute-start.21 = (f32[2,2,256,256]{3,2,1,0:T(8,128)S(1)}, f32[2,2,256,256]{3,2,1,0:T(8,128)S(1)}, u32[]{:S(2)}, u32[]{:S(2)}) collective-permute-start(f32[2,2,256,256]{3,2,1,0:T(8,128)S(1)} %get-tuple-element.60), channel_id=1, source_target_pairs={{0,1},{1,2},{2,3},{3,4},{4,5},{5,6},{6,7},{7,8},{8,9},{9,10},{10,1... | collective-permute-start | bytes 3145736 | tf_op jit(solution)/shard_map/ppermute | solution.py:36
  180.6 24.1 %collective-permute-start.20 = (f32[2,2,256,256]{3,2,1,0:T(8,128)S(1)}, f32[2,2,256,256]{3,2,1,0:T(8,128)S(1)}, u32[]{:S(2)}, u32[]{:S(2)}) collective-permute-start(f32[2,2,256,256]{3,2,1,0:T(8,128)S(1)} %get-tuple-element.57), channel_id=1, source_target_pairs={{0,1},{1,2},{2,3},{3,4},{4,5},{5,6},{6,7},{7,8},{8,9},{9,10},{10,1... | collective-permute-start | bytes 3145736 | tf_op jit(solution)/shard_map/ppermute | solution.py:36
  190.1 50.6 %collective-permute-start.23 = (f32[256,256]{1,0:T(8,128)S(1)}, f32[256,256]{1,0:T(8,128)S(1)}, u32[]{:S(2)}, u32[]{:S(2)}) collective-permute-start(f32[256,256]{1,0:T(8,128)S(1)} %get-tuple-element.63), channel_id=1, source_target_pairs={{0,34},{1,35},{2,48},{3,49},{4,38},{5,39},{6,52},{7,53},{8,42},{9,... | collective-permute-start | bytes 786440 | tf_op jit(solution)/shard_map/ppermute | solution.py:47
  204.8 37.8 %collective-permute-start.25 = (f32[2,256,256]{2,1,0:T(8,128)S(1)}, f32[2,256,256]{2,1,0:T(8,128)S(1)}, u32[]{:S(2)}, u32[]{:S(2)}) collective-permute-start(f32[2,256,256]{2,1,0:T(8,128)S(1)} %get-tuple-element.64), channel_id=1, source_target_pairs={{0,16},{16,32},{32,48},{48,64},{64,80},{80,96},{96,112},{112,128},... | collective-permute-start | bytes 1572872 | tf_op jit(solution)/shard_map/ppermute | solution.py:36
  206.7 35.9 %collective-permute-start.22 = (f32[256,256]{1,0:T(8,128)S(1)}, f32[256,256]{1,0:T(8,128)S(1)}, u32[]{:S(2)}, u32[]{:S(2)}) collective-permute-start(f32[256,256]{1,0:T(8,128)S(1)} %get-tuple-element.62), channel_id=1, source_target_pairs={{0,16},{16,32},{32,48},{48,64},{64,80},{80,96},{96,112},{112,128},... | collective-permute-start | bytes 786440 | tf_op jit(solution)/shard_map/ppermute | solution.py:36
  240.7 9.8 %collective-permute-start.24 = (f32[256,256]{1,0:T(8,128)S(1)}, f32[256,256]{1,0:T(8,128)S(1)}, u32[]{:S(2)}, u32[]{:S(2)}) collective-permute-start(f32[256,256]{1,0:T(8,128)S(1)} %collective-permute-done.23), channel_id=1, source_target_pairs={{0,34},{1,35},{2,48},{3,49},{4,38},{5,39},{6,52},{7,53},{8,42},{9,... | collective-permute-start | bytes 786440 | tf_op jit(solution)/shard_map/ppermute | solution.py:47

commit v5 on v4

--- a/solution.py
+++ b/solution.py
@@ -261,9 +261,15 @@
     return lax.rem(lax.axis_index("tx"), 4) == 0
 
 
-def join_kernel(near, far, both):
-    both[0] = near[...]
-    both[1] = far[...]
+def join_kernel(near, far, own, both, send):
+    for plane, part in enumerate((near, far)):
+        both[plane] = part[...]
+        send[plane] = jnp.where(leading(), own[plane], part[...])
+
+
+def choose_kernel(own, low, send):
+    for plane in range(2):
+        send[plane] = jnp.where(leading(), own[plane], low[plane])
 
 
 def sums_kernel(stay, side, diag, above, below):
@@ -338,9 +344,10 @@
     far = around(object_tiles[1, 1], -1, sizes)
     rgt = [shifted(own[s], "tx", -1) for s in (0, 1)]
     near = shifted(object_tiles[1, 0], "ty", -1)
-    (low1,) = call(join_kernel, [], [near, far], [f32(2, SIDE, SIDE)], flops=10**6)
+    (send0,) = call(choose_kernel, [], [own[0], low0], [f32(2, SIDE, SIDE)], flops=10**6)
+    low1, send1 = call(join_kernel, [], [near, far, own[1]], [f32(2, SIDE, SIDE)] * 2, flops=10**6)
     low = [low0, low1]
-    dia = [shifted(low[s], "tx", -1) for s in (0, 1)]
+    dia = [moved(send, diagonal_back, sizes) for send in (send0, send1)]
 
     rolled, prop, ampl = call(
         prepare_kernel, [offsets],

time: 253 us -> 248 us (0.980)
  the two profiles are of different devices: /device:TPU:17 before, /device:TPU:10 now
where the time goes in v5:
time: 248 us; the launch traced here: 247 us
  waiting for transfers between devices  129 us (52%)
  starting transfers between devices  88.9 us (36%)
  Pallas kernels  27.1 us (11%)
    ppermute x16, waiting for transfers between devices, shifted(): lax.ppermute(value, axis, [(source, source + steps) for source in range(f...  93.8 us
    ppermute x16, starting transfers between devices, shifted(): lax.ppermute(value, axis, [(source, source + steps) for source in range(f...  57.4 us
    ppermute x10, waiting for transfers between devices, moved(): return lax.ppermute(value, ('ty', 'tx'), pairs)  35 us
    ppermute x10, starting transfers between devices, moved(): return lax.ppermute(value, ('ty', 'tx'), pairs)  31.5 us
    pallas_call x16, Pallas kernels, call(): pl.pallas_call(body, out_shape=outs, in_specs=[SMEM] * len(scalars) + [VM...  27.1 us
  transfers between devices with their start and end apart: 26, of which 14 were waited for; matrix products, arithmetic and copies ran while one was open for 0% of the time, Pallas kernels for 6%

profile of v5, /device:TPU:10, one launch (start us, length us, event | category | flops | bytes accessed | tf_op | source)
XLA Modules:
  0.0 246.7 jit_solution(4824295544991292071)
XLA Ops:
  0.0 1.4 slice_bitcast_fusion
  1.4 0.0 copy-start
  1.4 0.0 copy-start.1
  1.4 0.0 copy-start.2
  1.4 0.0 copy-start.3
  1.4 0.0 copy-start.6
  1.4 8.2 %collective-permute-start.1 = (f32[2,256,256]{2,1,0:T(8,128)S(1)}, f32[2,256,256]{2,1,0:T(8,128)S(1)}, u32[]{:S(2)}, u32[]{:S(2)}) collective-permute-start(f32[2,256,256]{2,1,0:T(8,128)S(1)} %get-tuple-element.72.own.refs_5_.old), channel_id=1, source_target_pairs={{16,0},{32,16},{48,32},{64,48},{80,64},{96,80},{112,96},{128,112},... | collective-permute-start | bytes 1572872 | tf_op jit(solution)/shard_map/ppermute | solution.py:36
  9.7 1.9 collective-permute-start.5
  11.7 3.4 %collective-permute-start.4 = (f32[256,256]{1,0:T(8,128)S(1)}, f32[256,256]{1,0:T(8,128)S(1)}, u32[]{:S(2)}, u32[]{:S(2)}) collective-permute-start(f32[256,256]{1,0:T(8,128)S(1)} %get-tuple-element.70), channel_id=1, source_target_pairs={{16,0},{32,16},{48,32},{64,48},{80,64},{96,80},{112,96},{128,112},... | collective-permute-start | bytes 786440 | tf_op jit(solution)/shard_map/ppermute | solution.py:36
  15.0 17.3 %collective-permute-done.5 = f32[256,256]{1,0:T(8,128)S(1)} collective-permute-done((f32[256,256]{1,0:T(8,128)S(1)}, f32[256,256]{1,0:T(8,128)S(1)}, u32[]{:S(2)}, u32[]{:S(2)}) %collective-permute-start.5) | collective-permute-done | bytes 262176 | tf_op jit(solution)/shard_map/ppermute | solution.py:47
  32.3 1.9 collective-permute-start.6
  34.2 4.3 %collective-permute-start = (f32[2,256,256]{2,1,0:T(8,128)S(1)}, f32[2,256,256]{2,1,0:T(8,128)S(1)}, u32[]{:S(2)}, u32[]{:S(2)}) collective-permute-start(f32[2,256,256]{2,1,0:T(8,128)S(1)} %get-tuple-element.72.own.refs_5_.old), channel_id=1, source_target_pairs={{1,0},{2,1},{3,2},{4,3},{5,4},{6,5},{7,6},{8,7},{9,8},{10,9},{11,1... | collective-permute-start | bytes 1572872 | tf_op jit(solution)/shard_map/ppermute | solution.py:36
  38.5 0.1 shard_map.83
  38.6 2.4 collective-permute-start.2
  41.0 2.2 collective-permute-start.3
  43.2 2.2 collective-permute-done.4.near
  45.4 9.4 %collective-permute-done.6.far = f32[256,256]{1,0:T(8,128)S(1)} collective-permute-done((f32[256,256]{1,0:T(8,128)S(1)}, f32[256,256]{1,0:T(8,128)S(1)}, u32[]{:S(2)}, u32[]{:S(2)}) %collective-permute-start.6) | collective-permute-done | bytes 262176 | tf_op jit(solution)/shard_map/ppermute | solution.py:47
  54.9 0.1 shard_map.85
  54.9 1.9 collective-permute-start.7
  56.9 0.0 copy-start.4
  56.9 0.0 copy-start.5
  56.9 5.2 %shard_map.82 = (f32[2,2,2,256,256]{4,3,2,1,0:T(8,128)S(1)}, f32[2,2,256,128]{3,2,1,0:T(8,128)S(1)}, f32[2,2,2,256,128]{4,3,2,1,0:T(8,128)S(1)}) custom-call(s32[2,2,2]{2,1,0:T(2,128)S(1)} %bitcast.12, f32[2,256,256]{2,1,0:T(8,128)S(1)} %copy-done.1, f32[256,256]{1,0:T(8,128)S(1)} %copy-done.2, f32[2,2,256,256]{3,2,1,0:T(8,128)S(1)} %bitcast.11, ...), custom_call_target="tpu_custom_call" | custom-call | flops 4000000000 | bytes 8388608 | tf_op jit(solution)/shard_map/pallas_call | solution.py:318
  62.2 3.6 %shard_map.84.refs_2_ = f32[2,2,256,256]{3,2,1,0:T(8,128)S(1)} custom-call(s32[2,2,2]{2,1,0:T(2,128)S(1)} %bitcast.13, s32[2]{0:T(128)S(1)} %bitcast.19, f32[2,2,2,256,256]{4,3,2,1,0:T(8,128)S(1)} %get-tuple-element.37.refs_2_.refs_3_, f32[2,2,256,128]{3,2,1,0:T(8,128)S(1)} %get-tuple-element.38.refs_3_.refs_4_, bf16[2,2,2,256,256]{4,3,2,1,0:T(8,128)(2,1)S(1)} %copy-done.5, ...), custom_call_target="tpu_custom_call" | custom-call | flops 4000000000 | bytes 8388608 | tf_op jit(solution)/shard_map/pallas_call | solution.py:318
  65.8 0.2 collective-permute-done.7.refs_8_
  66.0 4.8 %shard_map.86 = (f32[2,2,256,256]{3,2,1,0:T(8,128)S(1)}, f32[2,256,256]{2,1,0:T(8,128)S(1)}, f32[2,256,256]{2,1,0:T(8,128)S(1)}, f32[2,2,256,256]{3,2,1,0:T(8,128)S(1)}) custom-call(s32[2,2,2]{2,1,0:T(2,128)S(1)} %bitcast.14, s32[2]{0:T(128)S(1)} %bitcast.20, f32[2,2,256,256]{3,2,1,0:T(8,128)S(1)} %shard_map.84.refs_2_, ...), custom_call_target="tpu_custom_call" | custom-call | flops 4000000000 | bytes 8388608 | tf_op jit(solution)/shard_map/pallas_call | solution.py:318
  70.8 3.8 %shard_map.87 = (f32[2,2,256,256]{3,2,1,0:T(8,128)S(1)}, f32[2,256,256]{2,1,0:T(8,128)S(1)}, f32[2,256,256]{2,1,0:T(8,128)S(1)}) custom-call(s32[2,2,2]{2,1,0:T(2,128)S(1)} %bitcast.15, s32[2]{0:T(128)S(1)} %bitcast.21, f32[2,2,256,256]{3,2,1,0:T(8,128)S(1)} %get-tuple-element.42.refs_2_, f32[2,2,2,256,256]{4,3,2,1,0:T(8,128)S(1)} %get-tuple-element.37.refs_2_.refs_3_, ...), custom_call_target="tpu_custom_call" | custom-call | flops 4000000000 | bytes 8388608 | tf_op jit(solution)/shard_map/pallas_call | solution.py:318
  74.7 1.9 collective-permute-start.8
  76.6 5.0 %collective-permute-start.9 = (f32[2,256,256]{2,1,0:T(8,128)S(1)}, f32[2,256,256]{2,1,0:T(8,128)S(1)}, u32[]{:S(2)}, u32[]{:S(2)}) collective-permute-start(f32[2,256,256]{2,1,0:T(8,128)S(1)} %get-tuple-element.45), channel_id=1, source_target_pairs={{0,1},{1,2},{2,3},{3,20},{4,5},{5,6},{6,7},{7,24},{8,9},{9,10},{10... | collective-permute-start | bytes 1572872 | tf_op jit(solution)/shard_map/ppermute | solution.py:47
  81.6 1.9 collective-permute-start.12
  83.6 2.2 collective-permute-start.13
  85.8 1.8 collective-permute-done.8.side
  87.6 5.7 %collective-permute-done.9.diag = f32[2,256,256]{2,1,0:T(8,128)S(1)} collective-permute-done((f32[2,256,256]{2,1,0:T(8,128)S(1)}, f32[2,256,256]{2,1,0:T(8,128)S(1)}, u32[]{:S(2)}, u32[]{:S(2)}) %collective-permute-start.9) | collective-permute-done | bytes 524320 | tf_op jit(solution)/shard_map/ppermute | solution.py:47
  93.4 0.1 shard_map.88
  93.5 1.9 collective-permute-start.11
  95.5 6.1 %collective-permute-start.10 = (f32[2,256,256]{2,1,0:T(8,128)S(1)}, f32[2,256,256]{2,1,0:T(8,128)S(1)}, u32[]{:S(2)}, u32[]{:S(2)}) collective-permute-start(f32[2,256,256]{2,1,0:T(8,128)S(1)} %get-tuple-element.47.below), channel_id=1, source_target_pairs={{0,16},{16,32},{32,48},{48,64},{64,80},{80,96},{96,112},{112,128},... | collective-permute-start | bytes 1572872 | tf_op jit(solution)/shard_map/ppermute | solution.py:36
  101.5 19.2 %collective-permute-done.12.side = f32[2,256,256]{2,1,0:T(8,128)S(1)} collective-permute-done((f32[2,256,256]{2,1,0:T(8,128)S(1)}, f32[2,256,256]{2,1,0:T(8,128)S(1)}, u32[]{:S(2)}, u32[]{:S(2)}) %collective-permute-start.12) | collective-permute-done | bytes 524320 | tf_op jit(solution)/shard_map/ppermute | solution.py:36
  120.7 0.1 shard_map.90
  120.9 1.9 collective-permute-start.15
  122.8 7.4 %collective-permute-start.14 = (f32[2,256,256]{2,1,0:T(8,128)S(1)}, f32[2,256,256]{2,1,0:T(8,128)S(1)}, u32[]{:S(2)}, u32[]{:S(2)}) collective-permute-start(f32[2,256,256]{2,1,0:T(8,128)S(1)} %get-tuple-element.53.below), channel_id=1, source_target_pairs={{0,16},{16,32},{32,48},{48,64},{64,80},{80,96},{96,112},{112,128},... | collective-permute-start | bytes 1572872 | tf_op jit(solution)/shard_map/ppermute | solution.py:36
  130.3 0.5 collective-permute-done.10.from_above
  130.8 0.3 shard_map.89
  131.1 4.6 %collective-permute-start.17 = (f32[2,256,256]{2,1,0:T(8,128)S(1)}, f32[2,256,256]{2,1,0:T(8,128)S(1)}, u32[]{:S(2)}, u32[]{:S(2)}) collective-permute-start(f32[2,256,256]{2,1,0:T(8,128)S(1)} %get-tuple-element.56), channel_id=1, source_target_pairs={{1,0},{2,1},{3,2},{5,4},{6,5},{7,6},{9,8},{10,9},{11,10},{13,12},{... | collective-permute-start | bytes 1572872 | tf_op jit(solution)/shard_map/ppermute | solution.py:47
  135.7 5.7 %collective-permute-start.16 = (f32[2,256,256]{2,1,0:T(8,128)S(1)}, f32[2,256,256]{2,1,0:T(8,128)S(1)}, u32[]{:S(2)}, u32[]{:S(2)}) collective-permute-start(f32[2,256,256]{2,1,0:T(8,128)S(1)} %get-tuple-element.48.refs_5_.one), channel_id=1, source_target_pairs={{1,0},{2,1},{3,2},{4,3},{5,4},{6,5},{7,6},{8,7},{9,8},{10,9},{11,1... | collective-permute-start | bytes 1572872 | tf_op jit(solution)/shard_map/ppermute | solution.py:36
  141.3 6.7 %collective-permute-done.15.from_below = f32[2,256,256]{2,1,0:T(8,128)S(1)} collective-permute-done((f32[2,256,256]{2,1,0:T(8,128)S(1)}, f32[2,256,256]{2,1,0:T(8,128)S(1)}, u32[]{:S(2)}, u32[]{:S(2)}) %collective-permute-start.15) | collective-permute-done | bytes 524320 | tf_op jit(solution)/shard_map/ppermute | solution.py:36
  148.0 0.3 shard_map.91
  148.3 7.7 %collective-permute-start.19 = (f32[2,256,256]{2,1,0:T(8,128)S(1)}, f32[2,256,256]{2,1,0:T(8,128)S(1)}, u32[]{:S(2)}, u32[]{:S(2)}) collective-permute-start(f32[2,256,256]{2,1,0:T(8,128)S(1)} %get-tuple-element.58), channel_id=1, source_target_pairs={{1,0},{2,1},{3,2},{5,4},{6,5},{7,6},{9,8},{10,9},{11,10},{13,12},{... | collective-permute-start | bytes 1572872 | tf_op jit(solution)/shard_map/ppermute | solution.py:47
  156.0 4.7 %collective-permute-start.18 = (f32[2,256,256]{2,1,0:T(8,128)S(1)}, f32[2,256,256]{2,1,0:T(8,128)S(1)}, u32[]{:S(2)}, u32[]{:S(2)}) collective-permute-start(f32[2,256,256]{2,1,0:T(8,128)S(1)} %get-tuple-element.54.refs_5_.two), channel_id=1, source_target_pairs={{1,0},{2,1},{3,2},{4,3},{5,4},{6,5},{7,6},{8,7},{9,8},{10,9},{11,1... | collective-permute-start | bytes 1572872 | tf_op jit(solution)/shard_map/ppermute | solution.py:36
  160.8 2.1 shard_map.92.refs_2_
  162.8 2.3 collective-permute-done.19.refs_8_
  165.1 5.0 %collective-permute-done.18.refs_6_ = f32[2,256,256]{2,1,0:T(8,128)S(1)} collective-permute-done((f32[2,256,256]{2,1,0:T(8,128)S(1)}, f32[2,256,256]{2,1,0:T(8,128)S(1)}, u32[]{:S(2)}, u32[]{:S(2)}) %collective-permute-start.18) | collective-permute-done | bytes 524320 | tf_op jit(solution)/shard_map/ppermute | solution.py:36
  170.2 2.9 %shard_map.93 = (f32[2,2,256,256]{3,2,1,0:T(8,128)S(1)}, f32[2,2,256,256]{3,2,1,0:T(8,128)S(1)}, f32[2,2,256,256]{3,2,1,0:T(8,128)S(1)}) custom-call(s32[2,2,2]{2,1,0:T(2,128)S(1)} %bitcast.17, s32[2]{0:T(128)S(1)} %bitcast.23, f32[2,2,256,256]{3,2,1,0:T(8,128)S(1)} %shard_map.92.refs_2_, f32[2,2,2,256,128]{4,3,2,1,0:T(8,128)S(1)} %get-tuple-element.39.refs_3_, ...), custom_call_target="tpu_custom_call" | custom-call | flops 4000000000 | bytes 8388608 | tf_op jit(solution)/shard_map/pallas_call | solution.py:318
  173.0 1.9 collective-permute-start.21
  175.0 2.3 shard_map.94
  177.3 1.9 collective-permute-start.20
  179.2 22.0 %collective-permute-done.21.came = f32[2,2,256,256]{3,2,1,0:T(8,128)S(1)} collective-permute-done((f32[2,2,256,256]{3,2,1,0:T(8,128)S(1)}, f32[2,2,256,256]{3,2,1,0:T(8,128)S(1)}, u32[]{:S(2)}, u32[]{:S(2)}) %collective-permute-start.21) | collective-permute-done | bytes 1048608 | tf_op jit(solution)/shard_map/ppermute | solution.py:36
  201.2 0.1 shard_map.96
  201.4 1.9 collective-permute-start.23
  203.3 20.9 %collective-permute-done.20.came = f32[2,2,256,256]{3,2,1,0:T(8,128)S(1)} collective-permute-done((f32[2,2,256,256]{3,2,1,0:T(8,128)S(1)}, f32[2,2,256,256]{3,2,1,0:T(8,128)S(1)}, u32[]{:S(2)}, u32[]{:S(2)}) %collective-permute-start.20) | collective-permute-done | bytes 1048608 | tf_op jit(solution)/shard_map/ppermute | solution.py:36
  224.2 0.1 shard_map.95
  224.4 1.9 collective-permute-start.25
  226.3 1.9 collective-permute-start.22
  228.2 1.9 collective-permute-start.24
  230.2 15.4 %collective-permute-done.22.near2 = f32[256,256]{1,0:T(8,128)S(1)} collective-permute-done((f32[256,256]{1,0:T(8,128)S(1)}, f32[256,256]{1,0:T(8,128)S(1)}, u32[]{:S(2)}, u32[]{:S(2)}) %collective-permute-start.22) | collective-permute-done | bytes 262176 | tf_op jit(solution)/shard_map/ppermute | solution.py:36
  245.5 1.2 shard_map.97
  (22 shorter events, 0.1 us)
Async XLA Ops:
  0.0 9.7 %copy-start.7 = (f32[2,2,256,256]{3,2,1,0:T(8,128)S(1)}, f32[2,2,256,256]{3,2,1,0:T(8,128)}, u32[]{:S(2)}) copy-start(f32[2,2,256,256]{3,2,1,0:T(8,128)} %param.8) | copy-start | bytes 3145732
  1.4 55.5 %copy-start = (f32[2,1,1,2,256,256]{5,4,3,2,1,0:T(8,128)S(1)}, f32[2,1,1,2,256,256]{5,4,3,2,1,0:T(8,128)}, u32[]{:S(2)}) copy-start(f32[2,1,1,2,256,256]{5,4,3,2,1,0:T(8,128)} %param.13) | copy-start | bytes 3145732
  1.4 55.5 %copy-start.1 = (f32[2,256,256]{2,1,0:T(8,128)S(1)}, f32[2,256,256]{2,1,0:T(8,128)}, u32[]{:S(2)}) copy-start(f32[2,256,256]{2,1,0:T(8,128)} %probe_ref.1) | copy-start | bytes 1572868
  1.4 55.5 %copy-start.2 = (f32[256,256]{1,0:T(8,128)S(1)}, f32[256,256]{1,0:T(8,128)}, u32[]{:S(2)}) copy-start(f32[256,256]{1,0:T(8,128)} %angle_ref.1) | copy-start | bytes 786436
  1.4 55.5 %copy-start.3 = (s32[2,1,1,2,2]{4,3,2,1,0:T(2,128)S(1)}, s32[2,1,1,2,2]{4,3,2,1,0:T(2,128)}, u32[]{:S(2)}) copy-start(s32[2,1,1,2,2]{4,3,2,1,0:T(2,128)} %param.11) | copy-start | bytes 100
  1.4 55.5 %copy-start.6 = (bf16[2,256,256]{2,1,0:T(8,128)(2,1)S(1)}, bf16[2,256,256]{2,1,0:T(8,128)(2,1)}, u32[]{:S(2)}) copy-start(bf16[2,256,256]{2,1,0:T(8,128)(2,1)} %constant.5.clone.perm_ref) | copy-start | bytes 786436
  1.4 37.1 %collective-permute-start.1 = (f32[2,256,256]{2,1,0:T(8,128)S(1)}, f32[2,256,256]{2,1,0:T(8,128)S(1)}, u32[]{:S(2)}, u32[]{:S(2)}) collective-permute-start(f32[2,256,256]{2,1,0:T(8,128)S(1)} %get-tuple-element.72.own.refs_5_.old), channel_id=1, source_target_pairs={{16,0},{32,16},{48,32},{64,48},{80,64},{96,80},{112,96},{128,112},... | collective-permute-start | bytes 1572872 | tf_op jit(solution)/shard_map/ppermute | solution.py:36
  9.7 22.5 %collective-permute-start.5 = (f32[256,256]{1,0:T(8,128)S(1)}, f32[256,256]{1,0:T(8,128)S(1)}, u32[]{:S(2)}, u32[]{:S(2)}) collective-permute-start(f32[256,256]{1,0:T(8,128)S(1)} %get-tuple-element.69), channel_id=1, source_target_pairs={{16,34},{17,35},{18,48},{19,49},{20,38},{21,39},{22,52},{23,53},{2... | collective-permute-start | bytes 786440 | tf_op jit(solution)/shard_map/ppermute | solution.py:47
  11.7 33.8 %collective-permute-start.4 = (f32[256,256]{1,0:T(8,128)S(1)}, f32[256,256]{1,0:T(8,128)S(1)}, u32[]{:S(2)}, u32[]{:S(2)}) collective-permute-start(f32[256,256]{1,0:T(8,128)S(1)} %get-tuple-element.70), channel_id=1, source_target_pairs={{16,0},{32,16},{48,32},{64,48},{80,64},{96,80},{112,96},{128,112},... | collective-permute-start | bytes 786440 | tf_op jit(solution)/shard_map/ppermute | solution.py:36
  32.3 22.6 %collective-permute-start.6 = (f32[256,256]{1,0:T(8,128)S(1)}, f32[256,256]{1,0:T(8,128)S(1)}, u32[]{:S(2)}, u32[]{:S(2)}) collective-permute-start(f32[256,256]{1,0:T(8,128)S(1)} %collective-permute-done.5), channel_id=1, source_target_pairs={{0,18},{1,19},{2,32},{3,33},{4,22},{5,23},{6,36},{7,37},{8,26},{9,... | collective-permute-start | bytes 786440 | tf_op jit(solution)/shard_map/ppermute | solution.py:47
  34.2 28.0 %collective-permute-start = (f32[2,256,256]{2,1,0:T(8,128)S(1)}, f32[2,256,256]{2,1,0:T(8,128)S(1)}, u32[]{:S(2)}, u32[]{:S(2)}) collective-permute-start(f32[2,256,256]{2,1,0:T(8,128)S(1)} %get-tuple-element.72.own.refs_5_.old), channel_id=1, source_target_pairs={{1,0},{2,1},{3,2},{4,3},{5,4},{6,5},{7,6},{8,7},{9,8},{10,9},{11,1... | collective-permute-start | bytes 1572872 | tf_op jit(solution)/shard_map/ppermute | solution.py:36
  38.6 23.6 %collective-permute-start.2 = (f32[2,256,256]{2,1,0:T(8,128)S(1)}, f32[2,256,256]{2,1,0:T(8,128)S(1)}, u32[]{:S(2)}, u32[]{:S(2)}) collective-permute-start(f32[2,256,256]{2,1,0:T(8,128)S(1)} %shard_map.83), channel_id=1, source_target_pairs={{1,0},{2,1},{3,2},{5,4},{6,5},{7,6},{9,8},{10,9},{11,10},{13,12},{... | collective-permute-start | bytes 1572872 | tf_op jit(solution)/shard_map/ppermute | solution.py:47
  41.0 24.8 %collective-permute-start.3 = (f32[2,256,256]{2,1,0:T(8,128)S(1)}, f32[2,256,256]{2,1,0:T(8,128)S(1)}, u32[]{:S(2)}, u32[]{:S(2)}) collective-permute-start(f32[2,256,256]{2,1,0:T(8,128)S(1)} %get-tuple-element.71.own.refs_5_.old), channel_id=1, source_target_pairs={{1,0},{2,1},{3,2},{4,3},{5,4},{6,5},{7,6},{8,7},{9,8},{10,9},{11,1... | collective-permute-start | bytes 1572872 | tf_op jit(solution)/shard_map/ppermute | solution.py:36
  54.9 11.1 %collective-permute-start.7 = (f32[2,256,256]{2,1,0:T(8,128)S(1)}, f32[2,256,256]{2,1,0:T(8,128)S(1)}, u32[]{:S(2)}, u32[]{:S(2)}) collective-permute-start(f32[2,256,256]{2,1,0:T(8,128)S(1)} %get-tuple-element.41), channel_id=1, source_target_pairs={{1,0},{2,1},{3,2},{5,4},{6,5},{7,6},{9,8},{10,9},{11,10},{13,12},{... | collective-permute-start | bytes 1572872 | tf_op jit(solution)/shard_map/ppermute | solution.py:47
  56.9 5.3 %copy-start.4 = (s32[2,1,1]{0,2,1:T(1,128)S(1)}, s32[2,1,1]{0,2,1:T(1,128)}, u32[]{:S(2)}) copy-start(s32[2,1,1]{0,2,1:T(1,128)} %param.12) | copy-start | bytes 28
  56.9 5.3 %copy-start.5 = (bf16[2,2,2,256,256]{4,3,2,1,0:T(8,128)(2,1)S(1)}, bf16[2,2,2,256,256]{4,3,2,1,0:T(8,128)(2,1)}, u32[]{:S(2)}) copy-start(bf16[2,2,2,256,256]{4,3,2,1,0:T(8,128)(2,1)} %constant.4.clone.refs_4_.refs_5_) | copy-start | bytes 3145732
  74.7 12.9 %collective-permute-start.8 = (f32[2,256,256]{2,1,0:T(8,128)S(1)}, f32[2,256,256]{2,1,0:T(8,128)S(1)}, u32[]{:S(2)}, u32[]{:S(2)}) collective-permute-start(f32[2,256,256]{2,1,0:T(8,128)S(1)} %get-tuple-element.44), channel_id=1, source_target_pairs={{0,1},{1,2},{2,3},{3,4},{4,5},{5,6},{6,7},{7,8},{8,9},{9,10},{10,1... | collective-permute-start | bytes 1572872 | tf_op jit(solution)/shard_map/ppermute | solution.py:36
  76.6 16.8 %collective-permute-start.9 = (f32[2,256,256]{2,1,0:T(8,128)S(1)}, f32[2,256,256]{2,1,0:T(8,128)S(1)}, u32[]{:S(2)}, u32[]{:S(2)}) collective-permute-start(f32[2,256,256]{2,1,0:T(8,128)S(1)} %get-tuple-element.45), channel_id=1, source_target_pairs={{0,1},{1,2},{2,3},{3,20},{4,5},{5,6},{6,7},{7,24},{8,9},{9,10},{10... | collective-permute-start | bytes 1572872 | tf_op jit(solution)/shard_map/ppermute | solution.py:47
  81.6 39.1 %collective-permute-start.12 = (f32[2,256,256]{2,1,0:T(8,128)S(1)}, f32[2,256,256]{2,1,0:T(8,128)S(1)}, u32[]{:S(2)}, u32[]{:S(2)}) collective-permute-start(f32[2,256,256]{2,1,0:T(8,128)S(1)} %get-tuple-element.50), channel_id=1, source_target_pairs={{0,1},{1,2},{2,3},{3,4},{4,5},{5,6},{6,7},{7,8},{8,9},{9,10},{10,1... | collective-permute-start | bytes 1572872 | tf_op jit(solution)/shard_map/ppermute | solution.py:36
  83.6 37.2 %collective-permute-start.13 = (f32[2,256,256]{2,1,0:T(8,128)S(1)}, f32[2,256,256]{2,1,0:T(8,128)S(1)}, u32[]{:S(2)}, u32[]{:S(2)}) collective-permute-start(f32[2,256,256]{2,1,0:T(8,128)S(1)} %get-tuple-element.51), channel_id=1, source_target_pairs={{0,1},{1,2},{2,3},{3,20},{4,5},{5,6},{6,7},{7,24},{8,9},{9,10},{10... | collective-permute-start | bytes 1572872 | tf_op jit(solution)/shard_map/ppermute | solution.py:47
  93.5 36.7 %collective-permute-start.11 = (f32[2,256,256]{2,1,0:T(8,128)S(1)}, f32[2,256,256]{2,1,0:T(8,128)S(1)}, u32[]{:S(2)}, u32[]{:S(2)}) collective-permute-start(f32[2,256,256]{2,1,0:T(8,128)S(1)} %get-tuple-element.46.above), channel_id=1, source_target_pairs={{16,0},{32,16},{48,32},{64,48},{80,64},{96,80},{112,96},{128,112},... | collective-permute-start | bytes 1572872 | tf_op jit(solution)/shard_map/ppermute | solution.py:36
  95.5 35.4 %collective-permute-start.10 = (f32[2,256,256]{2,1,0:T(8,128)S(1)}, f32[2,256,256]{2,1,0:T(8,128)S(1)}, u32[]{:S(2)}, u32[]{:S(2)}) collective-permute-start(f32[2,256,256]{2,1,0:T(8,128)S(1)} %get-tuple-element.47.below), channel_id=1, source_target_pairs={{0,16},{16,32},{32,48},{48,64},{64,80},{80,96},{96,112},{112,128},... | collective-permute-start | bytes 1572872 | tf_op jit(solution)/shard_map/ppermute | solution.py:36
  120.9 27.1 %collective-permute-start.15 = (f32[2,256,256]{2,1,0:T(8,128)S(1)}, f32[2,256,256]{2,1,0:T(8,128)S(1)}, u32[]{:S(2)}, u32[]{:S(2)}) collective-permute-start(f32[2,256,256]{2,1,0:T(8,128)S(1)} %get-tuple-element.52.above), channel_id=1, source_target_pairs={{16,0},{32,16},{48,32},{64,48},{80,64},{96,80},{112,96},{128,112},... | collective-permute-start | bytes 1572872 | tf_op jit(solution)/shard_map/ppermute | solution.py:36
  122.8 25.2 %collective-permute-start.14 = (f32[2,256,256]{2,1,0:T(8,128)S(1)}, f32[2,256,256]{2,1,0:T(8,128)S(1)}, u32[]{:S(2)}, u32[]{:S(2)}) collective-permute-start(f32[2,256,256]{2,1,0:T(8,128)S(1)} %get-tuple-element.53.below), channel_id=1, source_target_pairs={{0,16},{16,32},{32,48},{48,64},{64,80},{80,96},{96,112},{112,128},... | collective-permute-start | bytes 1572872 | tf_op jit(solution)/shard_map/ppermute | solution.py:36
  131.1 29.7 %collective-permute-start.17 = (f32[2,256,256]{2,1,0:T(8,128)S(1)}, f32[2,256,256]{2,1,0:T(8,128)S(1)}, u32[]{:S(2)}, u32[]{:S(2)}) collective-permute-start(f32[2,256,256]{2,1,0:T(8,128)S(1)} %get-tuple-element.56), channel_id=1, source_target_pairs={{1,0},{2,1},{3,2},{5,4},{6,5},{7,6},{9,8},{10,9},{11,10},{13,12},{... | collective-permute-start | bytes 1572872 | tf_op jit(solution)/shard_map/ppermute | solution.py:47
  135.7 25.1 %collective-permute-start.16 = (f32[2,256,256]{2,1,0:T(8,128)S(1)}, f32[2,256,256]{2,1,0:T(8,128)S(1)}, u32[]{:S(2)}, u32[]{:S(2)}) collective-permute-start(f32[2,256,256]{2,1,0:T(8,128)S(1)} %get-tuple-element.48.refs_5_.one), channel_id=1, source_target_pairs={{1,0},{2,1},{3,2},{4,3},{5,4},{6,5},{7,6},{8,7},{9,8},{10,9},{11,1... | collective-permute-start | bytes 1572872 | tf_op jit(solution)/shard_map/ppermute | solution.py:36
  148.3 16.8 %collective-permute-start.19 = (f32[2,256,256]{2,1,0:T(8,128)S(1)}, f32[2,256,256]{2,1,0:T(8,128)S(1)}, u32[]{:S(2)}, u32[]{:S(2)}) collective-permute-start(f32[2,256,256]{2,1,0:T(8,128)S(1)} %get-tuple-element.58), channel_id=1, source_target_pairs={{1,0},{2,1},{3,2},{5,4},{6,5},{7,6},{9,8},{10,9},{11,10},{13,12},{... | collective-permute-start | bytes 1572872 | tf_op jit(solution)/shard_map/ppermute | solution.py:47
  156.0 14.2 %collective-permute-start.18 = (f32[2,256,256]{2,1,0:T(8,128)S(1)}, f32[2,256,256]{2,1,0:T(8,128)S(1)}, u32[]{:S(2)}, u32[]{:S(2)}) collective-permute-start(f32[2,256,256]{2,1,0:T(8,128)S(1)} %get-tuple-element.54.refs_5_.two), channel_id=1, source_target_pairs={{1,0},{2,1},{3,2},{4,3},{5,4},{6,5},{7,6},{8,7},{9,8},{10,9},{11,1... | collective-permute-start | bytes 1572872 | tf_op jit(solution)/shard_map/ppermute | solution.py:36
  173.0 28.2 %collective-permute-start.21 = (f32[2,2,256,256]{3,2,1,0:T(8,128)S(1)}, f32[2,2,256,256]{3,2,1,0:T(8,128)S(1)}, u32[]{:S(2)}, u32[]{:S(2)}) collective-permute-start(f32[2,2,256,256]{3,2,1,0:T(8,128)S(1)} %get-tuple-element.64), channel_id=1, source_target_pairs={{0,1},{1,2},{2,3},{3,4},{4,5},{5,6},{6,7},{7,8},{8,9},{9,10},{10,1... | collective-permute-start | bytes 3145736 | tf_op jit(solution)/shard_map/ppermute | solution.py:36
  177.3 46.9 %collective-permute-start.20 = (f32[2,2,256,256]{3,2,1,0:T(8,128)S(1)}, f32[2,2,256,256]{3,2,1,0:T(8,128)S(1)}, u32[]{:S(2)}, u32[]{:S(2)}) collective-permute-start(f32[2,2,256,256]{3,2,1,0:T(8,128)S(1)} %get-tuple-element.61), channel_id=1, source_target_pairs={{0,1},{1,2},{2,3},{3,4},{4,5},{5,6},{6,7},{7,8},{8,9},{9,10},{10,1... | collective-permute-start | bytes 3145736 | tf_op jit(solution)/shard_map/ppermute | solution.py:36
  201.4 26.9 %collective-permute-start.23 = (f32[256,256]{1,0:T(8,128)S(1)}, f32[256,256]{1,0:T(8,128)S(1)}, u32[]{:S(2)}, u32[]{:S(2)}) collective-permute-start(f32[256,256]{1,0:T(8,128)S(1)} %get-tuple-element.67), channel_id=1, source_target_pairs={{0,34},{1,35},{2,48},{3,49},{4,38},{5,39},{6,52},{7,53},{8,42},{9,... | collective-permute-start | bytes 786440 | tf_op jit(solution)/shard_map/ppermute | solution.py:47
  224.4 21.2 %collective-permute-start.25 = (f32[2,256,256]{2,1,0:T(8,128)S(1)}, f32[2,256,256]{2,1,0:T(8,128)S(1)}, u32[]{:S(2)}, u32[]{:S(2)}) collective-permute-start(f32[2,256,256]{2,1,0:T(8,128)S(1)} %get-tuple-element.68), channel_id=1, source_target_pairs={{0,16},{16,32},{32,48},{48,64},{64,80},{80,96},{96,112},{112,128},... | collective-permute-start | bytes 1572872 | tf_op jit(solution)/shard_map/ppermute | solution.py:36
  226.3 19.2 %collective-permute-start.22 = (f32[256,256]{1,0:T(8,128)S(1)}, f32[256,256]{1,0:T(8,128)S(1)}, u32[]{:S(2)}, u32[]{:S(2)}) collective-permute-start(f32[256,256]{1,0:T(8,128)S(1)} %get-tuple-element.66), channel_id=1, source_target_pairs={{0,16},{16,32},{32,48},{48,64},{64,80},{80,96},{96,112},{112,128},... | collective-permute-start | bytes 786440 | tf_op jit(solution)/shard_map/ppermute | solution.py:36
  228.2 17.3 %collective-permute-start.24 = (f32[256,256]{1,0:T(8,128)S(1)}, f32[256,256]{1,0:T(8,128)S(1)}, u32[]{:S(2)}, u32[]{:S(2)}) collective-permute-start(f32[256,256]{1,0:T(8,128)S(1)} %collective-permute-done.23), channel_id=1, source_target_pairs={{0,34},{1,35},{2,48},{3,49},{4,38},{5,39},{6,52},{7,53},{8,42},{9,... | collective-permute-start | bytes 786440 | tf_op jit(solution)/shard_map/ppermute | solution.py:47

commit v6 on v5

--- a/solution.py
+++ b/solution.py
@@ -280,13 +280,13 @@
         below[plane] = stay[1, plane] + jnp.where(leading(), zero, extra)
 
 
-def fall_kernel(stay, came, above, *below):
-    above[...] = stay[0] + came[0]
-    if len(below) == 1:
-        below[0][...] = stay[1] + came[1]
-    else:
-        for plane in range(2):
-            below[plane][...] = stay[1, plane] + came[1, plane]
+def fall_kernel(stay, diag, *below):
+    for plane in range(2):
+        total = stay[1, plane] + jnp.where(leading(), jnp.zeros((SIDE, SIDE), jnp.float32), diag[plane])
+        if len(below) == 1:
+            below[0][plane] = total
+        else:
+            below[plane][...] = total
 
 
 def update_kernel(above, below, from_above, from_below, old, old_low, own, low, send):
@@ -298,10 +298,12 @@
         send[plane] = jnp.where(leading(), one, two)
 
 
-def last_kernel(one, two, above1, above2, near2, far2, fallen1, out):
-    out[0] = one[...] - step_size * (above1[...] + fallen1[...])
-    out[1, 0] = two[0] - step_size * (above2[0] + near2[...])
-    out[1, 1] = two[1] - step_size * (above2[1] + far2[...])
+def last_kernel(one, two, stay1, side1, diag1, stay2, side2, diag2, near2, far2, fallen1, out):
+    for s, (old, stay, side, diag) in enumerate(((one, stay1, side1, diag1), (two, stay2, side2, diag2))):
+        for plane in range(2):
+            extra = jnp.where(leading(), diag[plane], jnp.zeros((SIDE, SIDE), jnp.float32))
+            fallen = fallen1[plane] if s == 0 else (near2, far2)[plane][...]
+            out[s, plane] = old[plane] - step_size * (stay[0, plane] + side[plane] + extra + fallen)
 
 
 SMEM = pl.BlockSpec(memory_space=pltpu.SMEM)
@@ -366,28 +368,26 @@
         scalars = [offsets, counts]
         (mid,) = call(bind(first_kernel), scalars, [rolled, prop, tables, *tiles[0]], [pair])
         last = iteration == ITERS - 1
-        moves = [pair] if last else [tile, tile]
+        moves = [tile, tile]
         stay2, *moves2, carry = call(bind(second_kernel), scalars,
                                      [mid, ampl, tables, *tiles[1]], [pair, *moves, pair])
         stay1, *moves1 = call(bind(third_kernel), scalars,
                               [carry, rolled, prop, tables], [pair, *moves])
         stay = [stay1, stay2]
+        side, diag = [moves1[0], moves2[0]], [moves1[1], moves2[1]]
+        for s in (1, 0):
+            diag[s] = moved(diag[s], diagonal_on, sizes)
         if last:
-            came = [None, None]
-            for s in (1, 0):
-                came[s] = shifted([moves1, moves2][s][0], "tx", 1)
-            above2, near, far = call(fall_kernel, [], [stay[1], came[1]],
-                                     [tile, f32(SIDE, SIDE), f32(SIDE, SIDE)], flops=10**6)
-            above1, fallen = call(fall_kernel, [], [stay[0], came[0]], [tile, tile], flops=10**6)
+            near, far = call(fall_kernel, [], [stay[1], diag[1]], [f32(SIDE, SIDE)] * 2, flops=10**6)
+            (fallen,) = call(fall_kernel, [], [stay[0], diag[0]], [tile], flops=10**6)
             far = around(far, 1, sizes)
             near = shifted(near, "ty", 1)
             fallen = shifted(fallen, "ty", 1)
-            (out,) = call(last_kernel, [], [tiles[0][0], tiles[1][0], above1, above2, near, far, fallen],
-                          [pair], flops=10**6)
+            side = [shifted(side[s], "tx", 1) for s in (0, 1)]
+            (out,) = call(last_kernel, [],
+                          [tiles[0][0], tiles[1][0], stay[0], side[0], diag[0], stay[1], side[1], diag[1],
+                           near, far, fallen], [pair], flops=10**6)
             return out
-        side, diag = [moves1[0], moves2[0]], [moves1[1], moves2[1]]
-        for s in (1, 0):
-            diag[s] = moved(diag[s], diagonal_on, sizes)
         above, below = [None, None], [None, None]
         for s in (1, 0):
             side[s] = shifted(side[s], "tx", 1)

time: 248 us -> 244 us (0.984)
  the two profiles are of different devices: /device:TPU:10 before, /device:TPU:29 now
where the time goes in v6:
time: 244 us; the launch traced here: 243 us
  starting transfers between devices  125 us (51%)
  waiting for transfers between devices  93.9 us (38%)
  Pallas kernels  22.2 us (9%)
    ppermute x12, starting transfers between devices, moved(): return lax.ppermute(value, ('ty', 'tx'), pairs)  69.7 us
    ppermute x12, waiting for transfers between devices, moved(): return lax.ppermute(value, ('ty', 'tx'), pairs)  59.9 us
    ppermute x16, starting transfers between devices, shifted(): lax.ppermute(value, axis, [(source, source + steps) for source in range(f...  54.9 us
    ppermute x16, waiting for transfers between devices, shifted(): lax.ppermute(value, axis, [(source, source + steps) for source in range(f...  34 us
    pallas_call x16, Pallas kernels, call(): pl.pallas_call(body, out_shape=outs, in_specs=[SMEM] * len(scalars) + [VM...  22.2 us
  transfers between devices with their start and end apart: 28, of which 10 were waited for; matrix products, arithmetic and copies ran while one was open for 0% of the time, Pallas kernels for 5%

profile of v6, /device:TPU:29, one launch (start us, length us, event | category | flops | bytes accessed | tf_op | source)
XLA Modules:
  0.0 242.7 jit_solution(16293726979726629941)
XLA Ops:
  0.0 1.4 slice_bitcast_fusion
  1.4 0.0 copy-start
  1.4 0.0 copy-start.1
  1.4 0.0 copy-start.2
  1.4 0.0 copy-start.3
  1.4 0.0 copy-start.6
  1.4 8.2 %collective-permute-start.1 = (f32[2,256,256]{2,1,0:T(8,128)S(1)}, f32[2,256,256]{2,1,0:T(8,128)S(1)}, u32[]{:S(2)}, u32[]{:S(2)}) collective-permute-start(f32[2,256,256]{2,1,0:T(8,128)S(1)} %get-tuple-element.70.own.refs_5_.old), channel_id=1, source_target_pairs={{16,0},{32,16},{48,32},{64,48},{80,64},{96,80},{112,96},{128,112},... | collective-permute-start | bytes 1572872 | tf_op jit(solution)/shard_map/ppermute | solution.py:36
  9.7 1.9 collective-permute-start.5
  11.7 5.8 %collective-permute-start.4 = (f32[256,256]{1,0:T(8,128)S(1)}, f32[256,256]{1,0:T(8,128)S(1)}, u32[]{:S(2)}, u32[]{:S(2)}) collective-permute-start(f32[256,256]{1,0:T(8,128)S(1)} %get-tuple-element.68), channel_id=1, source_target_pairs={{16,0},{32,16},{48,32},{64,48},{80,64},{96,80},{112,96},{128,112},... | collective-permute-start | bytes 786440 | tf_op jit(solution)/shard_map/ppermute | solution.py:36
  17.5 14.6 %collective-permute-done.5 = f32[256,256]{1,0:T(8,128)S(1)} collective-permute-done((f32[256,256]{1,0:T(8,128)S(1)}, f32[256,256]{1,0:T(8,128)S(1)}, u32[]{:S(2)}, u32[]{:S(2)}) %collective-permute-start.5) | collective-permute-done | bytes 262176 | tf_op jit(solution)/shard_map/ppermute | solution.py:47
  32.1 1.9 collective-permute-start.6
  34.0 2.8 %collective-permute-start = (f32[2,256,256]{2,1,0:T(8,128)S(1)}, f32[2,256,256]{2,1,0:T(8,128)S(1)}, u32[]{:S(2)}, u32[]{:S(2)}) collective-permute-start(f32[2,256,256]{2,1,0:T(8,128)S(1)} %get-tuple-element.70.own.refs_5_.old), channel_id=1, source_target_pairs={{1,0},{2,1},{3,2},{4,3},{5,4},{6,5},{7,6},{8,7},{9,8},{10,9},{11,1... | collective-permute-start | bytes 1572872 | tf_op jit(solution)/shard_map/ppermute | solution.py:36
  36.8 0.0 collective-permute-done.1.low.refs_7_.old_low
  36.8 0.1 shard_map.83
  36.9 4.2 %collective-permute-start.2 = (f32[2,256,256]{2,1,0:T(8,128)S(1)}, f32[2,256,256]{2,1,0:T(8,128)S(1)}, u32[]{:S(2)}, u32[]{:S(2)}) collective-permute-start(f32[2,256,256]{2,1,0:T(8,128)S(1)} %shard_map.83), channel_id=1, source_target_pairs={{1,0},{2,1},{3,2},{5,4},{6,5},{7,6},{9,8},{10,9},{11,10},{13,12},{... | collective-permute-start | bytes 1572872 | tf_op jit(solution)/shard_map/ppermute | solution.py:47
  41.1 1.9 collective-permute-start.3
  43.0 11.0 %collective-permute-done.6.far = f32[256,256]{1,0:T(8,128)S(1)} collective-permute-done((f32[256,256]{1,0:T(8,128)S(1)}, f32[256,256]{1,0:T(8,128)S(1)}, u32[]{:S(2)}, u32[]{:S(2)}) %collective-permute-start.6) | collective-permute-done | bytes 262176 | tf_op jit(solution)/shard_map/ppermute | solution.py:47
  54.0 0.1 shard_map.85
  54.1 3.5 %collective-permute-start.7 = (f32[2,256,256]{2,1,0:T(8,128)S(1)}, f32[2,256,256]{2,1,0:T(8,128)S(1)}, u32[]{:S(2)}, u32[]{:S(2)}) collective-permute-start(f32[2,256,256]{2,1,0:T(8,128)S(1)} %get-tuple-element.40), channel_id=1, source_target_pairs={{1,0},{2,1},{3,2},{5,4},{6,5},{7,6},{9,8},{10,9},{11,10},{13,12},{... | collective-permute-start | bytes 1572872 | tf_op jit(solution)/shard_map/ppermute | solution.py:47
  57.7 0.0 copy-start.4
  57.7 0.0 copy-start.5
  57.7 5.2 %shard_map.82 = (f32[2,2,2,256,256]{4,3,2,1,0:T(8,128)S(1)}, f32[2,2,256,128]{3,2,1,0:T(8,128)S(1)}, f32[2,2,2,256,128]{4,3,2,1,0:T(8,128)S(1)}) custom-call(s32[2,2,2]{2,1,0:T(2,128)S(1)} %bitcast.12, f32[2,256,256]{2,1,0:T(8,128)S(1)} %copy-done.1, f32[256,256]{1,0:T(8,128)S(1)} %copy-done.2, f32[2,2,256,256]{3,2,1,0:T(8,128)S(1)} %bitcast.11, ...), custom_call_target="tpu_custom_call" | custom-call | flops 4000000000 | bytes 8388608 | tf_op jit(solution)/shard_map/pallas_call | solution.py:320
  62.9 0.0 collective-permute-done.2.refs_8_
  63.0 3.6 %shard_map.84.refs_2_ = f32[2,2,256,256]{3,2,1,0:T(8,128)S(1)} custom-call(s32[2,2,2]{2,1,0:T(2,128)S(1)} %bitcast.13, s32[2]{0:T(128)S(1)} %bitcast.19, f32[2,2,2,256,256]{4,3,2,1,0:T(8,128)S(1)} %get-tuple-element.36.refs_2_.refs_3_, f32[2,2,256,128]{3,2,1,0:T(8,128)S(1)} %get-tuple-element.37.refs_3_.refs_4_, bf16[2,2,2,256,256]{4,3,2,1,0:T(8,128)(2,1)S(1)} %copy-done.5, ...), custom_call_target="tpu_custom_call" | custom-call | flops 4000000000 | bytes 8388608 | tf_op jit(solution)/shard_map/pallas_call | solution.py:320
  66.6 4.8 %shard_map.86 = (f32[2,2,256,256]{3,2,1,0:T(8,128)S(1)}, f32[2,256,256]{2,1,0:T(8,128)S(1)}, f32[2,256,256]{2,1,0:T(8,128)S(1)}, f32[2,2,256,256]{3,2,1,0:T(8,128)S(1)}) custom-call(s32[2,2,2]{2,1,0:T(2,128)S(1)} %bitcast.14, s32[2]{0:T(128)S(1)} %bitcast.20, f32[2,2,256,256]{3,2,1,0:T(8,128)S(1)} %shard_map.84.refs_2_, ...), custom_call_target="tpu_custom_call" | custom-call | flops 4000000000 | bytes 8388608 | tf_op jit(solution)/shard_map/pallas_call | solution.py:320
  71.4 4.0 %shard_map.87 = (f32[2,2,256,256]{3,2,1,0:T(8,128)S(1)}, f32[2,256,256]{2,1,0:T(8,128)S(1)}, f32[2,256,256]{2,1,0:T(8,128)S(1)}) custom-call(s32[2,2,2]{2,1,0:T(2,128)S(1)} %bitcast.15, s32[2]{0:T(128)S(1)} %bitcast.21, f32[2,2,256,256]{3,2,1,0:T(8,128)S(1)} %get-tuple-element.41.refs_2_, f32[2,2,2,256,256]{4,3,2,1,0:T(8,128)S(1)} %get-tuple-element.36.refs_2_.refs_3_, ...), custom_call_target="tpu_custom_call" | custom-call | flops 4000000000 | bytes 8388608 | tf_op jit(solution)/shard_map/pallas_call | solution.py:320
  75.4 2.0 collective-permute-start.8
  77.4 1.9 collective-permute-start.9
  79.4 3.7 %collective-permute-start.12 = (f32[2,256,256]{2,1,0:T(8,128)S(1)}, f32[2,256,256]{2,1,0:T(8,128)S(1)}, u32[]{:S(2)}, u32[]{:S(2)}) collective-permute-start(f32[2,256,256]{2,1,0:T(8,128)S(1)} %get-tuple-element.49), channel_id=1, source_target_pairs={{0,1},{1,2},{2,3},{3,4},{4,5},{5,6},{6,7},{7,8},{8,9},{9,10},{10,1... | collective-permute-start | bytes 1572872 | tf_op jit(solution)/shard_map/ppermute | solution.py:36
  83.1 2.9 %collective-permute-start.13 = (f32[2,256,256]{2,1,0:T(8,128)S(1)}, f32[2,256,256]{2,1,0:T(8,128)S(1)}, u32[]{:S(2)}, u32[]{:S(2)}) collective-permute-start(f32[2,256,256]{2,1,0:T(8,128)S(1)} %get-tuple-element.50), channel_id=1, source_target_pairs={{0,1},{1,2},{2,3},{3,20},{4,5},{5,6},{6,7},{7,24},{8,9},{9,10},{10... | collective-permute-start | bytes 1572872 | tf_op jit(solution)/shard_map/ppermute | solution.py:47
  86.0 3.2 %collective-permute-done.9.diag = f32[2,256,256]{2,1,0:T(8,128)S(1)} collective-permute-done((f32[2,256,256]{2,1,0:T(8,128)S(1)}, f32[2,256,256]{2,1,0:T(8,128)S(1)}, u32[]{:S(2)}, u32[]{:S(2)}) %collective-permute-start.9) | collective-permute-done | bytes 524320 | tf_op jit(solution)/shard_map/ppermute | solution.py:47
  89.2 0.1 shard_map.88
  89.3 3.0 %collective-permute-start.11 = (f32[2,256,256]{2,1,0:T(8,128)S(1)}, f32[2,256,256]{2,1,0:T(8,128)S(1)}, u32[]{:S(2)}, u32[]{:S(2)}) collective-permute-start(f32[2,256,256]{2,1,0:T(8,128)S(1)} %get-tuple-element.45.above), channel_id=1, source_target_pairs={{16,0},{32,16},{48,32},{64,48},{80,64},{96,80},{112,96},{128,112},... | collective-permute-start | bytes 1572872 | tf_op jit(solution)/shard_map/ppermute | solution.py:36
  92.3 3.1 %collective-permute-start.10 = (f32[2,256,256]{2,1,0:T(8,128)S(1)}, f32[2,256,256]{2,1,0:T(8,128)S(1)}, u32[]{:S(2)}, u32[]{:S(2)}) collective-permute-start(f32[2,256,256]{2,1,0:T(8,128)S(1)} %get-tuple-element.46.below), channel_id=1, source_target_pairs={{0,16},{16,32},{32,48},{48,64},{64,80},{80,96},{96,112},{112,128},... | collective-permute-start | bytes 1572872 | tf_op jit(solution)/shard_map/ppermute | solution.py:36
  95.5 4.9 %collective-permute-done.13.diag = f32[2,256,256]{2,1,0:T(8,128)S(1)} collective-permute-done((f32[2,256,256]{2,1,0:T(8,128)S(1)}, f32[2,256,256]{2,1,0:T(8,128)S(1)}, u32[]{:S(2)}, u32[]{:S(2)}) %collective-permute-start.13) | collective-permute-done | bytes 524320 | tf_op jit(solution)/shard_map/ppermute | solution.py:47
  100.4 0.1 shard_map.90
  100.5 1.9 collective-permute-start.15
  102.5 4.3 %collective-permute-start.14 = (f32[2,256,256]{2,1,0:T(8,128)S(1)}, f32[2,256,256]{2,1,0:T(8,128)S(1)}, u32[]{:S(2)}, u32[]{:S(2)}) collective-permute-start(f32[2,256,256]{2,1,0:T(8,128)S(1)} %get-tuple-element.52.below), channel_id=1, source_target_pairs={{0,16},{16,32},{32,48},{48,64},{64,80},{80,96},{96,112},{112,128},... | collective-permute-start | bytes 1572872 | tf_op jit(solution)/shard_map/ppermute | solution.py:36
  106.7 3.5 %collective-permute-done.10.from_above = f32[2,256,256]{2,1,0:T(8,128)S(1)} collective-permute-done((f32[2,256,256]{2,1,0:T(8,128)S(1)}, f32[2,256,256]{2,1,0:T(8,128)S(1)}, u32[]{:S(2)}, u32[]{:S(2)}) %collective-permute-start.10) | collective-permute-done | bytes 524320 | tf_op jit(solution)/shard_map/ppermute | solution.py:36
  110.2 0.3 shard_map.89
  110.5 18.3 %collective-permute-start.17 = (f32[2,256,256]{2,1,0:T(8,128)S(1)}, f32[2,256,256]{2,1,0:T(8,128)S(1)}, u32[]{:S(2)}, u32[]{:S(2)}) collective-permute-start(f32[2,256,256]{2,1,0:T(8,128)S(1)} %get-tuple-element.55), channel_id=1, source_target_pairs={{1,0},{2,1},{3,2},{5,4},{6,5},{7,6},{9,8},{10,9},{11,10},{13,12},{... | collective-permute-start | bytes 1572872 | tf_op jit(solution)/shard_map/ppermute | solution.py:47
  128.8 3.0 %collective-permute-start.16 = (f32[2,256,256]{2,1,0:T(8,128)S(1)}, f32[2,256,256]{2,1,0:T(8,128)S(1)}, u32[]{:S(2)}, u32[]{:S(2)}) collective-permute-start(f32[2,256,256]{2,1,0:T(8,128)S(1)} %get-tuple-element.47.refs_5_.one), channel_id=1, source_target_pairs={{1,0},{2,1},{3,2},{4,3},{5,4},{6,5},{7,6},{8,7},{9,8},{10,9},{11,1... | collective-permute-start | bytes 1572872 | tf_op jit(solution)/shard_map/ppermute | solution.py:36
  131.8 4.3 %collective-permute-done.15.from_below = f32[2,256,256]{2,1,0:T(8,128)S(1)} collective-permute-done((f32[2,256,256]{2,1,0:T(8,128)S(1)}, f32[2,256,256]{2,1,0:T(8,128)S(1)}, u32[]{:S(2)}, u32[]{:S(2)}) %collective-permute-start.15) | collective-permute-done | bytes 524320 | tf_op jit(solution)/shard_map/ppermute | solution.py:36
  136.1 0.2 shard_map.91
  136.3 15.1 %collective-permute-start.19 = (f32[2,256,256]{2,1,0:T(8,128)S(1)}, f32[2,256,256]{2,1,0:T(8,128)S(1)}, u32[]{:S(2)}, u32[]{:S(2)}) collective-permute-start(f32[2,256,256]{2,1,0:T(8,128)S(1)} %get-tuple-element.57), channel_id=1, source_target_pairs={{1,0},{2,1},{3,2},{5,4},{6,5},{7,6},{9,8},{10,9},{11,10},{13,12},{... | collective-permute-start | bytes 1572872 | tf_op jit(solution)/shard_map/ppermute | solution.py:47
  151.5 1.9 collective-permute-start.18
  153.4 0.6 shard_map.92.refs_2_
  154.0 2.6 %collective-permute-done.19.refs_8_ = f32[2,256,256]{2,1,0:T(8,128)S(1)} collective-permute-done((f32[2,256,256]{2,1,0:T(8,128)S(1)}, f32[2,256,256]{2,1,0:T(8,128)S(1)}, u32[]{:S(2)}, u32[]{:S(2)}) %collective-permute-start.19) | collective-permute-done | bytes 524320 | tf_op jit(solution)/shard_map/ppermute | solution.py:47
  156.6 5.6 %collective-permute-done.18.refs_6_ = f32[2,256,256]{2,1,0:T(8,128)S(1)} collective-permute-done((f32[2,256,256]{2,1,0:T(8,128)S(1)}, f32[2,256,256]{2,1,0:T(8,128)S(1)}, u32[]{:S(2)}, u32[]{:S(2)}) %collective-permute-start.18) | collective-permute-done | bytes 524320 | tf_op jit(solution)/shard_map/ppermute | solution.py:36
  162.2 0.9 shard_map.93
  163.1 1.9 collective-permute-start.23
  165.1 0.7 shard_map.94
  165.8 11.4 %collective-permute-start.21 = (f32[2,256,256]{2,1,0:T(8,128)S(1)}, f32[2,256,256]{2,1,0:T(8,128)S(1)}, u32[]{:S(2)}, u32[]{:S(2)}) collective-permute-start(f32[2,256,256]{2,1,0:T(8,128)S(1)} %get-tuple-element.61), channel_id=1, source_target_pairs={{0,1},{1,2},{2,3},{3,20},{4,5},{5,6},{6,7},{7,24},{8,9},{9,10},{10... | collective-permute-start | bytes 1572872 | tf_op jit(solution)/shard_map/ppermute | solution.py:47
  177.2 5.2 %collective-permute-start.20 = (f32[2,256,256]{2,1,0:T(8,128)S(1)}, f32[2,256,256]{2,1,0:T(8,128)S(1)}, u32[]{:S(2)}, u32[]{:S(2)}) collective-permute-start(f32[2,256,256]{2,1,0:T(8,128)S(1)} %get-tuple-element.60), channel_id=1, source_target_pairs={{0,1},{1,2},{2,3},{3,4},{4,5},{5,6},{6,7},{7,8},{8,9},{9,10},{10,1... | collective-permute-start | bytes 1572872 | tf_op jit(solution)/shard_map/ppermute | solution.py:36
  182.4 1.9 collective-permute-start.22
  184.3 0.1 shard_map.95
  184.4 4.7 %collective-permute-start.25 = (f32[256,256]{1,0:T(8,128)S(1)}, f32[256,256]{1,0:T(8,128)S(1)}, u32[]{:S(2)}, u32[]{:S(2)}) collective-permute-start(f32[256,256]{1,0:T(8,128)S(1)} %get-tuple-element.66), channel_id=1, source_target_pairs={{0,34},{1,35},{2,48},{3,49},{4,38},{5,39},{6,52},{7,53},{8,42},{9,... | collective-permute-start | bytes 786440 | tf_op jit(solution)/shard_map/ppermute | solution.py:47
  189.2 0.1 shard_map.96
  189.3 3.1 %collective-permute-start.27 = (f32[2,256,256]{2,1,0:T(8,128)S(1)}, f32[2,256,256]{2,1,0:T(8,128)S(1)}, u32[]{:S(2)}, u32[]{:S(2)}) collective-permute-start(f32[2,256,256]{2,1,0:T(8,128)S(1)} %shard_map.96), channel_id=1, source_target_pairs={{0,16},{16,32},{32,48},{48,64},{64,80},{80,96},{96,112},{112,128},... | collective-permute-start | bytes 1572872 | tf_op jit(solution)/shard_map/ppermute | solution.py:36
  192.4 2.8 %collective-permute-start.24 = (f32[256,256]{1,0:T(8,128)S(1)}, f32[256,256]{1,0:T(8,128)S(1)}, u32[]{:S(2)}, u32[]{:S(2)}) collective-permute-start(f32[256,256]{1,0:T(8,128)S(1)} %get-tuple-element.65), channel_id=1, source_target_pairs={{0,16},{16,32},{32,48},{48,64},{64,80},{80,96},{96,112},{112,128},... | collective-permute-start | bytes 786440 | tf_op jit(solution)/shard_map/ppermute | solution.py:36
  195.2 23.7 %collective-permute-done.25 = f32[256,256]{1,0:T(8,128)S(1)} collective-permute-done((f32[256,256]{1,0:T(8,128)S(1)}, f32[256,256]{1,0:T(8,128)S(1)}, u32[]{:S(2)}, u32[]{:S(2)}) %collective-permute-start.25) | collective-permute-done | bytes 262176 | tf_op jit(solution)/shard_map/ppermute | solution.py:47
  218.9 1.9 collective-permute-start.26
  220.8 20.6 %collective-permute-done.24.near2 = f32[256,256]{1,0:T(8,128)S(1)} collective-permute-done((f32[256,256]{1,0:T(8,128)S(1)}, f32[256,256]{1,0:T(8,128)S(1)}, u32[]{:S(2)}, u32[]{:S(2)}) %collective-permute-start.24) | collective-permute-done | bytes 262176 | tf_op jit(solution)/shard_map/ppermute | solution.py:36
  241.4 1.3 shard_map.97
  (26 shorter events, 0.1 us)
Async XLA Ops:
  0.0 9.7 %copy-start.7 = (f32[2,2,256,256]{3,2,1,0:T(8,128)S(1)}, f32[2,2,256,256]{3,2,1,0:T(8,128)}, u32[]{:S(2)}) copy-start(f32[2,2,256,256]{3,2,1,0:T(8,128)} %param.8) | copy-start | bytes 3145732
  1.4 56.3 %copy-start = (f32[2,1,1,2,256,256]{5,4,3,2,1,0:T(8,128)S(1)}, f32[2,1,1,2,256,256]{5,4,3,2,1,0:T(8,128)}, u32[]{:S(2)}) copy-start(f32[2,1,1,2,256,256]{5,4,3,2,1,0:T(8,128)} %param.13) | copy-start | bytes 3145732
  1.4 56.3 %copy-start.1 = (f32[2,256,256]{2,1,0:T(8,128)S(1)}, f32[2,256,256]{2,1,0:T(8,128)}, u32[]{:S(2)}) copy-start(f32[2,256,256]{2,1,0:T(8,128)} %probe_ref.1) | copy-start | bytes 1572868
  1.4 56.2 %copy-start.2 = (f32[256,256]{1,0:T(8,128)S(1)}, f32[256,256]{1,0:T(8,128)}, u32[]{:S(2)}) copy-start(f32[256,256]{1,0:T(8,128)} %angle_ref.1) | copy-start | bytes 786436
  1.4 56.2 %copy-start.3 = (s32[2,1,1,2,2]{4,3,2,1,0:T(2,128)S(1)}, s32[2,1,1,2,2]{4,3,2,1,0:T(2,128)}, u32[]{:S(2)}) copy-start(s32[2,1,1,2,2]{4,3,2,1,0:T(2,128)} %param.11) | copy-start | bytes 100
  1.4 56.2 %copy-start.6 = (bf16[2,256,256]{2,1,0:T(8,128)(2,1)S(1)}, bf16[2,256,256]{2,1,0:T(8,128)(2,1)}, u32[]{:S(2)}) copy-start(bf16[2,256,256]{2,1,0:T(8,128)(2,1)} %constant.5.clone.perm_ref) | copy-start | bytes 786436
  1.4 35.4 %collective-permute-start.1 = (f32[2,256,256]{2,1,0:T(8,128)S(1)}, f32[2,256,256]{2,1,0:T(8,128)S(1)}, u32[]{:S(2)}, u32[]{:S(2)}) collective-permute-start(f32[2,256,256]{2,1,0:T(8,128)S(1)} %get-tuple-element.70.own.refs_5_.old), channel_id=1, source_target_pairs={{16,0},{32,16},{48,32},{64,48},{80,64},{96,80},{112,96},{128,112},... | collective-permute-start | bytes 1572872 | tf_op jit(solution)/shard_map/ppermute | solution.py:36
  9.7 22.3 %collective-permute-start.5 = (f32[256,256]{1,0:T(8,128)S(1)}, f32[256,256]{1,0:T(8,128)S(1)}, u32[]{:S(2)}, u32[]{:S(2)}) collective-permute-start(f32[256,256]{1,0:T(8,128)S(1)} %get-tuple-element.67), channel_id=1, source_target_pairs={{16,34},{17,35},{18,48},{19,49},{20,38},{21,39},{22,52},{23,53},{2... | collective-permute-start | bytes 786440 | tf_op jit(solution)/shard_map/ppermute | solution.py:47
  11.7 31.4 %collective-permute-start.4 = (f32[256,256]{1,0:T(8,128)S(1)}, f32[256,256]{1,0:T(8,128)S(1)}, u32[]{:S(2)}, u32[]{:S(2)}) collective-permute-start(f32[256,256]{1,0:T(8,128)S(1)} %get-tuple-element.68), channel_id=1, source_target_pairs={{16,0},{32,16},{48,32},{64,48},{80,64},{96,80},{112,96},{128,112},... | collective-permute-start | bytes 786440 | tf_op jit(solution)/shard_map/ppermute | solution.py:36
  32.1 22.0 %collective-permute-start.6 = (f32[256,256]{1,0:T(8,128)S(1)}, f32[256,256]{1,0:T(8,128)S(1)}, u32[]{:S(2)}, u32[]{:S(2)}) collective-permute-start(f32[256,256]{1,0:T(8,128)S(1)} %collective-permute-done.5), channel_id=1, source_target_pairs={{0,18},{1,19},{2,32},{3,33},{4,22},{5,23},{6,36},{7,37},{8,26},{9,... | collective-permute-start | bytes 786440 | tf_op jit(solution)/shard_map/ppermute | solution.py:47
  34.0 29.0 %collective-permute-start = (f32[2,256,256]{2,1,0:T(8,128)S(1)}, f32[2,256,256]{2,1,0:T(8,128)S(1)}, u32[]{:S(2)}, u32[]{:S(2)}) collective-permute-start(f32[2,256,256]{2,1,0:T(8,128)S(1)} %get-tuple-element.70.own.refs_5_.old), channel_id=1, source_target_pairs={{1,0},{2,1},{3,2},{4,3},{5,4},{6,5},{7,6},{8,7},{9,8},{10,9},{11,1... | collective-permute-start | bytes 1572872 | tf_op jit(solution)/shard_map/ppermute | solution.py:36
  36.9 26.1 %collective-permute-start.2 = (f32[2,256,256]{2,1,0:T(8,128)S(1)}, f32[2,256,256]{2,1,0:T(8,128)S(1)}, u32[]{:S(2)}, u32[]{:S(2)}) collective-permute-start(f32[2,256,256]{2,1,0:T(8,128)S(1)} %shard_map.83), channel_id=1, source_target_pairs={{1,0},{2,1},{3,2},{5,4},{6,5},{7,6},{9,8},{10,9},{11,10},{13,12},{... | collective-permute-start | bytes 1572872 | tf_op jit(solution)/shard_map/ppermute | solution.py:47
  41.1 25.4 %collective-permute-start.3 = (f32[2,256,256]{2,1,0:T(8,128)S(1)}, f32[2,256,256]{2,1,0:T(8,128)S(1)}, u32[]{:S(2)}, u32[]{:S(2)}) collective-permute-start(f32[2,256,256]{2,1,0:T(8,128)S(1)} %get-tuple-element.69.own.refs_5_.old), channel_id=1, source_target_pairs={{1,0},{2,1},{3,2},{4,3},{5,4},{6,5},{7,6},{8,7},{9,8},{10,9},{11,1... | collective-permute-start | bytes 1572872 | tf_op jit(solution)/shard_map/ppermute | solution.py:36
  54.1 12.4 %collective-permute-start.7 = (f32[2,256,256]{2,1,0:T(8,128)S(1)}, f32[2,256,256]{2,1,0:T(8,128)S(1)}, u32[]{:S(2)}, u32[]{:S(2)}) collective-permute-start(f32[2,256,256]{2,1,0:T(8,128)S(1)} %get-tuple-element.40), channel_id=1, source_target_pairs={{1,0},{2,1},{3,2},{5,4},{6,5},{7,6},{9,8},{10,9},{11,10},{13,12},{... | collective-permute-start | bytes 1572872 | tf_op jit(solution)/shard_map/ppermute | solution.py:47
  57.7 5.3 %copy-start.4 = (s32[2,1,1]{0,2,1:T(1,128)S(1)}, s32[2,1,1]{0,2,1:T(1,128)}, u32[]{:S(2)}) copy-start(s32[2,1,1]{0,2,1:T(1,128)} %param.12) | copy-start | bytes 28
  57.7 5.3 %copy-start.5 = (bf16[2,2,2,256,256]{4,3,2,1,0:T(8,128)(2,1)S(1)}, bf16[2,2,2,256,256]{4,3,2,1,0:T(8,128)(2,1)}, u32[]{:S(2)}) copy-start(bf16[2,2,2,256,256]{4,3,2,1,0:T(8,128)(2,1)} %constant.4.clone.refs_4_.refs_5_) | copy-start | bytes 3145732
  75.4 10.6 %collective-permute-start.8 = (f32[2,256,256]{2,1,0:T(8,128)S(1)}, f32[2,256,256]{2,1,0:T(8,128)S(1)}, u32[]{:S(2)}, u32[]{:S(2)}) collective-permute-start(f32[2,256,256]{2,1,0:T(8,128)S(1)} %get-tuple-element.43), channel_id=1, source_target_pairs={{0,1},{1,2},{2,3},{3,4},{4,5},{5,6},{6,7},{7,8},{8,9},{9,10},{10,1... | collective-permute-start | bytes 1572872 | tf_op jit(solution)/shard_map/ppermute | solution.py:36
  77.4 11.7 %collective-permute-start.9 = (f32[2,256,256]{2,1,0:T(8,128)S(1)}, f32[2,256,256]{2,1,0:T(8,128)S(1)}, u32[]{:S(2)}, u32[]{:S(2)}) collective-permute-start(f32[2,256,256]{2,1,0:T(8,128)S(1)} %get-tuple-element.44), channel_id=1, source_target_pairs={{0,1},{1,2},{2,3},{3,20},{4,5},{5,6},{6,7},{7,24},{8,9},{9,10},{10... | collective-permute-start | bytes 1572872 | tf_op jit(solution)/shard_map/ppermute | solution.py:47
  79.4 16.1 %collective-permute-start.12 = (f32[2,256,256]{2,1,0:T(8,128)S(1)}, f32[2,256,256]{2,1,0:T(8,128)S(1)}, u32[]{:S(2)}, u32[]{:S(2)}) collective-permute-start(f32[2,256,256]{2,1,0:T(8,128)S(1)} %get-tuple-element.49), channel_id=1, source_target_pairs={{0,1},{1,2},{2,3},{3,4},{4,5},{5,6},{6,7},{7,8},{8,9},{9,10},{10,1... | collective-permute-start | bytes 1572872 | tf_op jit(solution)/shard_map/ppermute | solution.py:36
  83.1 17.3 %collective-permute-start.13 = (f32[2,256,256]{2,1,0:T(8,128)S(1)}, f32[2,256,256]{2,1,0:T(8,128)S(1)}, u32[]{:S(2)}, u32[]{:S(2)}) collective-permute-start(f32[2,256,256]{2,1,0:T(8,128)S(1)} %get-tuple-element.50), channel_id=1, source_target_pairs={{0,1},{1,2},{2,3},{3,20},{4,5},{5,6},{6,7},{7,24},{8,9},{9,10},{10... | collective-permute-start | bytes 1572872 | tf_op jit(solution)/shard_map/ppermute | solution.py:47
  89.3 17.4 %collective-permute-start.11 = (f32[2,256,256]{2,1,0:T(8,128)S(1)}, f32[2,256,256]{2,1,0:T(8,128)S(1)}, u32[]{:S(2)}, u32[]{:S(2)}) collective-permute-start(f32[2,256,256]{2,1,0:T(8,128)S(1)} %get-tuple-element.45.above), channel_id=1, source_target_pairs={{16,0},{32,16},{48,32},{64,48},{80,64},{96,80},{112,96},{128,112},... | collective-permute-start | bytes 1572872 | tf_op jit(solution)/shard_map/ppermute | solution.py:36
  92.3 17.9 %collective-permute-start.10 = (f32[2,256,256]{2,1,0:T(8,128)S(1)}, f32[2,256,256]{2,1,0:T(8,128)S(1)}, u32[]{:S(2)}, u32[]{:S(2)}) collective-permute-start(f32[2,256,256]{2,1,0:T(8,128)S(1)} %get-tuple-element.46.below), channel_id=1, source_target_pairs={{0,16},{16,32},{32,48},{48,64},{64,80},{80,96},{96,112},{112,128},... | collective-permute-start | bytes 1572872 | tf_op jit(solution)/shard_map/ppermute | solution.py:36
  100.5 35.6 %collective-permute-start.15 = (f32[2,256,256]{2,1,0:T(8,128)S(1)}, f32[2,256,256]{2,1,0:T(8,128)S(1)}, u32[]{:S(2)}, u32[]{:S(2)}) collective-permute-start(f32[2,256,256]{2,1,0:T(8,128)S(1)} %get-tuple-element.51.above), channel_id=1, source_target_pairs={{16,0},{32,16},{48,32},{64,48},{80,64},{96,80},{112,96},{128,112},... | collective-permute-start | bytes 1572872 | tf_op jit(solution)/shard_map/ppermute | solution.py:36
  102.5 33.6 %collective-permute-start.14 = (f32[2,256,256]{2,1,0:T(8,128)S(1)}, f32[2,256,256]{2,1,0:T(8,128)S(1)}, u32[]{:S(2)}, u32[]{:S(2)}) collective-permute-start(f32[2,256,256]{2,1,0:T(8,128)S(1)} %get-tuple-element.52.below), channel_id=1, source_target_pairs={{0,16},{16,32},{32,48},{48,64},{64,80},{80,96},{96,112},{112,128},... | collective-permute-start | bytes 1572872 | tf_op jit(solution)/shard_map/ppermute | solution.py:36
  110.5 42.9 %collective-permute-start.17 = (f32[2,256,256]{2,1,0:T(8,128)S(1)}, f32[2,256,256]{2,1,0:T(8,128)S(1)}, u32[]{:S(2)}, u32[]{:S(2)}) collective-permute-start(f32[2,256,256]{2,1,0:T(8,128)S(1)} %get-tuple-element.55), channel_id=1, source_target_pairs={{1,0},{2,1},{3,2},{5,4},{6,5},{7,6},{9,8},{10,9},{11,10},{13,12},{... | collective-permute-start | bytes 1572872 | tf_op jit(solution)/shard_map/ppermute | solution.py:47
  128.8 24.6 %collective-permute-start.16 = (f32[2,256,256]{2,1,0:T(8,128)S(1)}, f32[2,256,256]{2,1,0:T(8,128)S(1)}, u32[]{:S(2)}, u32[]{:S(2)}) collective-permute-start(f32[2,256,256]{2,1,0:T(8,128)S(1)} %get-tuple-element.47.refs_5_.one), channel_id=1, source_target_pairs={{1,0},{2,1},{3,2},{4,3},{5,4},{6,5},{7,6},{8,7},{9,8},{10,9},{11,1... | collective-permute-start | bytes 1572872 | tf_op jit(solution)/shard_map/ppermute | solution.py:36
  136.3 20.3 %collective-permute-start.19 = (f32[2,256,256]{2,1,0:T(8,128)S(1)}, f32[2,256,256]{2,1,0:T(8,128)S(1)}, u32[]{:S(2)}, u32[]{:S(2)}) collective-permute-start(f32[2,256,256]{2,1,0:T(8,128)S(1)} %get-tuple-element.57), channel_id=1, source_target_pairs={{1,0},{2,1},{3,2},{5,4},{6,5},{7,6},{9,8},{10,9},{11,10},{13,12},{... | collective-permute-start | bytes 1572872 | tf_op jit(solution)/shard_map/ppermute | solution.py:47
  151.5 10.8 %collective-permute-start.18 = (f32[2,256,256]{2,1,0:T(8,128)S(1)}, f32[2,256,256]{2,1,0:T(8,128)S(1)}, u32[]{:S(2)}, u32[]{:S(2)}) collective-permute-start(f32[2,256,256]{2,1,0:T(8,128)S(1)} %get-tuple-element.53.refs_5_.two), channel_id=1, source_target_pairs={{1,0},{2,1},{3,2},{4,3},{5,4},{6,5},{7,6},{8,7},{9,8},{10,9},{11,1... | collective-permute-start | bytes 1572872 | tf_op jit(solution)/shard_map/ppermute | solution.py:36
  163.1 21.2 %collective-permute-start.23 = (f32[2,256,256]{2,1,0:T(8,128)S(1)}, f32[2,256,256]{2,1,0:T(8,128)S(1)}, u32[]{:S(2)}, u32[]{:S(2)}) collective-permute-start(f32[2,256,256]{2,1,0:T(8,128)S(1)} %get-tuple-element.64), channel_id=1, source_target_pairs={{0,1},{1,2},{2,3},{3,20},{4,5},{5,6},{6,7},{7,24},{8,9},{9,10},{10... | collective-permute-start | bytes 1572872 | tf_op jit(solution)/shard_map/ppermute | solution.py:47
  165.8 23.4 %collective-permute-start.21 = (f32[2,256,256]{2,1,0:T(8,128)S(1)}, f32[2,256,256]{2,1,0:T(8,128)S(1)}, u32[]{:S(2)}, u32[]{:S(2)}) collective-permute-start(f32[2,256,256]{2,1,0:T(8,128)S(1)} %get-tuple-element.61), channel_id=1, source_target_pairs={{0,1},{1,2},{2,3},{3,20},{4,5},{5,6},{6,7},{7,24},{8,9},{9,10},{10... | collective-permute-start | bytes 1572872 | tf_op jit(solution)/shard_map/ppermute | solution.py:47
  177.2 43.6 %collective-permute-start.20 = (f32[2,256,256]{2,1,0:T(8,128)S(1)}, f32[2,256,256]{2,1,0:T(8,128)S(1)}, u32[]{:S(2)}, u32[]{:S(2)}) collective-permute-start(f32[2,256,256]{2,1,0:T(8,128)S(1)} %get-tuple-element.60), channel_id=1, source_target_pairs={{0,1},{1,2},{2,3},{3,4},{4,5},{5,6},{6,7},{7,8},{8,9},{9,10},{10,1... | collective-permute-start | bytes 1572872 | tf_op jit(solution)/shard_map/ppermute | solution.py:36
  182.4 38.5 %collective-permute-start.22 = (f32[2,256,256]{2,1,0:T(8,128)S(1)}, f32[2,256,256]{2,1,0:T(8,128)S(1)}, u32[]{:S(2)}, u32[]{:S(2)}) collective-permute-start(f32[2,256,256]{2,1,0:T(8,128)S(1)} %get-tuple-element.63), channel_id=1, source_target_pairs={{0,1},{1,2},{2,3},{3,4},{4,5},{5,6},{6,7},{7,8},{8,9},{9,10},{10,1... | collective-permute-start | bytes 1572872 | tf_op jit(solution)/shard_map/ppermute | solution.py:36
  184.4 34.5 %collective-permute-start.25 = (f32[256,256]{1,0:T(8,128)S(1)}, f32[256,256]{1,0:T(8,128)S(1)}, u32[]{:S(2)}, u32[]{:S(2)}) collective-permute-start(f32[256,256]{1,0:T(8,128)S(1)} %get-tuple-element.66), channel_id=1, source_target_pairs={{0,34},{1,35},{2,48},{3,49},{4,38},{5,39},{6,52},{7,53},{8,42},{9,... | collective-permute-start | bytes 786440 | tf_op jit(solution)/shard_map/ppermute | solution.py:47
  189.3 52.1 %collective-permute-start.27 = (f32[2,256,256]{2,1,0:T(8,128)S(1)}, f32[2,256,256]{2,1,0:T(8,128)S(1)}, u32[]{:S(2)}, u32[]{:S(2)}) collective-permute-start(f32[2,256,256]{2,1,0:T(8,128)S(1)} %shard_map.96), channel_id=1, source_target_pairs={{0,16},{16,32},{32,48},{48,64},{64,80},{80,96},{96,112},{112,128},... | collective-permute-start | bytes 1572872 | tf_op jit(solution)/shard_map/ppermute | solution.py:36
  192.4 49.0 %collective-permute-start.24 = (f32[256,256]{1,0:T(8,128)S(1)}, f32[256,256]{1,0:T(8,128)S(1)}, u32[]{:S(2)}, u32[]{:S(2)}) collective-permute-start(f32[256,256]{1,0:T(8,128)S(1)} %get-tuple-element.65), channel_id=1, source_target_pairs={{0,16},{16,32},{32,48},{48,64},{64,80},{80,96},{96,112},{112,128},... | collective-permute-start | bytes 786440 | tf_op jit(solution)/shard_map/ppermute | solution.py:36
  218.9 22.5 %collective-permute-start.26 = (f32[256,256]{1,0:T(8,128)S(1)}, f32[256,256]{1,0:T(8,128)S(1)}, u32[]{:S(2)}, u32[]{:S(2)}) collective-permute-start(f32[256,256]{1,0:T(8,128)S(1)} %collective-permute-done.25), channel_id=1, source_target_pairs={{0,34},{1,35},{2,48},{3,49},{4,38},{5,39},{6,52},{7,53},{8,42},{9,... | collective-permute-start | bytes 786440 | tf_op jit(solution)/shard_map/ppermute | solution.py:47
